TPU v7x, 128 devices: a whole 4x4x4 slice. The times are simulated.
128 devices in a mesh: chain: 4 (over z_hi, core), gx: 32 (over y, z_lo, x).
Axes of the slice: x: 4, y: 4, z: 4 (z_hi: 2, z_lo: 2; z = z_hi * 2 + z_lo), core: 2. Of those that a mesh axis runs over, the one named last changes fastest.
Arguments:
- position: float32 [8, 256, 16, 1024], P('chain', 'gx'), may hold values from -6 to 6
- momentum_draw: float32 [8, 256, 16, 1024], P('chain', 'gx'), may hold values from -6 to 6
- viscosity: float32 [256, 16, 1024], P('gx'), may hold values from 0.3 to 3
- observed: float32 [256, 16, 1024], P('gx'), may hold values from -18 to 18
Outputs:
- new_position: float32 [8, 256, 16, 1024], P('chain', 'gx')
- new_momentum: float32 [8, 256, 16, 1024], P('chain', 'gx')
- energies: float32 [2, 8], P(None, 'chain')
All inputs are finite; a program needn't handle non-finite values.
Results may differ from a plain program's by a relative error of at most 0.00002.
Values sent between devices are 32-bit elements; how exact they have to be, the bound alone decides.
No kernel may reach another device: no remote copies, remote signals or barrier semaphores. Data moves between devices by JAX's collectives and lax.ppermute only.
A program may use at most 64 MiB of HBM per device.

v0:
```python
import jax
import jax.numpy as jnp
from jax import lax
from jax.sharding import PartitionSpec as P

LEAPS = 2


stencil_weights = (4.0, -0.3, -0.1, -0.05)
inv_noise = 0.25
prior_weight = 0.5
step_size = 0.05


def with_halo(block, sides, width):
    for axis, dim in sides:
        count = lax.axis_size(axis)
        forward = [(i, i + 1) for i in range(count - 1)]
        forward.append((count - 1, 0))
        backward = [(target, source) for source, target in forward]
        low = lax.ppermute(
            lax.slice_in_dim(block, block.shape[dim] - width, None, axis=dim), axis, forward
        )
        high = lax.ppermute(lax.slice_in_dim(block, 0, width, axis=dim), axis, backward)
        block = jnp.concatenate([low, block, high], axis=dim)
    return block


def apply_kernel(extended):
    lead = extended.ndim - 3
    padded = jnp.pad(extended, ((0, 0),) * lead + ((0, 0), (1, 1), (1, 1)))
    planes = extended.shape[lead] - 2
    depth_cells = extended.shape[lead + 1]
    across = extended.shape[lead + 2]
    summed = jnp.zeros(extended.shape[:lead] + (planes, depth_cells, across), jnp.float32)
    for shift_x in range(3):
        for shift_z in range(3):
            for shift_y in range(3):
                order = abs(shift_x - 1) + abs(shift_z - 1) + abs(shift_y - 1)
                summed = (
                    summed
                    + stencil_weights[order]
                    * padded[
                        ...,
                        shift_x : shift_x + planes,
                        shift_z : shift_z + depth_cells,
                        shift_y : shift_y + across,
                    ]
                )
    return summed


def gradient_narrow(source, viscosity, observed):
    extended = with_halo(source, (("gx", 1),), 1)
    misfit = viscosity * apply_kernel(extended) - observed
    scaled = viscosity * misfit
    rims = with_halo(scaled, (("gx", 1),), 1)
    return (inv_noise * apply_kernel(rims) + prior_weight * source, misfit)


def local_sums(source, misfit, moment, inverse_mass):
    potential = 0.5 * inv_noise * jnp.sum(
        misfit * misfit, axis=(1, 2, 3)
    ) + 0.5 * prior_weight * jnp.sum(source * source, axis=(1, 2, 3))
    kinetic = 0.5 * jnp.sum(inverse_mass * moment * moment, axis=(1, 2, 3))
    return (potential, kinetic)


def local(position, momentum_draw, viscosity, observed):
    chain_count = position.shape[0] * lax.axis_size("chain")
    cells = position.shape[1] * lax.axis_size("gx") * position.shape[2] * position.shape[3]
    local_first = jnp.sum(position, axis=0)
    local_second = jnp.sum(position * position, axis=0)
    first, second = lax.psum((local_first, local_second), "chain")
    mean_value = first / chain_count
    inverse_mass = 0.5 + second / chain_count - mean_value * mean_value

    def gradient(source):
        return gradient_narrow(source, viscosity, observed)

    moment = momentum_draw / jnp.sqrt(inverse_mass)
    source = position
    slope, misfit = gradient(source)
    start_potential, start_kinetic = local_sums(source, misfit, moment, inverse_mass)
    start_potential, start_kinetic = lax.psum((start_potential, start_kinetic), "gx")
    for leap in range(LEAPS):
        moment = moment - 0.5 * step_size * slope
        source = source + step_size * inverse_mass * moment
        slope, misfit = gradient(source)
        moment = moment - 0.5 * step_size * slope
    end_potential, end_kinetic = local_sums(source, misfit, moment, inverse_mass)
    end_potential, end_kinetic = lax.psum((end_potential, end_kinetic), "gx")
    energies = jnp.stack(
        [(start_potential + start_kinetic) / cells, (end_potential + end_kinetic) / cells]
    )
    return (source, moment, energies)


def solution(mesh):
    in_specs = (
        P("chain", "gx", None, None),
        P("chain", "gx", None, None),
        P("gx", None, None),
        P("gx", None, None),
    )
    out_specs = (P("chain", "gx", None, None), P("chain", "gx", None, None), P(None, "chain"))
    return jax.shard_map(local, mesh=mesh, in_specs=in_specs, out_specs=out_specs, check_vma=False)
```

profile of v0, /device:TPU:0, one launch (start us, length us, event | category | flops | bytes accessed | tf_op | source)
XLA Modules:
  0.0 222.0 jit_solution(4960773505325387408)
XLA Ops:
  7.2 1.1 fusion.200
  8.3 1.6 collective-permute-start
  9.9 5.2 %collective-permute-start.1 = (f32[2,1,16,1024]{3,2,1,0:T(8,128)S(1)}, f32[2,1,16,1024]{3,2,1,0:T(8,128)S(1)}, u32[]{:S(2)}, u32[]{:S(2)}) collective-permute-start(f32[2,1,16,1024]{3,2,1,0:T(8,128)S(1)} %get-tuple-element.35), channel_id=1, source_target_pairs={{1,0},{2,1},{3,2},{4,3},{5,4},{6,5},{7,6},{8,7},{9,8},{10,9},{11,1... | collective-permute-start | bytes 393224 | tf_op jit(solution)/shard_map/ppermute | solution.py:24
  15.1 2.8 %multiply_reduce_fusion.3 = (f32[2]{0:T(128)S(1)}, f32[8,16,1024]{2,1,0:T(8,128)}, f32[8,16,1024]{2,1,0:T(8,128)}) fusion(f32[2,8,16,1024]{3,2,1,0:T(8,128)} %param.4), kind=kLoop, calls=%fused_computation.371 | loop fusion | flops 786430 | bytes 2097160 | tf_op jit(solution)/shard_map/reduce_sum | solution.py:64
  19.2 4.6 %multiply_reduce_fusion.2 = (f32[2]{0:T(128)S(1)}, f32[2,8,16,1024]{3,2,1,0:T(8,128)S(1)}) fusion(f32[8,16,1024]{2,1,0:T(8,128)S(1)} %copy-done.6, f32[2,10,18,1026]{3,2,1,0:T(8,128)S(1)} %select_maximum_fusion.10, f32[2,1,16,1024]{3,2,1,0:T(8,128)S(1)} %collective-permute-done.1, f32[2,8,16,1024]{3,2,1,0:T(8,128)S(1)} %copy-done, ...), kind=kLoop, calls=%fused_computation.368 | loop fusion | flops 15466494 | bytes 28573704 | tf_op jit(solution)/shard_map/reduce_sum | solution.py:62
  24.0 6.2 %collective-permute-start.3 = (f32[2,1,16,1024]{3,2,1,0:T(8,128)S(1)}, f32[2,1,16,1024]{3,2,1,0:T(8,128)S(1)}, u32[]{:S(2)}, u32[]{:S(2)}) collective-permute-start(f32[2,1,16,1024]{3,2,1,0:T(8,128)S(1)} %get-tuple-element.33), channel_id=1, source_target_pairs={{1,0},{2,1},{3,2},{4,3},{5,4},{6,5},{7,6},{8,7},{9,8},{10,9},{11,1... | collective-permute-start | bytes 393224 | tf_op jit(solution)/shard_map/ppermute | solution.py:24
  30.3 2.9 %collective-permute-done.2 = f32[2,1,16,1024]{3,2,1,0:T(8,128)S(1)} collective-permute-done((f32[2,1,16,1024]{3,2,1,0:T(8,128)S(1)}, f32[2,1,16,1024]{3,2,1,0:T(8,128)S(1)}, u32[]{:S(2)}, u32[]{:S(2)}) %collective-permute-start.2) | collective-permute-done | bytes 131104 | tf_op jit(solution)/shard_map/ppermute | solution.py:21
  33.9 29.9 %all-reduce.10.cloned.1.call-done = (f32[8,16,1024]{2,1,0:T(8,128)}, f32[8,16,1024]{2,1,0:T(8,128)}) async-done(((f32[8,16,1024]{2,1,0:T(8,128)}, f32[8,16,1024]{2,1,0:T(8,128)}), (f32[8,16,1024]{2,1,0:T(8,128)}, f32[8,16,1024]{2,1,0:T(8,128)})) %all-reduce.10.cloned.1.call-update) | async-done | bytes 1048592 | tf_op jit(solution)/shard_map/psum | solution.py:74
  63.8 1.5 broadcast_multiply_fusion.2
  65.7 5.3 %multiply_add_fusion.1 = (f32[2,8,16,1024]{3,2,1,0:T(8,128)S(1)}, f32[2,8,16,1024]{3,2,1,0:T(8,128)}) fusion(f32[2,8,16,1024]{3,2,1,0:T(8,128)S(1)} %copy-done, f32[8,16,1024]{2,1,0:T(8,128)S(1)} %get-tuple-element.22, f32[2,10,18,1026]{3,2,1,0:T(8,128)S(1)} %select_maximum_fusion.8, f32[2,1,16,1024]{3,2,1,0:T(8,128)S(1)} %collective-permute-done.3, ...), kind=kLoop, calls=%fused_computation.370 | loop fusion | flops 16515072 | bytes 31719424 | tf_op jit(solution)/shard_map/add | solution.py:88
  71.0 1.5 collective-permute-start.4
  72.5 4.8 %collective-permute-start.5 = (f32[2,1,16,1024]{3,2,1,0:T(8,128)S(1)}, f32[2,1,16,1024]{3,2,1,0:T(8,128)S(1)}, u32[]{:S(2)}, u32[]{:S(2)}) collective-permute-start(f32[2,1,16,1024]{3,2,1,0:T(8,128)S(1)} %get-tuple-element.31), channel_id=1, source_target_pairs={{1,0},{2,1},{3,2},{4,3},{5,4},{6,5},{7,6},{8,7},{9,8},{10,9},{11,1... | collective-permute-start | bytes 393224 | tf_op jit(solution)/shard_map/ppermute | solution.py:24
  77.3 3.7 %collective-permute-done.4 = f32[2,1,16,1024]{3,2,1,0:T(8,128)S(1)} collective-permute-done((f32[2,1,16,1024]{3,2,1,0:T(8,128)S(1)}, f32[2,1,16,1024]{3,2,1,0:T(8,128)S(1)}, u32[]{:S(2)}, u32[]{:S(2)}) %collective-permute-start.4) | collective-permute-done | bytes 131104 | tf_op jit(solution)/shard_map/ppermute | solution.py:21
  81.8 4.5 %fusion.101 = f32[2,8,16,1024]{3,2,1,0:T(8,128)S(1)} fusion(f32[2,10,18,1026]{3,2,1,0:T(8,128)S(1)} %select_maximum_fusion.6, f32[2,1,16,1024]{3,2,1,0:T(8,128)S(1)} %collective-permute-done.5, f32[2,8,16,1024]{3,2,1,0:T(8,128)S(1)} %get-tuple-element.20, f32[2,1,16,1024]{3,2,1,0:T(8,128)S(1)} %collective-permute-done.4, f32[8,16,1024]{2,1,0:T(8,128)S(1)} %copy-done.7, ...), kind=kLoop, calls=%fused_computation.199 | loop fusion | flops 15204352 | bytes 28573696 | tf_op jit(solution)/shard_map/mul | solution.py:56
  86.3 6.2 %collective-permute-start.7 = (f32[2,1,16,1024]{3,2,1,0:T(8,128)S(1)}, f32[2,1,16,1024]{3,2,1,0:T(8,128)S(1)}, u32[]{:S(2)}, u32[]{:S(2)}) collective-permute-start(f32[2,1,16,1024]{3,2,1,0:T(8,128)S(1)} %get-tuple-element.29), channel_id=1, source_target_pairs={{1,0},{2,1},{3,2},{4,3},{5,4},{6,5},{7,6},{8,7},{9,8},{10,9},{11,1... | collective-permute-start | bytes 393224 | tf_op jit(solution)/shard_map/ppermute | solution.py:24
  92.6 2.9 %collective-permute-done.6 = f32[2,1,16,1024]{3,2,1,0:T(8,128)S(1)} collective-permute-done((f32[2,1,16,1024]{3,2,1,0:T(8,128)S(1)}, f32[2,1,16,1024]{3,2,1,0:T(8,128)S(1)}, u32[]{:S(2)}, u32[]{:S(2)}) %collective-permute-start.6) | collective-permute-done | bytes 131104 | tf_op jit(solution)/shard_map/ppermute | solution.py:21
  96.2 4.7 %multiply_reduce_fusion = (f32[2]{0:T(128)S(1)}, f32[2,8,16,1024]{3,2,1,0:T(8,128)S(1)}, f32[2,8,16,1024]{3,2,1,0:T(8,128)S(1)}) fusion(f32[2,8,16,1024]{3,2,1,0:T(8,128)S(1)} %get-tuple-element.20, f32[8,16,1024]{2,1,0:T(8,128)S(1)} %get-tuple-element.22, f32[2,8,16,1024]{3,2,1,0:T(8,128)S(1)} %copy-done.9, ...), kind=kLoop, calls=%fused_computation.366 | loop fusion | flops 17039358 | bytes 31195144 | tf_op jit(solution)/shard_map/reduce_sum | solution.py:64
  101.0 6.3 %collective-permute-start.9 = (f32[2,1,16,1024]{3,2,1,0:T(8,128)S(1)}, f32[2,1,16,1024]{3,2,1,0:T(8,128)S(1)}, u32[]{:S(2)}, u32[]{:S(2)}) collective-permute-start(f32[2,1,16,1024]{3,2,1,0:T(8,128)S(1)} %get-tuple-element.27), channel_id=1, source_target_pairs={{1,0},{2,1},{3,2},{4,3},{5,4},{6,5},{7,6},{8,7},{9,8},{10,9},{11,1... | collective-permute-start | bytes 393224 | tf_op jit(solution)/shard_map/ppermute | solution.py:24
  107.3 2.9 %collective-permute-done.8 = f32[2,1,16,1024]{3,2,1,0:T(8,128)S(1)} collective-permute-done((f32[2,1,16,1024]{3,2,1,0:T(8,128)S(1)}, f32[2,1,16,1024]{3,2,1,0:T(8,128)S(1)}, u32[]{:S(2)}, u32[]{:S(2)}) %collective-permute-start.8) | collective-permute-done | bytes 131104 | tf_op jit(solution)/shard_map/ppermute | solution.py:21
  110.9 4.6 %multiply_reduce_fusion.1 = (f32[2]{0:T(128)S(1)}, f32[2,8,16,1024]{3,2,1,0:T(8,128)S(1)}) fusion(f32[8,16,1024]{2,1,0:T(8,128)S(1)} %copy-done.7, f32[2,10,18,1026]{3,2,1,0:T(8,128)S(1)} %select_maximum_fusion.2, f32[2,1,16,1024]{3,2,1,0:T(8,128)S(1)} %collective-permute-done.9, f32[2,8,16,1024]{3,2,1,0:T(8,128)S(1)} %get-tuple-element.17, ...), kind=kLoop, calls=%fused_computation.367 | loop fusion | flops 15466494 | bytes 28573704 | tf_op jit(solution)/shard_map/reduce_sum | solution.py:62
  115.7 6.6 %collective-permute-start.11 = (f32[2,1,16,1024]{3,2,1,0:T(8,128)S(1)}, f32[2,1,16,1024]{3,2,1,0:T(8,128)S(1)}, u32[]{:S(2)}, u32[]{:S(2)}) collective-permute-start(f32[2,1,16,1024]{3,2,1,0:T(8,128)S(1)} %get-tuple-element.25), channel_id=1, source_target_pairs={{1,0},{2,1},{3,2},{4,3},{5,4},{6,5},{7,6},{8,7},{9,8},{10,9},{11,1... | collective-permute-start | bytes 393224 | tf_op jit(solution)/shard_map/ppermute | solution.py:24
  122.4 2.6 %collective-permute-done.10 = f32[2,1,16,1024]{3,2,1,0:T(8,128)S(1)} collective-permute-done((f32[2,1,16,1024]{3,2,1,0:T(8,128)S(1)}, f32[2,1,16,1024]{3,2,1,0:T(8,128)S(1)}, u32[]{:S(2)}, u32[]{:S(2)}) %collective-permute-start.10) | collective-permute-done | bytes 131104 | tf_op jit(solution)/shard_map/ppermute | solution.py:21
  125.7 5.5 %fusion.3 = (f32[2]{0:T(128)S(1)}, f32[2]{0:T(128)S(1)}, f32[2,8,16,1024]{3,2,1,0:T(8,128)}) fusion(f32[8,16,1024]{2,1,0:T(8,128)S(1)} %get-tuple-element.23, f32[2,8,16,1024]{3,2,1,0:T(8,128)S(1)} %copy-done.8, f32[8,16,1024]{2,1,0:T(8,128)S(1)} %sqrt.3, f32[2,8,16,1024]{3,2,1,0:T(8,128)S(1)} %get-tuple-element.18, ...), kind=kLoop, calls=%fused_computation.22 | loop fusion | flops 17563644 | bytes 31719440 | tf_op jit(solution)/shard_map/reduce_sum | solution.py:65
  131.2 83.3 %all-reduce.6 = (f32[2]{0:T(128)S(1)}, f32[2]{0:T(128)S(1)}) all-reduce(f32[2]{0:T(128)S(1)} %get-tuple-element.36, f32[2]{0:T(128)S(1)} %get-tuple-element.37), channel_id=1, replica_groups=mesh['chain'=4,'gx'=32] {'gx'}, use_global_device_ids=true, to_apply=%region_11.12 | all-reduce | flops 4 | bytes 32 | tf_op jit(solution)/shard_map/psum | solution.py:92
  (51 shorter events, 6.5 us)
Async XLA Ops:
  7.2 11.3 %copy-start = (f32[2,8,16,1024]{3,2,1,0:T(8,128)S(1)}, f32[2,8,16,1024]{3,2,1,0:T(8,128)}, u32[]{:S(2)}) copy-start(f32[2,8,16,1024]{3,2,1,0:T(8,128)} %param.4) | copy-start | bytes 3145732
  7.2 56.7 %all-reduce.10.cloned.1.call-start = ((), (), s32[]{:S(2)}) async-start(), calls=%async_computation | async-start | bytes 2097152 | tf_op jit(solution)/shard_map/psum | solution.py:74
  8.3 10.2 %collective-permute-start = (f32[2,1,16,1024]{3,2,1,0:T(8,128)S(1)}, f32[2,1,16,1024]{3,2,1,0:T(8,128)S(1)}, u32[]{:S(2)}, u32[]{:S(2)}) collective-permute-start(f32[2,1,16,1024]{3,2,1,0:T(8,128)S(1)} %get-tuple-element.34), channel_id=1, source_target_pairs={{0,1},{1,2},{2,3},{3,4},{4,5},{5,6},{6,7},{7,8},{8,9},{9,10},{10,1... | collective-permute-start | bytes 393224 | tf_op jit(solution)/shard_map/ppermute | solution.py:21
  9.9 8.6 %collective-permute-start.1 = (f32[2,1,16,1024]{3,2,1,0:T(8,128)S(1)}, f32[2,1,16,1024]{3,2,1,0:T(8,128)S(1)}, u32[]{:S(2)}, u32[]{:S(2)}) collective-permute-start(f32[2,1,16,1024]{3,2,1,0:T(8,128)S(1)} %get-tuple-element.35), channel_id=1, source_target_pairs={{1,0},{2,1},{3,2},{4,3},{5,4},{6,5},{7,6},{8,7},{9,8},{10,9},{11,1... | collective-permute-start | bytes 393224 | tf_op jit(solution)/shard_map/ppermute | solution.py:24
  17.8 1.4 copy-start.2
  17.9 1.4 copy-start.6
  23.9 9.3 %copy-start.4 = (f32[2,8,16,1024]{3,2,1,0:T(8,128)}, f32[2,8,16,1024]{3,2,1,0:T(8,128)S(1)}, u32[]{:S(2)}) copy-start(f32[2,8,16,1024]{3,2,1,0:T(8,128)S(1)} %broadcast_multiply_fusion.1) | copy-start | bytes 3145732
  24.0 9.3 %collective-permute-start.2 = (f32[2,1,16,1024]{3,2,1,0:T(8,128)S(1)}, f32[2,1,16,1024]{3,2,1,0:T(8,128)S(1)}, u32[]{:S(2)}, u32[]{:S(2)}) collective-permute-start(f32[2,1,16,1024]{3,2,1,0:T(8,128)S(1)} %get-tuple-element.32), channel_id=1, source_target_pairs={{0,1},{1,2},{2,3},{3,4},{4,5},{5,6},{6,7},{7,8},{8,9},{9,10},{10,1... | collective-permute-start | bytes 393224 | tf_op jit(solution)/shard_map/ppermute | solution.py:21
  24.0 9.2 %collective-permute-start.3 = (f32[2,1,16,1024]{3,2,1,0:T(8,128)S(1)}, f32[2,1,16,1024]{3,2,1,0:T(8,128)S(1)}, u32[]{:S(2)}, u32[]{:S(2)}) collective-permute-start(f32[2,1,16,1024]{3,2,1,0:T(8,128)S(1)} %get-tuple-element.33), channel_id=1, source_target_pairs={{1,0},{2,1},{3,2},{4,3},{5,4},{6,5},{7,6},{8,7},{9,8},{10,9},{11,1... | collective-permute-start | bytes 393224 | tf_op jit(solution)/shard_map/ppermute | solution.py:24
  63.8 1.6 copy-start.5
  63.8 1.9 copy-start.8
  71.0 10.8 %copy-start.3 = (f32[8,16,1024]{2,1,0:T(8,128)S(1)}, f32[8,16,1024]{2,1,0:T(8,128)}, u32[]{:S(2)}) copy-start(f32[8,16,1024]{2,1,0:T(8,128)} %param.6) | copy-start | bytes 1572868
  71.0 10.8 %copy-start.7 = (f32[8,16,1024]{2,1,0:T(8,128)S(1)}, f32[8,16,1024]{2,1,0:T(8,128)}, u32[]{:S(2)}) copy-start(f32[8,16,1024]{2,1,0:T(8,128)} %param.7) | copy-start | bytes 1572868
  71.0 10.0 %collective-permute-start.4 = (f32[2,1,16,1024]{3,2,1,0:T(8,128)S(1)}, f32[2,1,16,1024]{3,2,1,0:T(8,128)S(1)}, u32[]{:S(2)}, u32[]{:S(2)}) collective-permute-start(f32[2,1,16,1024]{3,2,1,0:T(8,128)S(1)} %get-tuple-element.30), channel_id=1, source_target_pairs={{0,1},{1,2},{2,3},{3,4},{4,5},{5,6},{6,7},{7,8},{8,9},{9,10},{10,1... | collective-permute-start | bytes 393224 | tf_op jit(solution)/shard_map/ppermute | solution.py:21
  72.5 8.5 %collective-permute-start.5 = (f32[2,1,16,1024]{3,2,1,0:T(8,128)S(1)}, f32[2,1,16,1024]{3,2,1,0:T(8,128)S(1)}, u32[]{:S(2)}, u32[]{:S(2)}) collective-permute-start(f32[2,1,16,1024]{3,2,1,0:T(8,128)S(1)} %get-tuple-element.31), channel_id=1, source_target_pairs={{1,0},{2,1},{3,2},{4,3},{5,4},{6,5},{7,6},{8,7},{9,8},{10,9},{11,1... | collective-permute-start | bytes 393224 | tf_op jit(solution)/shard_map/ppermute | solution.py:24
  86.2 10.0 %copy-start.9 = (f32[2,8,16,1024]{3,2,1,0:T(8,128)S(1)}, f32[2,8,16,1024]{3,2,1,0:T(8,128)}, u32[]{:S(2)}) copy-start(f32[2,8,16,1024]{3,2,1,0:T(8,128)} %get-tuple-element.21) | copy-start | bytes 3145732
  86.3 9.3 %collective-permute-start.6 = (f32[2,1,16,1024]{3,2,1,0:T(8,128)S(1)}, f32[2,1,16,1024]{3,2,1,0:T(8,128)S(1)}, u32[]{:S(2)}, u32[]{:S(2)}) collective-permute-start(f32[2,1,16,1024]{3,2,1,0:T(8,128)S(1)} %get-tuple-element.28), channel_id=1, source_target_pairs={{0,1},{1,2},{2,3},{3,4},{4,5},{5,6},{6,7},{7,8},{8,9},{9,10},{10,1... | collective-permute-start | bytes 393224 | tf_op jit(solution)/shard_map/ppermute | solution.py:21
  86.3 9.2 %collective-permute-start.7 = (f32[2,1,16,1024]{3,2,1,0:T(8,128)S(1)}, f32[2,1,16,1024]{3,2,1,0:T(8,128)S(1)}, u32[]{:S(2)}, u32[]{:S(2)}) collective-permute-start(f32[2,1,16,1024]{3,2,1,0:T(8,128)S(1)} %get-tuple-element.29), channel_id=1, source_target_pairs={{1,0},{2,1},{3,2},{4,3},{5,4},{6,5},{7,6},{8,7},{9,8},{10,9},{11,1... | collective-permute-start | bytes 393224 | tf_op jit(solution)/shard_map/ppermute | solution.py:24
  100.9 24.8 %copy-start.1 = (f32[2,8,16,1024]{3,2,1,0:T(8,128)}, f32[2,8,16,1024]{3,2,1,0:T(8,128)S(1)}, u32[]{:S(2)}) copy-start(f32[2,8,16,1024]{3,2,1,0:T(8,128)S(1)} %get-tuple-element.17) | copy-start | bytes 3145732
  101.0 9.3 %collective-permute-start.8 = (f32[2,1,16,1024]{3,2,1,0:T(8,128)S(1)}, f32[2,1,16,1024]{3,2,1,0:T(8,128)S(1)}, u32[]{:S(2)}, u32[]{:S(2)}) collective-permute-start(f32[2,1,16,1024]{3,2,1,0:T(8,128)S(1)} %get-tuple-element.26), channel_id=1, source_target_pairs={{0,1},{1,2},{2,3},{3,4},{4,5},{5,6},{6,7},{7,8},{8,9},{9,10},{10,1... | collective-permute-start | bytes 393224 | tf_op jit(solution)/shard_map/ppermute | solution.py:21
  101.0 9.2 %collective-permute-start.9 = (f32[2,1,16,1024]{3,2,1,0:T(8,128)S(1)}, f32[2,1,16,1024]{3,2,1,0:T(8,128)S(1)}, u32[]{:S(2)}, u32[]{:S(2)}) collective-permute-start(f32[2,1,16,1024]{3,2,1,0:T(8,128)S(1)} %get-tuple-element.27), channel_id=1, source_target_pairs={{1,0},{2,1},{3,2},{4,3},{5,4},{6,5},{7,6},{8,7},{9,8},{10,9},{11,1... | collective-permute-start | bytes 393224 | tf_op jit(solution)/shard_map/ppermute | solution.py:24
  115.7 9.3 %collective-permute-start.10 = (f32[2,1,16,1024]{3,2,1,0:T(8,128)S(1)}, f32[2,1,16,1024]{3,2,1,0:T(8,128)S(1)}, u32[]{:S(2)}, u32[]{:S(2)}) collective-permute-start(f32[2,1,16,1024]{3,2,1,0:T(8,128)S(1)} %get-tuple-element.24), channel_id=1, source_target_pairs={{0,1},{1,2},{2,3},{3,4},{4,5},{5,6},{6,7},{7,8},{8,9},{9,10},{10,1... | collective-permute-start | bytes 393224 | tf_op jit(solution)/shard_map/ppermute | solution.py:21
  115.7 9.3 %collective-permute-start.11 = (f32[2,1,16,1024]{3,2,1,0:T(8,128)S(1)}, f32[2,1,16,1024]{3,2,1,0:T(8,128)S(1)}, u32[]{:S(2)}, u32[]{:S(2)}) collective-permute-start(f32[2,1,16,1024]{3,2,1,0:T(8,128)S(1)} %get-tuple-element.25), channel_id=1, source_target_pairs={{1,0},{2,1},{3,2},{4,3},{5,4},{6,5},{7,6},{8,7},{9,8},{10,9},{11,1... | collective-permute-start | bytes 393224 | tf_op jit(solution)/shard_map/ppermute | solution.py:24
Sparse Core Ops, SparseCore 0:
  18.0 45.7 all-reduce.9
where the time goes:
time: 222 us
  blocking collectives  83.3 us (38%)
  waiting for transfers between devices  45.7 us (21%)
  starting transfers between devices  38.8 us (17%)
  other arithmetic  38.3 us (17%)
  between operations  14.3 us (6%)
    psum x1, blocking collectives, local(): end_potential, end_kinetic = lax.psum((end_potential, end_kinetic), 'gx')  83.3 us
    ppermute x6, starting transfers between devices, with_halo(): lax.ppermute(lax.slice_in_dim(block, 0, width, axis=dim), axis, backward)  35.3 us
    psum x1, waiting for transfers between devices, local(): first, second = lax.psum((local_first, local_second), 'chain')  29.9 us
    ppermute x6, waiting for transfers between devices, with_halo(): lax.ppermute(lax.slice_in_dim(block, block.shape[dim] - width, None, axis...  15.7 us
    reduce_sum x2, other arithmetic, local_sums(): jnp.sum(misfit * misfit, axis=(1, 2, 3))  9.17 us
    reduce_sum x2, other arithmetic, local_sums(): jnp.sum(source * source, axis=(1, 2, 3))  7.45 us
    reduce_sum x1, other arithmetic, local_sums(): kinetic = 0.5 * jnp.sum(inverse_mass * moment * moment, axis=(1, 2, 3))  5.51 us
    add x1, other arithmetic, local(): source = source + step_size * inverse_mass * moment  5.28 us
  transfers between devices with their start and end apart: 13, of which 7 were waited for; matrix products, arithmetic and copies ran while one was open for 4% of the time, Pallas kernels for 0%

commit v1 on v0

--- a/solution.py
+++ b/solution.py
@@ -66,14 +66,36 @@
     return (potential, kinetic)
 
 
+def chain_inverse_mass(position, chain_count):
+    count = lax.axis_size("chain")
+    near = [(i, i ^ 1) for i in range(count)]
+    far = [(i, i ^ 2) for i in range(count)]
+    sums = jnp.stack([jnp.sum(position, axis=0), jnp.sum(position * position, axis=0)], axis=1)
+    half = sums.shape[0] // 2
+    core = lax.axis_index("chain") % 2
+    keep = lax.dynamic_slice_in_dim(sums, half * core, half, 0)
+    send = lax.dynamic_slice_in_dim(sums, half * (1 - core), half, 0)
+    part = keep + lax.ppermute(send, "chain", near)
+    part = part + lax.ppermute(part, "chain", far)
+    mean_value = part[:, 0] / chain_count
+    mine = 0.5 + part[:, 1] / chain_count - mean_value * mean_value
+    other = lax.ppermute(mine, "chain", near)
+    return jnp.concatenate(
+        [jnp.where(core == 0, mine, other), jnp.where(core == 0, other, mine)], axis=0
+    )
+
+
+def slab_total(parts):
+    count = lax.axis_size("gx")
+    row = jnp.pad(parts.reshape(1, -1), ((0, 0), (0, 128 - parts.size)))
+    rows = lax.all_to_all(jnp.broadcast_to(row, (count, 128)), "gx", 0, 0, tiled=True)
+    return jnp.sum(rows, axis=0)[: parts.size].reshape(parts.shape)
+
+
 def local(position, momentum_draw, viscosity, observed):
     chain_count = position.shape[0] * lax.axis_size("chain")
     cells = position.shape[1] * lax.axis_size("gx") * position.shape[2] * position.shape[3]
-    local_first = jnp.sum(position, axis=0)
-    local_second = jnp.sum(position * position, axis=0)
-    first, second = lax.psum((local_first, local_second), "chain")
-    mean_value = first / chain_count
-    inverse_mass = 0.5 + second / chain_count - mean_value * mean_value
+    inverse_mass = chain_inverse_mass(position, chain_count)
 
     def gradient(source):
         return gradient_narrow(source, viscosity, observed)
@@ -82,17 +104,15 @@
     source = position
     slope, misfit = gradient(source)
     start_potential, start_kinetic = local_sums(source, misfit, moment, inverse_mass)
-    start_potential, start_kinetic = lax.psum((start_potential, start_kinetic), "gx")
     for leap in range(LEAPS):
         moment = moment - 0.5 * step_size * slope
         source = source + step_size * inverse_mass * moment
         slope, misfit = gradient(source)
         moment = moment - 0.5 * step_size * slope
     end_potential, end_kinetic = local_sums(source, misfit, moment, inverse_mass)
-    end_potential, end_kinetic = lax.psum((end_potential, end_kinetic), "gx")
-    energies = jnp.stack(
-        [(start_potential + start_kinetic) / cells, (end_potential + end_kinetic) / cells]
-    )
+    energies = slab_total(
+        jnp.stack([start_potential + start_kinetic, end_potential + end_kinetic])
+    ) / cells
     return (source, moment, energies)
 
 

time: 222 us -> 123 us (0.55)
  blocking collectives: 83.3 us -> 16.3 us
  waiting for transfers between devices: 45.7 us -> 22.3 us
  between operations: 14.3 us -> 0.93 us
  starting transfers between devices: 38.8 us -> 42.2 us
    psum x1 -> x0, blocking collectives: 83.3 us -> none  [local(): end_potential, end_kinetic = lax.psum((end_potential, end_kinetic), 'gx')]
    psum x1 -> x0, waiting for transfers between devices: 29.9 us -> none  [local(): first, second = lax.psum((local_first, local_second), 'chain')]
    all_to_all x0 -> x1, blocking collectives: none -> 16.3 us  [slab_total(): lax.all_to_all(jnp.broadcast_to(row, (count, 128)), 'gx', 0, 0, tiled=True)]
    ppermute x0 -> x3, waiting for transfers between devices: none -> 8.67 us  [the longest x1 7.88 us: chain_inverse_mass(): part = part + lax.ppermute(part, 'chain', far)]
    ppermute x0 -> x3, starting transfers between devices: none -> 3.75 us  [the longest x1 3.66 us: chain_inverse_mass(): part = part + lax.ppermute(part, 'chain', far)]
    add x0 -> x2, other arithmetic: none -> 2.26 us  [the longest x1 1.15 us: chain_inverse_mass(): part = part + lax.ppermute(part, 'chain', far)]
  transfers between devices with their start and end apart: 13 -> 15, of which waited for: 7 -> 7; matrix products, arithmetic and copies ran while one was open for 4% -> 8% of each run, Pallas kernels for 0% -> 0%
where the time goes in v1:
time: 123 us; the launch traced here: 122 us
  starting transfers between devices  42.2 us (34%)
  other arithmetic  37.9 us (31%)
  waiting for transfers between devices  22.3 us (18%)
  blocking collectives  16.3 us (13%)
  local copies, waits for them, and re-layouts  2.76 us (2%)
    ppermute x6, starting transfers between devices, with_halo(): lax.ppermute(lax.slice_in_dim(block, 0, width, axis=dim), axis, backward)  36.5 us
    all_to_all x1, blocking collectives, slab_total(): lax.all_to_all(jnp.broadcast_to(row, (count, 128)), 'gx', 0, 0, tiled=True)  16.3 us
    ppermute x6, waiting for transfers between devices, with_halo(): lax.ppermute(lax.slice_in_dim(block, block.shape[dim] - width, None, axis...  13.6 us
    reduce_sum x2, other arithmetic, local_sums(): jnp.sum(misfit * misfit, axis=(1, 2, 3))  9.13 us
    ppermute x1, waiting for transfers between devices, chain_inverse_mass(): part = part + lax.ppermute(part, 'chain', far)  7.88 us
    reduce_sum x2, other arithmetic, local_sums(): jnp.sum(source * source, axis=(1, 2, 3))  6.43 us
    reduce_sum x1, other arithmetic, local_sums(): kinetic = 0.5 * jnp.sum(inverse_mass * moment * moment, axis=(1, 2, 3))  5.55 us
    mul x3, other arithmetic, gradient_narrow(): scaled = viscosity * misfit  4.68 us
  transfers between devices with their start and end apart: 15, of which 7 were waited for; matrix products, arithmetic and copies ran while one was open for 8% of the time, Pallas kernels for 0%

profile of v1, /device:TPU:0, one launch (start us, length us, event | category | flops | bytes accessed | tf_op | source)
XLA Modules:
  0.0 122.4 jit_solution(10071992240004535853)
XLA Ops:
  0.6 1.7 %fusion.208 = (f32[2,1,16,1024]{3,2,1,0:T(8,128)}, f32[2,1,16,1024]{3,2,1,0:T(8,128)S(1)}) fusion(f32[2,8,16,1024]{3,2,1,0:T(8,128)} %param.4), kind=kLoop, calls=%fused_computation.404 | loop fusion | bytes 524288 | tf_op jit(solution)/shard_map/slice | solution.py:22
  2.4 1.6 %collective-permute-start.3 = (f32[2,1,16,1024]{3,2,1,0:T(8,128)}, f32[2,1,16,1024]{3,2,1,0:T(8,128)S(1)}, u32[]{:S(2)}, u32[]{:S(2)}) collective-permute-start(f32[2,1,16,1024]{3,2,1,0:T(8,128)} %get-tuple-element.28), channel_id=1, source_target_pairs={{0,1},{1,2},{2,3},{3,4},{4,5},{5,6},{6,7},{7,8},{8,9},{9,10},{10,1... | collective-permute-start | bytes 393224 | tf_op jit(solution)/shard_map/ppermute | solution.py:21
  4.0 5.1 %collective-permute-start.4 = (f32[2,1,16,1024]{3,2,1,0:T(8,128)S(1)}, f32[2,1,16,1024]{3,2,1,0:T(8,128)S(1)}, u32[]{:S(2)}, u32[]{:S(2)}) collective-permute-start(f32[2,1,16,1024]{3,2,1,0:T(8,128)S(1)} %get-tuple-element.29), channel_id=1, source_target_pairs={{1,0},{2,1},{3,2},{4,3},{5,4},{6,5},{7,6},{8,7},{9,8},{10,9},{11,1... | collective-permute-start | bytes 393224 | tf_op jit(solution)/shard_map/ppermute | solution.py:24
  9.0 1.8 %multiply_reduce_fusion.3 = (f32[2]{0:T(128)S(1)}, f32[8,16,1024]{2,1,0:T(8,128)S(1)}, f32[8,16,1024]{2,1,0:T(8,128)S(1)}) fusion(f32[2,8,16,1024]{3,2,1,0:T(8,128)} %param.4), kind=kLoop, calls=%fused_computation.375 | loop fusion | flops 786430 | bytes 2097160 | tf_op jit(solution)/shard_map/reduce_sum | solution.py:64
  13.5 4.6 %multiply_reduce_fusion.2 = (f32[2]{0:T(128)S(1)}, f32[2,8,16,1024]{3,2,1,0:T(8,128)S(1)}) fusion(f32[8,16,1024]{2,1,0:T(8,128)S(1)} %copy-done.3, f32[2,10,18,1026]{3,2,1,0:T(8,128)S(1)} %select_maximum_fusion.10, f32[2,1,16,1024]{3,2,1,0:T(8,128)S(1)} %collective-permute-done.4, f32[2,8,16,1024]{3,2,1,0:T(8,128)S(1)} %copy-done, ...), kind=kLoop, calls=%fused_computation.372 | loop fusion | flops 15466494 | bytes 28573704 | tf_op jit(solution)/shard_map/reduce_sum | solution.py:62
  18.0 1.1 fusion.193
  19.1 3.7 %collective-permute-start.1 = (f32[4,2,16,1024]{3,2,0,1:T(8,128)S(1)}, f32[4,2,16,1024]{3,2,0,1:T(8,128)S(1)}, u32[]{:S(2)}, u32[]{:S(2)}) collective-permute-start(f32[4,2,16,1024]{3,2,0,1:T(8,128)S(1)} %fusion.193), channel_id=1, source_target_pairs={{0,64},{32,96},{64,0},{96,32},{1,65},{33,97},{65,1},{97,33},{2,66}... | collective-permute-start | bytes 1572872 | tf_op jit(solution)/shard_map/ppermute | solution.py:79
  23.0 6.2 %collective-permute-start.6 = (f32[2,1,16,1024]{3,2,1,0:T(8,128)S(1)}, f32[2,1,16,1024]{3,2,1,0:T(8,128)S(1)}, u32[]{:S(2)}, u32[]{:S(2)}) collective-permute-start(f32[2,1,16,1024]{3,2,1,0:T(8,128)S(1)} %get-tuple-element.27), channel_id=1, source_target_pairs={{1,0},{2,1},{3,2},{4,3},{5,4},{6,5},{7,6},{8,7},{9,8},{10,9},{11,1... | collective-permute-start | bytes 393224 | tf_op jit(solution)/shard_map/ppermute | solution.py:24
  29.3 7.9 %collective-permute-done.1 = f32[4,2,16,1024]{3,2,0,1:T(8,128)S(1)} collective-permute-done((f32[4,2,16,1024]{3,2,0,1:T(8,128)S(1)}, f32[4,2,16,1024]{3,2,0,1:T(8,128)S(1)}, u32[]{:S(2)}, u32[]{:S(2)}) %collective-permute-start.1) | collective-permute-done | bytes 524320 | tf_op jit(solution)/shard_map/ppermute | solution.py:79
  37.2 1.2 fusion.209
  40.4 4.5 %multiply_add_fusion.1 = (f32[2,8,16,1024]{3,2,1,0:T(8,128)S(1)}, f32[2,8,16,1024]{3,2,1,0:T(8,128)S(1)}) fusion(f32[2,8,16,1024]{3,2,1,0:T(8,128)S(1)} %copy-done, f32[8,16,1024]{2,1,0:T(8,128)S(1)} %get-tuple-element.31, f32[2,10,18,1026]{3,2,1,0:T(8,128)S(1)} %select_maximum_fusion.8, f32[2,1,16,1024]{3,2,1,0:T(8,128)S(1)} %collective-permute-done.6, ...), kind=kLoop, calls=%fused_computation.374 | loop fusion | flops 16515072 | bytes 31719424 | tf_op jit(solution)/shard_map/add | solution.py:109
  45.1 6.2 %collective-permute-start.8 = (f32[2,1,16,1024]{3,2,1,0:T(8,128)S(1)}, f32[2,1,16,1024]{3,2,1,0:T(8,128)S(1)}, u32[]{:S(2)}, u32[]{:S(2)}) collective-permute-start(f32[2,1,16,1024]{3,2,1,0:T(8,128)S(1)} %get-tuple-element.25), channel_id=1, source_target_pairs={{1,0},{2,1},{3,2},{4,3},{5,4},{6,5},{7,6},{8,7},{9,8},{10,9},{11,1... | collective-permute-start | bytes 393224 | tf_op jit(solution)/shard_map/ppermute | solution.py:24
  51.3 3.9 %collective-permute-done.7 = f32[2,1,16,1024]{3,2,1,0:T(8,128)S(1)} collective-permute-done((f32[2,1,16,1024]{3,2,1,0:T(8,128)S(1)}, f32[2,1,16,1024]{3,2,1,0:T(8,128)S(1)}, u32[]{:S(2)}, u32[]{:S(2)}) %collective-permute-start.7) | collective-permute-done | bytes 131104 | tf_op jit(solution)/shard_map/ppermute | solution.py:21
  55.9 4.4 %fusion.101 = f32[2,8,16,1024]{3,2,1,0:T(8,128)S(1)} fusion(f32[2,10,18,1026]{3,2,1,0:T(8,128)S(1)} %select_maximum_fusion.6, f32[2,1,16,1024]{3,2,1,0:T(8,128)S(1)} %collective-permute-done.8, f32[2,8,16,1024]{3,2,1,0:T(8,128)S(1)} %get-tuple-element.16, f32[2,1,16,1024]{3,2,1,0:T(8,128)S(1)} %collective-permute-done.7, f32[8,16,1024]{2,1,0:T(8,128)S(1)} %copy-done.3, ...), kind=kLoop, calls=%fused_computation.203 | loop fusion | flops 15204352 | bytes 28573696 | tf_op jit(solution)/shard_map/mul | solution.py:56
  60.4 6.2 %collective-permute-start.10 = (f32[2,1,16,1024]{3,2,1,0:T(8,128)S(1)}, f32[2,1,16,1024]{3,2,1,0:T(8,128)S(1)}, u32[]{:S(2)}, u32[]{:S(2)}) collective-permute-start(f32[2,1,16,1024]{3,2,1,0:T(8,128)S(1)} %get-tuple-element.23), channel_id=1, source_target_pairs={{1,0},{2,1},{3,2},{4,3},{5,4},{6,5},{7,6},{8,7},{9,8},{10,9},{11,1... | collective-permute-start | bytes 393224 | tf_op jit(solution)/shard_map/ppermute | solution.py:24
  66.6 3.1 %collective-permute-done.9 = f32[2,1,16,1024]{3,2,1,0:T(8,128)S(1)} collective-permute-done((f32[2,1,16,1024]{3,2,1,0:T(8,128)S(1)}, f32[2,1,16,1024]{3,2,1,0:T(8,128)S(1)}, u32[]{:S(2)}, u32[]{:S(2)}) %collective-permute-start.9) | collective-permute-done | bytes 131104 | tf_op jit(solution)/shard_map/ppermute | solution.py:21
  70.4 4.7 %multiply_reduce_fusion = (f32[2]{0:T(128)S(1)}, f32[2,8,16,1024]{3,2,1,0:T(8,128)S(1)}, f32[2,8,16,1024]{3,2,1,0:T(8,128)S(1)}) fusion(f32[2,8,16,1024]{3,2,1,0:T(8,128)S(1)} %get-tuple-element.16, f32[8,16,1024]{2,1,0:T(8,128)S(1)} %get-tuple-element.31, f32[2,8,16,1024]{3,2,1,0:T(8,128)S(1)} %get-tuple-element.17, ...), kind=kLoop, calls=%fused_computation.370 | loop fusion | flops 17039358 | bytes 31195144 | tf_op jit(solution)/shard_map/reduce_sum | solution.py:64
  75.2 6.2 %collective-permute-start.12 = (f32[2,1,16,1024]{3,2,1,0:T(8,128)S(1)}, f32[2,1,16,1024]{3,2,1,0:T(8,128)S(1)}, u32[]{:S(2)}, u32[]{:S(2)}) collective-permute-start(f32[2,1,16,1024]{3,2,1,0:T(8,128)S(1)} %get-tuple-element.21), channel_id=1, source_target_pairs={{1,0},{2,1},{3,2},{4,3},{5,4},{6,5},{7,6},{8,7},{9,8},{10,9},{11,1... | collective-permute-start | bytes 393224 | tf_op jit(solution)/shard_map/ppermute | solution.py:24
  81.4 2.9 %collective-permute-done.11 = f32[2,1,16,1024]{3,2,1,0:T(8,128)S(1)} collective-permute-done((f32[2,1,16,1024]{3,2,1,0:T(8,128)S(1)}, f32[2,1,16,1024]{3,2,1,0:T(8,128)S(1)}, u32[]{:S(2)}, u32[]{:S(2)}) %collective-permute-start.11) | collective-permute-done | bytes 131104 | tf_op jit(solution)/shard_map/ppermute | solution.py:21
  85.1 4.6 %multiply_reduce_fusion.1 = (f32[2]{0:T(128)S(1)}, f32[2,8,16,1024]{3,2,1,0:T(8,128)S(1)}) fusion(f32[8,16,1024]{2,1,0:T(8,128)S(1)} %copy-done.3, f32[2,10,18,1026]{3,2,1,0:T(8,128)S(1)} %select_maximum_fusion.2, f32[2,1,16,1024]{3,2,1,0:T(8,128)S(1)} %collective-permute-done.12, f32[2,8,16,1024]{3,2,1,0:T(8,128)S(1)} %get-tuple-element.13, ...), kind=kLoop, calls=%fused_computation.371 | loop fusion | flops 15466494 | bytes 28573704 | tf_op jit(solution)/shard_map/reduce_sum | solution.py:62
  89.9 6.5 %collective-permute-start.14 = (f32[2,1,16,1024]{3,2,1,0:T(8,128)S(1)}, f32[2,1,16,1024]{3,2,1,0:T(8,128)S(1)}, u32[]{:S(2)}, u32[]{:S(2)}) collective-permute-start(f32[2,1,16,1024]{3,2,1,0:T(8,128)S(1)} %get-tuple-element.19), channel_id=1, source_target_pairs={{1,0},{2,1},{3,2},{4,3},{5,4},{6,5},{7,6},{8,7},{9,8},{10,9},{11,1... | collective-permute-start | bytes 393224 | tf_op jit(solution)/shard_map/ppermute | solution.py:24
  96.4 2.6 %collective-permute-done.13 = f32[2,1,16,1024]{3,2,1,0:T(8,128)S(1)} collective-permute-done((f32[2,1,16,1024]{3,2,1,0:T(8,128)S(1)}, f32[2,1,16,1024]{3,2,1,0:T(8,128)S(1)}, u32[]{:S(2)}, u32[]{:S(2)}) %collective-permute-start.13) | collective-permute-done | bytes 131104 | tf_op jit(solution)/shard_map/ppermute | solution.py:21
  99.8 5.5 %fusion.3 = (f32[2]{0:T(128)S(1)}, f32[2]{0:T(128)S(1)}, f32[2,8,16,1024]{3,2,1,0:T(8,128)}) fusion(f32[8,16,1024]{2,1,0:T(8,128)S(1)} %get-tuple-element.30, f32[2,8,16,1024]{3,2,1,0:T(8,128)S(1)} %copy-done.4, f32[8,16,1024]{2,1,0:T(8,128)S(1)} %get-tuple-element.32, f32[2,8,16,1024]{3,2,1,0:T(8,128)S(1)} %get-tuple-element.14, ...), kind=kLoop, calls=%fused_computation.26 | loop fusion | flops 17563644 | bytes 31719440 | tf_op jit(solution)/shard_map/reduce_sum | solution.py:65
  105.4 16.3 %all_to_all.6 = f32[32,1,128]{2,1,0:T(1,128)S(1)} all-to-all(f32[32,1,128]{2,1,0:T(1,128)S(1)} %broadcast_in_dim.2), channel_id=1, replica_groups=mesh['chain'=4,'gx'=32] {'gx'}, dimensions={0} | all-to-all | bytes 32768 | tf_op jit(solution)/shard_map/all_to_all | solution.py:91
  (52 shorter events, 9.0 us)
Async XLA Ops:
  0.6 12.1 %copy-start = (f32[2,8,16,1024]{3,2,1,0:T(8,128)S(1)}, f32[2,8,16,1024]{3,2,1,0:T(8,128)}, u32[]{:S(2)}) copy-start(f32[2,8,16,1024]{3,2,1,0:T(8,128)} %param.4) | copy-start | bytes 3145732
  2.4 10.3 %collective-permute-start.3 = (f32[2,1,16,1024]{3,2,1,0:T(8,128)}, f32[2,1,16,1024]{3,2,1,0:T(8,128)S(1)}, u32[]{:S(2)}, u32[]{:S(2)}) collective-permute-start(f32[2,1,16,1024]{3,2,1,0:T(8,128)} %get-tuple-element.28), channel_id=1, source_target_pairs={{0,1},{1,2},{2,3},{3,4},{4,5},{5,6},{6,7},{7,8},{8,9},{9,10},{10,1... | collective-permute-start | bytes 393224 | tf_op jit(solution)/shard_map/ppermute | solution.py:21
  4.0 8.8 %collective-permute-start.4 = (f32[2,1,16,1024]{3,2,1,0:T(8,128)S(1)}, f32[2,1,16,1024]{3,2,1,0:T(8,128)S(1)}, u32[]{:S(2)}, u32[]{:S(2)}) collective-permute-start(f32[2,1,16,1024]{3,2,1,0:T(8,128)S(1)} %get-tuple-element.29), channel_id=1, source_target_pairs={{1,0},{2,1},{3,2},{4,3},{5,4},{6,5},{7,6},{8,7},{9,8},{10,9},{11,1... | collective-permute-start | bytes 393224 | tf_op jit(solution)/shard_map/ppermute | solution.py:24
  10.8 2.6 %copy-start.2 = (f32[8,16,1024]{2,1,0:T(8,128)S(1)}, f32[8,16,1024]{2,1,0:T(8,128)}, u32[]{:S(2)}) copy-start(f32[8,16,1024]{2,1,0:T(8,128)} %param.6) | copy-start | bytes 1572868
  10.8 2.6 %copy-start.3 = (f32[8,16,1024]{2,1,0:T(8,128)S(1)}, f32[8,16,1024]{2,1,0:T(8,128)}, u32[]{:S(2)}) copy-start(f32[8,16,1024]{2,1,0:T(8,128)} %param.7) | copy-start | bytes 1572868
  11.7 6.3 %collective-permute-start = (f32[4,2,16,1024]{3,2,0,1:T(8,128)}, f32[4,2,16,1024]{3,2,0,1:T(8,128)}, u32[]{:S(2)}, u32[]{:S(2)}) collective-permute-start(f32[4,2,16,1024]{3,2,0,1:T(8,128)} %fusion.191), channel_id=1, source_target_pairs={{0,32},{32,0},{64,96},{96,64},{1,33},{33,1},{65,97},{97,65},{2,34}... | collective-permute-start | bytes 1572872 | tf_op jit(solution)/shard_map/ppermute | solution.py:78
  19.1 18.0 %collective-permute-start.1 = (f32[4,2,16,1024]{3,2,0,1:T(8,128)S(1)}, f32[4,2,16,1024]{3,2,0,1:T(8,128)S(1)}, u32[]{:S(2)}, u32[]{:S(2)}) collective-permute-start(f32[4,2,16,1024]{3,2,0,1:T(8,128)S(1)} %fusion.193), channel_id=1, source_target_pairs={{0,64},{32,96},{64,0},{96,32},{1,65},{33,97},{65,1},{97,33},{2,66}... | collective-permute-start | bytes 1572872 | tf_op jit(solution)/shard_map/ppermute | solution.py:79
  23.0 15.5 %collective-permute-start.5 = (f32[2,1,16,1024]{3,2,1,0:T(8,128)S(1)}, f32[2,1,16,1024]{3,2,1,0:T(8,128)S(1)}, u32[]{:S(2)}, u32[]{:S(2)}) collective-permute-start(f32[2,1,16,1024]{3,2,1,0:T(8,128)S(1)} %get-tuple-element.26), channel_id=1, source_target_pairs={{0,1},{1,2},{2,3},{3,4},{4,5},{5,6},{6,7},{7,8},{8,9},{9,10},{10,1... | collective-permute-start | bytes 393224 | tf_op jit(solution)/shard_map/ppermute | solution.py:21
  23.0 15.4 %collective-permute-start.6 = (f32[2,1,16,1024]{3,2,1,0:T(8,128)S(1)}, f32[2,1,16,1024]{3,2,1,0:T(8,128)S(1)}, u32[]{:S(2)}, u32[]{:S(2)}) collective-permute-start(f32[2,1,16,1024]{3,2,1,0:T(8,128)S(1)} %get-tuple-element.27), channel_id=1, source_target_pairs={{1,0},{2,1},{3,2},{4,3},{5,4},{6,5},{7,6},{8,7},{9,8},{10,9},{11,1... | collective-permute-start | bytes 393224 | tf_op jit(solution)/shard_map/ppermute | solution.py:24
  38.4 1.6 %collective-permute-start.2 = (f32[4,16,1024]{2,1,0:T(8,128)S(1)}, f32[4,16,1024]{2,1,0:T(8,128)S(1)}, u32[]{:S(2)}, u32[]{:S(2)}) collective-permute-start(f32[4,16,1024]{2,1,0:T(8,128)S(1)} %fusion.196), channel_id=1, source_target_pairs={{0,32},{32,0},{64,96},{96,64},{1,33},{33,1},{65,97},{97,65},{2,34}... | collective-permute-start | bytes 786440 | tf_op jit(solution)/shard_map/ppermute | solution.py:82
  39.2 1.2 %copy-start.4 = (f32[2,8,16,1024]{3,2,1,0:T(8,128)S(1)}, f32[2,8,16,1024]{3,2,1,0:T(8,128)}, u32[]{:S(2)}) copy-start(f32[2,8,16,1024]{3,2,1,0:T(8,128)} %param.5) | copy-start | bytes 3145732
  45.0 10.2 %collective-permute-start.7 = (f32[2,1,16,1024]{3,2,1,0:T(8,128)S(1)}, f32[2,1,16,1024]{3,2,1,0:T(8,128)S(1)}, u32[]{:S(2)}, u32[]{:S(2)}) collective-permute-start(f32[2,1,16,1024]{3,2,1,0:T(8,128)S(1)} %get-tuple-element.24), channel_id=1, source_target_pairs={{0,1},{1,2},{2,3},{3,4},{4,5},{5,6},{6,7},{7,8},{8,9},{9,10},{10,1... | collective-permute-start | bytes 393224 | tf_op jit(solution)/shard_map/ppermute | solution.py:21
  45.1 10.1 %collective-permute-start.8 = (f32[2,1,16,1024]{3,2,1,0:T(8,128)S(1)}, f32[2,1,16,1024]{3,2,1,0:T(8,128)S(1)}, u32[]{:S(2)}, u32[]{:S(2)}) collective-permute-start(f32[2,1,16,1024]{3,2,1,0:T(8,128)S(1)} %get-tuple-element.25), channel_id=1, source_target_pairs={{1,0},{2,1},{3,2},{4,3},{5,4},{6,5},{7,6},{8,7},{9,8},{10,9},{11,1... | collective-permute-start | bytes 393224 | tf_op jit(solution)/shard_map/ppermute | solution.py:24
  60.3 9.4 %collective-permute-start.9 = (f32[2,1,16,1024]{3,2,1,0:T(8,128)S(1)}, f32[2,1,16,1024]{3,2,1,0:T(8,128)S(1)}, u32[]{:S(2)}, u32[]{:S(2)}) collective-permute-start(f32[2,1,16,1024]{3,2,1,0:T(8,128)S(1)} %get-tuple-element.22), channel_id=1, source_target_pairs={{0,1},{1,2},{2,3},{3,4},{4,5},{5,6},{6,7},{7,8},{8,9},{9,10},{10,1... | collective-permute-start | bytes 393224 | tf_op jit(solution)/shard_map/ppermute | solution.py:21
  60.4 9.3 %collective-permute-start.10 = (f32[2,1,16,1024]{3,2,1,0:T(8,128)S(1)}, f32[2,1,16,1024]{3,2,1,0:T(8,128)S(1)}, u32[]{:S(2)}, u32[]{:S(2)}) collective-permute-start(f32[2,1,16,1024]{3,2,1,0:T(8,128)S(1)} %get-tuple-element.23), channel_id=1, source_target_pairs={{1,0},{2,1},{3,2},{4,3},{5,4},{6,5},{7,6},{8,7},{9,8},{10,9},{11,1... | collective-permute-start | bytes 393224 | tf_op jit(solution)/shard_map/ppermute | solution.py:24
  75.1 24.7 %copy-start.1 = (f32[2,8,16,1024]{3,2,1,0:T(8,128)}, f32[2,8,16,1024]{3,2,1,0:T(8,128)S(1)}, u32[]{:S(2)}) copy-start(f32[2,8,16,1024]{3,2,1,0:T(8,128)S(1)} %get-tuple-element.13) | copy-start | bytes 3145732
  75.1 9.3 %collective-permute-start.11 = (f32[2,1,16,1024]{3,2,1,0:T(8,128)S(1)}, f32[2,1,16,1024]{3,2,1,0:T(8,128)S(1)}, u32[]{:S(2)}, u32[]{:S(2)}) collective-permute-start(f32[2,1,16,1024]{3,2,1,0:T(8,128)S(1)} %get-tuple-element.20), channel_id=1, source_target_pairs={{0,1},{1,2},{2,3},{3,4},{4,5},{5,6},{6,7},{7,8},{8,9},{9,10},{10,1... | collective-permute-start | bytes 393224 | tf_op jit(solution)/shard_map/ppermute | solution.py:21
  75.2 9.2 %collective-permute-start.12 = (f32[2,1,16,1024]{3,2,1,0:T(8,128)S(1)}, f32[2,1,16,1024]{3,2,1,0:T(8,128)S(1)}, u32[]{:S(2)}, u32[]{:S(2)}) collective-permute-start(f32[2,1,16,1024]{3,2,1,0:T(8,128)S(1)} %get-tuple-element.21), channel_id=1, source_target_pairs={{1,0},{2,1},{3,2},{4,3},{5,4},{6,5},{7,6},{8,7},{9,8},{10,9},{11,1... | collective-permute-start | bytes 393224 | tf_op jit(solution)/shard_map/ppermute | solution.py:24
  89.8 9.3 %collective-permute-start.13 = (f32[2,1,16,1024]{3,2,1,0:T(8,128)S(1)}, f32[2,1,16,1024]{3,2,1,0:T(8,128)S(1)}, u32[]{:S(2)}, u32[]{:S(2)}) collective-permute-start(f32[2,1,16,1024]{3,2,1,0:T(8,128)S(1)} %get-tuple-element.18), channel_id=1, source_target_pairs={{0,1},{1,2},{2,3},{3,4},{4,5},{5,6},{6,7},{7,8},{8,9},{9,10},{10,1... | collective-permute-start | bytes 393224 | tf_op jit(solution)/shard_map/ppermute | solution.py:21
  89.9 9.2 %collective-permute-start.14 = (f32[2,1,16,1024]{3,2,1,0:T(8,128)S(1)}, f32[2,1,16,1024]{3,2,1,0:T(8,128)S(1)}, u32[]{:S(2)}, u32[]{:S(2)}) collective-permute-start(f32[2,1,16,1024]{3,2,1,0:T(8,128)S(1)} %get-tuple-element.19), channel_id=1, source_target_pairs={{1,0},{2,1},{3,2},{4,3},{5,4},{6,5},{7,6},{8,7},{9,8},{10,9},{11,1... | collective-permute-start | bytes 393224 | tf_op jit(solution)/shard_map/ppermute | solution.py:24

commit v2 on v0

v2 whole, which is shorter than its diff:
```python
import jax
import jax.numpy as jnp
from jax import lax
from jax.experimental import pallas as pl
from jax.experimental.pallas import tpu as pltpu
from jax.sharding import PartitionSpec as P

LEAPS = 2

unit = -0.05
inv_noise = 0.25
prior_weight = 0.5
step_size = 0.05
LANES = 128
WIDE = 2


def call(kernel, out_shapes, scratch, name, work):
    spec = pl.BlockSpec(memory_space=pltpu.VMEM)
    return pl.pallas_call(
        kernel,
        out_shape=[jax.ShapeDtypeStruct(shape, jnp.float32) for shape in out_shapes],
        out_specs=[spec] * len(out_shapes),
        scratch_shapes=[pltpu.VMEM(shape, jnp.float32) for shape in scratch],
        compiler_params=pltpu.CompilerParams(vmem_limit_bytes=32 << 20),
        cost_estimate=pl.CostEstimate(flops=work, bytes_accessed=work // 8, transcendentals=0),
        name=name,
    )


def tiles(width):
    return [slice(j * LANES, (j + 1) * LANES) for j in range(width // LANES)]


def depth_sum(v):
    depth = v.shape[0]
    row = lax.broadcasted_iota(jnp.int32, v.shape, 0)
    below = jnp.where(row == 0, 0.0, pltpu.roll(v, 1, 0))
    above = jnp.where(row == depth - 1, 0.0, pltpu.roll(v, depth - 1, 0))
    return below + above


def stencil_plane(field, deep, chain, plane):
    cuts = tiles(field.shape[-1])
    edge_terms, own_terms = [], []
    for cut in cuts:
        v = field[chain, plane, :, cut]
        w = deep[chain, plane, :, cut] + (
            field[chain, plane - 1, :, cut] + field[chain, plane + 1, :, cut]
        )
        corner = deep[chain, plane - 1, :, cut] + deep[chain, plane + 1, :, cut]
        t = 6.0 * v + (2.0 * w + corner)
        d = t + w
        edge_terms.append(t)
        own_terms.append((d + d) - 92.0 * v)
    lane = lax.broadcasted_iota(jnp.int32, edge_terms[0].shape, 1)
    ups = [pltpu.roll(t, 1, 1) for t in edge_terms]
    downs = [pltpu.roll(t, LANES - 1, 1) for t in edge_terms]
    result = []
    for j in range(len(cuts)):
        before = ups[j - 1] if j else 0.0
        after = downs[j + 1] if j + 1 < len(cuts) else 0.0
        left = jnp.where(lane == 0, before, ups[j])
        right = jnp.where(lane == LANES - 1, after, downs[j])
        result.append(own_terms[j] + (left + right))
    return list(zip(cuts, result, strict=True))


def fill(field, deep, chain, target, source, index):
    for cut in tiles(field.shape[-1]):
        v = source[index + (slice(None), cut)]
        field[chain, target, :, cut] = v
        deep[chain, target, :, cut] = depth_sum(v)


def extend(q, low, high, field, deep):
    chains, planes = q.shape[:2]
    for chain in range(chains):
        for i in range(WIDE):
            fill(field, deep, chain, i, low, (chain * WIDE + i,))
            fill(field, deep, chain, WIDE + planes + i, high, (chain * WIDE + i,))

        def body(x, carry, chain=chain):
            fill(field, deep, chain, WIDE + x, q, (chain, x))
            return carry

        lax.fori_loop(0, planes, body, 0)


def weigh(field, deep, viscous, target, scaled, scaled_deep, want):
    chains, planes = field.shape[0], field.shape[1] - 2 * WIDE
    totals = []
    for chain in range(chains):

        def plane(x, total, chain=chain):
            for cut, k in stencil_plane(field, deep, chain, x + 1):
                nu = viscous[x, :, cut]
                misfit = (unit * nu) * k - target[x, :, cut]
                s = nu * misfit
                scaled[chain, x, :, cut] = s
                scaled_deep[chain, x, :, cut] = depth_sum(s)
                if total is not None:
                    total = total + misfit * misfit
            return total

        def rim(i, carry, plane=plane):
            plane(i * (planes + 1), None)
            return carry

        lax.fori_loop(0, 2, rim, 0)
        if want:
            zero = jnp.zeros((field.shape[2], LANES), jnp.float32)
            totals.append(lax.fori_loop(1, planes + 1, plane, zero))
        else:

            def quiet(x, carry, plane=plane):
                plane(x, None)
                return carry

            lax.fori_loop(1, planes + 1, quiet, 0)
    return totals


def fold(total):
    return total[:8] + total[8:]


def start_kernel(q, nu, obs, keep, send, to_high, to_low):
    core = lax.rem(lax.axis_index("chain"), 2)
    chains, planes = q.shape[:2]
    half = planes // 2

    def body(x, carry):
        for out, base in ((keep, core * half), (send, (1 - core) * half)):
            for cut in tiles(q.shape[-1]):
                first = q[0, base + x, :, cut]
                second = first * first
                for chain in range(1, chains):
                    v = q[chain, base + x, :, cut]
                    first = first + v
                    second = second + v * v
                out[x, 0, :, cut] = first
                out[x, 1, :, cut] = second
        return carry

    lax.fori_loop(0, half, body, 0)
    for chain in range(chains):
        for i in range(WIDE):
            to_high[chain * WIDE + i] = q[chain, planes - WIDE + i]
            to_low[chain * WIDE + i] = q[chain, i]
    to_high[chains * WIDE] = nu[planes - 1]
    to_low[chains * WIDE] = nu[0]
    to_high[chains * WIDE + 1] = obs[planes - 1]
    to_low[chains * WIDE + 1] = obs[0]


def first_kernel(q, low, high, nu, obs, slope, nu_wide, obs_wide, potential, field, deep, scaled, scaled_deep):
    chains, planes = q.shape[:2]
    for wide, own, at in ((nu_wide, nu, chains * WIDE), (obs_wide, obs, chains * WIDE + 1)):
        wide[0] = low[at]
        wide[planes + 1] = high[at]

        def body(x, carry, wide=wide, own=own):
            wide[x + 1] = own[x]
            return carry

        lax.fori_loop(0, planes, body, 0)
    extend(q, low, high, field, deep)
    misfits = weigh(field, deep, nu_wide, obs_wide, scaled, scaled_deep, True)
    for chain in range(chains):

        def body(x, total, chain=chain):
            for cut, k in stencil_plane(scaled, scaled_deep, chain, x + 1):
                v = q[chain, x, :, cut]
                slope[chain, x, :, cut] = (inv_noise * unit) * k + prior_weight * v
                total = total + v * v
            return total

        squares = lax.fori_loop(0, planes, body, jnp.zeros_like(misfits[chain]))
        potential[chain] = fold(
            (0.5 * inv_noise) * misfits[chain] + (0.5 * prior_weight) * squares
        )


def add_kernel(a, b, out):
    def body(x, carry):
        out[x] = a[x] + b[x]
        return carry

    lax.fori_loop(0, a.shape[0], body, 0)


def mass_kernel(count, a, b, out):
    def body(x, carry):
        mean = (a[x, 0] + b[x, 0]) / count
        out[x] = 0.5 + (a[x, 1] + b[x, 1]) / count - mean * mean
        return carry

    lax.fori_loop(0, a.shape[0], body, 0)


def launch_kernel(q, draw, slope, mine, other, new_q, new_p, mass, kinetic, to_high, to_low):
    core = lax.rem(lax.axis_index("chain"), 2)
    chains, planes = q.shape[:2]
    half = planes // 2
    totals = [jnp.zeros((q.shape[2], LANES), jnp.float32)] * chains
    for part, base in ((mine, core * half), (other, (1 - core) * half)):

        def body(i, totals, part=part, base=base):
            x = base + i
            totals = list(totals)
            for cut in tiles(q.shape[-1]):
                im = part[i, :, cut]
                mass[x, :, cut] = im
                inverse_root = 1.0 / jnp.sqrt(im)
                for chain in range(chains):
                    p = draw[chain, x, :, cut] * inverse_root
                    totals[chain] = totals[chain] + im * p * p
                    p = p - (0.5 * step_size) * slope[chain, x, :, cut]
                    new_p[chain, x, :, cut] = p
                    new_q[chain, x, :, cut] = q[chain, x, :, cut] + step_size * im * p
            return tuple(totals)

        totals = lax.fori_loop(0, half, body, tuple(totals))
    for chain in range(chains):
        kinetic[chain] = fold(0.5 * totals[chain])
        for i in range(WIDE):
            to_high[chain * WIDE + i] = new_q[chain, planes - WIDE + i]
            to_low[chain * WIDE + i] = new_q[chain, i]


def leap_kernel(q, low, high, nu, obs, p, mass, new_q, new_p, to_high, to_low, field, deep, scaled, scaled_deep):
    chains, planes = q.shape[:2]
    extend(q, low, high, field, deep)
    weigh(field, deep, nu, obs, scaled, scaled_deep, False)
    for chain in range(chains):

        def body(x, carry, chain=chain):
            for cut, k in stencil_plane(scaled, scaled_deep, chain, x + 1):
                v = q[chain, x, :, cut]
                slope = (inv_noise * unit) * k + prior_weight * v
                moment = p[chain, x, :, cut] - step_size * slope
                new_p[chain, x, :, cut] = moment
                new_q[chain, x, :, cut] = v + step_size * mass[x, :, cut] * moment
            return carry

        lax.fori_loop(0, planes, body, 0)
        for i in range(WIDE):
            to_high[chain * WIDE + i] = new_q[chain, planes - WIDE + i]
            to_low[chain * WIDE + i] = new_q[chain, i]


def last_kernel(q, low, high, nu, obs, p, mass, potential, kinetic, new_p, rows, field, deep, scaled, scaled_deep):
    chains, planes = q.shape[:2]
    extend(q, low, high, field, deep)
    misfits = weigh(field, deep, nu, obs, scaled, scaled_deep, True)
    sub = lax.broadcasted_iota(jnp.int32, (8, LANES), 0)
    lane = lax.broadcasted_iota(jnp.int32, (8, LANES), 1)
    mark = jnp.zeros((8, LANES), jnp.float32)
    for chain in range(chains):

        def body(x, total, chain=chain):
            for cut, k in stencil_plane(scaled, scaled_deep, chain, x + 1):
                v = q[chain, x, :, cut]
                slope = (inv_noise * unit) * k + prior_weight * v
                moment = p[chain, x, :, cut] - (0.5 * step_size) * slope
                new_p[chain, x, :, cut] = moment
                total = total + (
                    (0.5 * prior_weight) * (v * v) + (0.5 * mass[x, :, cut]) * (moment * moment)
                )
            return total

        rest = lax.fori_loop(0, planes, body, jnp.zeros_like(misfits[chain]))
        end = fold((0.5 * inv_noise) * misfits[chain] + rest)
        start = potential[chain] + kinetic[chain]
        for row, tile in enumerate((start, end)):
            mark = jnp.where((sub == row) & (lane == chain), jnp.sum(tile), mark)
    for i in range(rows.shape[0]):
        rows[i] = mark


def local(position, momentum_draw, viscosity, observed):
    chains, planes, depth, across = position.shape
    groups, slabs = lax.axis_size("chain"), lax.axis_size("gx")
    cells = planes * slabs * depth * across
    near = [(i, i ^ 1) for i in range(groups)]
    far = [(i, i ^ 2) for i in range(groups)]
    forward = [(i, (i + 1) % slabs) for i in range(slabs)]
    backward = [(i, (i - 1) % slabs) for i in range(slabs)]
    half = planes // 2
    block, plane = (chains, planes, depth, across), (depth, across)
    rim = (chains * WIDE, *plane)
    wide = (planes + 2, *plane)
    field = (chains, planes + 2 * WIDE, *plane)
    scaled = (chains, *wide)
    scratch = [field, field, scaled, scaled]
    sums = (half, 2, *plane)
    tile = (chains, 8, LANES)
    cells_here = chains * planes * depth * across

    keep, send, to_high, to_low = call(
        start_kernel, [sums, sums, (chains * WIDE + 2, *plane), (chains * WIDE + 2, *plane)], [], "start", cells_here * 4
    )(position, viscosity, observed)
    part = call(add_kernel, [sums], [], "add", cells_here)(keep, lax.ppermute(send, "chain", near))[0]
    far_part = lax.ppermute(part, "chain", far)
    low = lax.ppermute(to_high, "gx", forward)
    high = lax.ppermute(to_low, "gx", backward)
    slope, nu, obs, potential = call(
        first_kernel, [block, wide, wide, tile], scratch, "first", cells_here * 60
    )(position, low, high, viscosity, observed)

    def mass_body(*refs):
        mass_kernel(chains * groups, *refs)

    mine = call(mass_body, [(half, *plane)], [], "mass", cells_here)(part, far_part)[0]
    other = lax.ppermute(mine, "chain", near)
    q, p, mass, kinetic, to_high, to_low = call(
        launch_kernel, [block, block, (planes, *plane), tile, rim, rim], [], "launch", cells_here * 8
    )(position, momentum_draw, slope, mine, other)
    for _ in range(LEAPS - 1):
        low = lax.ppermute(to_high, "gx", forward)
        high = lax.ppermute(to_low, "gx", backward)
        q, p, to_high, to_low = call(
            leap_kernel, [block, block, rim, rim], scratch, "leap", cells_here * 60
        )(q, low, high, nu, obs, p, mass)
    low = lax.ppermute(to_high, "gx", forward)
    high = lax.ppermute(to_low, "gx", backward)
    p, rows = call(
        last_kernel, [block, (slabs, 8, LANES)], scratch, "last", cells_here * 60
    )(q, low, high, nu, obs, p, mass, potential, kinetic)
    rows = lax.all_to_all(rows, "gx", 0, 0, tiled=True)
    energies = jnp.sum(rows[:, :2, :chains], axis=0) / cells
    return (q, p, energies)


def solution(mesh):
    in_specs = (
        P("chain", "gx", None, None),
        P("chain", "gx", None, None),
        P("gx", None, None),
        P("gx", None, None),
    )
    out_specs = (P("chain", "gx", None, None), P("chain", "gx", None, None), P(None, "chain"))
    return jax.shard_map(local, mesh=mesh, in_specs=in_specs, out_specs=out_specs, check_vma=False)
```

time: 222 us -> 91.9 us (0.41)
  blocking collectives: 83.3 us -> 16.2 us
  other arithmetic: 38.3 us -> 0.61 us
  Pallas kernels: 0 us -> 17.7 us
  waiting for transfers between devices: 45.7 us -> 28.9 us
  starting transfers between devices: 38.8 us -> 23 us
  between operations: 14.3 us -> 0.78 us
  local copies, waits for them, and re-layouts: 1.56 us -> 4.55 us
    psum x1 -> x0, blocking collectives: 83.3 us -> none  [local(): end_potential, end_kinetic = lax.psum((end_potential, end_kinetic), 'gx')]
    psum x1 -> x0, waiting for transfers between devices: 29.9 us -> none  [local(): first, second = lax.psum((local_first, local_second), 'chain')]
    reduce_sum x5 -> x1, other arithmetic: 22.1 us -> 0.04 us  [local(): energies = jnp.sum(rows[:, :2, :chains], axis=0) / cells]
    pallas_call x0 -> x7, Pallas kernels: none -> 17.7 us  [the longest x1 6.03 us: local(): call(leap_kernel, [block, block, rim, rim], scratch, 'leap', cells_here *...]
    all_to_all x0 -> x1, blocking collectives: none -> 16.2 us  [local(): rows = lax.all_to_all(rows, 'gx', 0, 0, tiled=True)]
    ppermute x12 -> x9, starting transfers between devices: 38.8 us -> 23 us  [the longest x3 17.2 us: local(): high = lax.ppermute(to_low, 'gx', backward)]
    ppermute x12 -> x9, waiting for transfers between devices: 15.8 us -> 28.9 us  [the longest x1 14.4 us: local(): far_part = lax.ppermute(part, 'chain', far)]
    mul x4 -> x0, other arithmetic: 6.15 us -> none  [the longest x3 4.68 us: gradient_narrow(): scaled = viscosity * misfit]
  transfers between devices with their start and end apart: 13 -> 9, of which waited for: 7 -> 4; matrix products, arithmetic and copies ran while one was open for 4% -> 0% of each run, Pallas kernels for 0% -> 5%
where the time goes in v2:
time: 91.9 us; the launch traced here: 91.6 us
  waiting for transfers between devices  28.9 us (31%)
  starting transfers between devices  23 us (25%)
  Pallas kernels  17.7 us (19%)
  blocking collectives  16.2 us (18%)
  local copies, waits for them, and re-layouts  4.55 us (5%)
    ppermute x3, starting transfers between devices, local(): high = lax.ppermute(to_low, 'gx', backward)  17.2 us
    all_to_all x1, blocking collectives, local(): rows = lax.all_to_all(rows, 'gx', 0, 0, tiled=True)  16.2 us
    ppermute x1, waiting for transfers between devices, local(): far_part = lax.ppermute(part, 'chain', far)  14.4 us
    ppermute x3, waiting for transfers between devices, local(): low = lax.ppermute(to_high, 'gx', forward)  12.5 us
    pallas_call x1, Pallas kernels, local(): call(leap_kernel, [block, block, rim, rim], scratch, 'leap', cells_here *...  6.03 us
    pallas_call x1, Pallas kernels, local(): call(last_kernel, [block, (slabs, 8, LANES)], scratch, 'last', cells_here...  5.92 us
    pallas_call x1, Pallas kernels, local(): call(first_kernel, [block, wide, wide, tile], scratch, 'first', cells_her...  4.87 us
    unnamed x16, local copies, waits for them, and re-layouts  4.55 us
  transfers between devices with their start and end apart: 9, of which 4 were waited for; matrix products, arithmetic and copies ran while one was open for 0% of the time, Pallas kernels for 5%

profile of v2, /device:TPU:0, one launch (start us, length us, event | category | flops | bytes accessed | tf_op | source)
XLA Modules:
  0.0 91.6 jit_solution(16156927482191296529)
XLA Ops:
  0.6 1.2 %copy-done = f32[2,8,16,1024]{3,2,1,0:T(8,128)S(1)} copy-done((f32[2,8,16,1024]{3,2,1,0:T(8,128)S(1)}, f32[2,8,16,1024]{3,2,1,0:T(8,128)}, u32[]{:S(2)}) %copy-start) | copy-done | bytes 1048600
  1.9 1.0 %copy-done.2 = f32[8,16,1024]{2,1,0:T(8,128)S(1)} copy-done((f32[8,16,1024]{2,1,0:T(8,128)S(1)}, f32[8,16,1024]{2,1,0:T(8,128)}, u32[]{:S(2)}) %copy-start.2) | copy-done | bytes 524312
  2.9 1.0 %copy-done.4 = f32[8,16,1024]{2,1,0:T(8,128)S(1)} copy-done((f32[8,16,1024]{2,1,0:T(8,128)S(1)}, f32[8,16,1024]{2,1,0:T(8,128)}, u32[]{:S(2)}) %copy-start.4) | copy-done | bytes 524312
  3.9 0.1 start.1
  4.1 0.1 collective-permute-start.2
  4.2 1.9 %collective-permute-done.2.b = f32[4,2,16,1024]{3,2,1,0:T(8,128)S(1)} collective-permute-done((f32[4,2,16,1024]{3,2,1,0:T(8,128)S(1)}, f32[4,2,16,1024]{3,2,1,0:T(8,128)S(1)}, u32[]{:S(2)}, u32[]{:S(2)}) %collective-permute-start.2) | collective-permute-done | bytes 524320 | tf_op jit(solution)/shard_map/ppermute | solution.py:304
  6.2 4.0 %collective-permute-start.3 = (f32[4,2,16,1024]{3,2,1,0:T(8,128)S(1)}, f32[4,2,16,1024]{3,2,1,0:T(8,128)S(1)}, u32[]{:S(2)}, u32[]{:S(2)}) collective-permute-start(f32[4,2,16,1024]{3,2,1,0:T(8,128)S(1)} %add.1.refs_0_), channel_id=1, source_target_pairs={{0,64},{32,96},{64,0},{96,32},{1,65},{33,97},{65,1},{97,33},{2,66}... | collective-permute-start | bytes 1572872 | tf_op jit(solution)/shard_map/ppermute | solution.py:305
  10.2 1.5 %collective-permute-start = (f32[6,16,1024]{2,1,0:T(8,128)S(1)}, f32[6,16,1024]{2,1,0:T(8,128)S(1)}, u32[]{:S(2)}, u32[]{:S(2)}) collective-permute-start(f32[6,16,1024]{2,1,0:T(8,128)S(1)} %get-tuple-element.23), channel_id=1, source_target_pairs={{0,1},{1,2},{2,3},{3,4},{4,5},{5,6},{6,7},{7,8},{8,9},{9,10},{10,1... | collective-permute-start | bytes 1179656 | tf_op jit(solution)/shard_map/ppermute | solution.py:306
  11.7 4.8 %collective-permute-start.1 = (f32[6,16,1024]{2,1,0:T(8,128)S(1)}, f32[6,16,1024]{2,1,0:T(8,128)S(1)}, u32[]{:S(2)}, u32[]{:S(2)}) collective-permute-start(f32[6,16,1024]{2,1,0:T(8,128)S(1)} %get-tuple-element.24), channel_id=1, source_target_pairs={{0,31},{1,0},{2,1},{3,2},{4,3},{5,4},{6,5},{7,6},{8,7},{9,8},{10,9... | collective-permute-start | bytes 1179656 | tf_op jit(solution)/shard_map/ppermute | solution.py:307
  16.5 14.4 %collective-permute-done.3.refs_1_ = f32[4,2,16,1024]{3,2,1,0:T(8,128)S(1)} collective-permute-done((f32[4,2,16,1024]{3,2,1,0:T(8,128)S(1)}, f32[4,2,16,1024]{3,2,1,0:T(8,128)S(1)}, u32[]{:S(2)}, u32[]{:S(2)}) %collective-permute-start.3) | collective-permute-done | bytes 524320 | tf_op jit(solution)/shard_map/ppermute | solution.py:305
  30.9 0.1 mass.1.mine
  31.0 0.1 collective-permute-start.4
  31.1 4.9 %first.1 = (f32[2,8,16,1024]{3,2,1,0:T(8,128)S(1)}, f32[10,16,1024]{2,1,0:T(8,128)S(1)}, f32[10,16,1024]{2,1,0:T(8,128)S(1)}, f32[2,8,128]{2,1,0:T(8,128)S(1)}) custom-call(f32[2,8,16,1024]{3,2,1,0:T(8,128)S(1)} %copy-done.1, f32[6,16,1024]{2,1,0:T(8,128)S(1)} %collective-permute-done.low, f32[6,16,1024]{2,1,0:T(8,128)S(1)} %collective-permute-done.1.high, ...), custom_call_target="tpu_custom_call" | custom-call | flops 15728640 | bytes 1966080 | tf_op jit(solution)/shard_map/first/pallas_call | solution.py:308
  36.0 0.6 launch.1
  36.6 0.1 collective-permute-start.5
  36.6 6.2 %collective-permute-start.6 = (f32[4,16,1024]{2,1,0:T(8,128)S(1)}, f32[4,16,1024]{2,1,0:T(8,128)S(1)}, u32[]{:S(2)}, u32[]{:S(2)}) collective-permute-start(f32[4,16,1024]{2,1,0:T(8,128)S(1)} %get-tuple-element.30), channel_id=1, source_target_pairs={{0,31},{1,0},{2,1},{3,2},{4,3},{5,4},{6,5},{7,6},{8,7},{9,8},{10,9... | collective-permute-start | bytes 786440 | tf_op jit(solution)/shard_map/ppermute | solution.py:322
  42.9 6.7 %collective-permute-done.5.low = f32[4,16,1024]{2,1,0:T(8,128)S(1)} collective-permute-done((f32[4,16,1024]{2,1,0:T(8,128)S(1)}, f32[4,16,1024]{2,1,0:T(8,128)S(1)}, u32[]{:S(2)}, u32[]{:S(2)}) %collective-permute-start.5) | collective-permute-done | bytes 262176 | tf_op jit(solution)/shard_map/ppermute | solution.py:321
  49.5 6.0 %leap.1 = (f32[2,8,16,1024]{3,2,1,0:T(8,128)}, f32[2,8,16,1024]{3,2,1,0:T(8,128)S(1)}, f32[4,16,1024]{2,1,0:T(8,128)S(1)}, f32[4,16,1024]{2,1,0:T(8,128)S(1)}) custom-call(f32[2,8,16,1024]{3,2,1,0:T(8,128)S(1)} %get-tuple-element.28.q, f32[4,16,1024]{2,1,0:T(8,128)S(1)} %collective-permute-done.5.low, f32[4,16,1024]{2,1,0:T(8,128)S(1)} %collective-permute-done.6.high, ...), custom_call_target="tpu_custom_call" | custom-call | flops 15728640 | bytes 1966080 | tf_op jit(solution)/shard_map/leap/pallas_call | solution.py:323
  55.6 6.2 %collective-permute-start.8 = (f32[4,16,1024]{2,1,0:T(8,128)S(1)}, f32[4,16,1024]{2,1,0:T(8,128)S(1)}, u32[]{:S(2)}, u32[]{:S(2)}) collective-permute-start(f32[4,16,1024]{2,1,0:T(8,128)S(1)} %get-tuple-element.37), channel_id=1, source_target_pairs={{0,31},{1,0},{2,1},{3,2},{4,3},{5,4},{6,5},{7,6},{8,7},{9,8},{10,9... | collective-permute-start | bytes 786440 | tf_op jit(solution)/shard_map/ppermute | solution.py:327
  61.8 5.9 %collective-permute-done.7.low = f32[4,16,1024]{2,1,0:T(8,128)S(1)} collective-permute-done((f32[4,16,1024]{2,1,0:T(8,128)S(1)}, f32[4,16,1024]{2,1,0:T(8,128)S(1)}, u32[]{:S(2)}, u32[]{:S(2)}) %collective-permute-start.7) | collective-permute-done | bytes 262176 | tf_op jit(solution)/shard_map/ppermute | solution.py:326
  67.7 1.2 %copy-done.7 = f32[2,8,16,1024]{3,2,1,0:T(8,128)S(1)} copy-done((f32[2,8,16,1024]{3,2,1,0:T(8,128)S(1)}, f32[2,8,16,1024]{3,2,1,0:T(8,128)}, u32[]{:S(2)}) %copy-start.7) | copy-done | bytes 1048600
  68.9 5.9 %last.1 = (f32[2,8,16,1024]{3,2,1,0:T(8,128)}, f32[32,8,128]{2,1,0:T(8,128)S(1)}) custom-call(f32[2,8,16,1024]{3,2,1,0:T(8,128)S(1)} %copy-done.7, f32[4,16,1024]{2,1,0:T(8,128)S(1)} %collective-permute-done.7.low, f32[4,16,1024]{2,1,0:T(8,128)S(1)} %collective-permute-done.8.high, f32[10,16,1024]{2,1,0:T(8,128)S(1)} %get-tuple-element.31.nu, ...), custom_call_target="tpu_custom_call" | custom-call | flops 15728640 | bytes 1966080 | tf_op jit(solution)/shard_map/last/pallas_call | solution.py:328
  74.9 16.2 %all_to_all.5 = f32[32,8,128]{2,1,0:T(8,128)S(1)} all-to-all(f32[32,8,128]{2,1,0:T(8,128)S(1)} %get-tuple-element.42), channel_id=1, replica_groups=mesh['chain'=4,'gx'=32] {'gx'}, dimensions={0} | all-to-all | bytes 262144 | tf_op jit(solution)/shard_map/all_to_all | solution.py:331
  91.1 0.6 broadcast_multiply_fusion
  (20 shorter events, 0.1 us)
Async XLA Ops:
  0.6 1.2 %copy-start = (f32[2,8,16,1024]{3,2,1,0:T(8,128)S(1)}, f32[2,8,16,1024]{3,2,1,0:T(8,128)}, u32[]{:S(2)}) copy-start(f32[2,8,16,1024]{3,2,1,0:T(8,128)} %q.5) | copy-start | bytes 3145732
  1.9 1.0 %copy-start.2 = (f32[8,16,1024]{2,1,0:T(8,128)S(1)}, f32[8,16,1024]{2,1,0:T(8,128)}, u32[]{:S(2)}) copy-start(f32[8,16,1024]{2,1,0:T(8,128)} %nu.3) | copy-start | bytes 1572868
  2.9 1.0 %copy-start.4 = (f32[8,16,1024]{2,1,0:T(8,128)S(1)}, f32[8,16,1024]{2,1,0:T(8,128)}, u32[]{:S(2)}) copy-start(f32[8,16,1024]{2,1,0:T(8,128)} %obs.3) | copy-start | bytes 1572868
  4.1 2.0 %collective-permute-start.2 = (f32[4,2,16,1024]{3,2,1,0:T(8,128)S(1)}, f32[4,2,16,1024]{3,2,1,0:T(8,128)S(1)}, u32[]{:S(2)}, u32[]{:S(2)}) collective-permute-start(f32[4,2,16,1024]{3,2,1,0:T(8,128)S(1)} %get-tuple-element.27), channel_id=1, source_target_pairs={{0,32},{32,0},{64,96},{96,64},{1,33},{33,1},{65,97},{97,65},{2,34}... | collective-permute-start | bytes 1572872 | tf_op jit(solution)/shard_map/ppermute | solution.py:304
  6.1 25.0 %copy-start.3 = (f32[8,16,1024]{2,1,0:T(8,128)S(1)}, f32[8,16,1024]{2,1,0:T(8,128)}, u32[]{:S(2)}) copy-start(f32[8,16,1024]{2,1,0:T(8,128)} %nu.3) | copy-start | bytes 1572868
  6.1 25.0 %copy-start.5 = (f32[8,16,1024]{2,1,0:T(8,128)S(1)}, f32[8,16,1024]{2,1,0:T(8,128)}, u32[]{:S(2)}) copy-start(f32[8,16,1024]{2,1,0:T(8,128)} %obs.3) | copy-start | bytes 1572868
  6.2 24.9 %copy-start.1 = (f32[2,8,16,1024]{3,2,1,0:T(8,128)S(1)}, f32[2,8,16,1024]{3,2,1,0:T(8,128)}, u32[]{:S(2)}) copy-start(f32[2,8,16,1024]{3,2,1,0:T(8,128)} %q.5) | copy-start | bytes 3145732
  6.2 24.7 %collective-permute-start.3 = (f32[4,2,16,1024]{3,2,1,0:T(8,128)S(1)}, f32[4,2,16,1024]{3,2,1,0:T(8,128)S(1)}, u32[]{:S(2)}, u32[]{:S(2)}) collective-permute-start(f32[4,2,16,1024]{3,2,1,0:T(8,128)S(1)} %add.1.refs_0_), channel_id=1, source_target_pairs={{0,64},{32,96},{64,0},{96,32},{1,65},{33,97},{65,1},{97,33},{2,66}... | collective-permute-start | bytes 1572872 | tf_op jit(solution)/shard_map/ppermute | solution.py:305
  10.2 20.8 %collective-permute-start = (f32[6,16,1024]{2,1,0:T(8,128)S(1)}, f32[6,16,1024]{2,1,0:T(8,128)S(1)}, u32[]{:S(2)}, u32[]{:S(2)}) collective-permute-start(f32[6,16,1024]{2,1,0:T(8,128)S(1)} %get-tuple-element.23), channel_id=1, source_target_pairs={{0,1},{1,2},{2,3},{3,4},{4,5},{5,6},{6,7},{7,8},{8,9},{9,10},{10,1... | collective-permute-start | bytes 1179656 | tf_op jit(solution)/shard_map/ppermute | solution.py:306
  11.7 19.4 %collective-permute-start.1 = (f32[6,16,1024]{2,1,0:T(8,128)S(1)}, f32[6,16,1024]{2,1,0:T(8,128)S(1)}, u32[]{:S(2)}, u32[]{:S(2)}) collective-permute-start(f32[6,16,1024]{2,1,0:T(8,128)S(1)} %get-tuple-element.24), channel_id=1, source_target_pairs={{0,31},{1,0},{2,1},{3,2},{4,3},{5,4},{6,5},{7,6},{8,7},{9,8},{10,9... | collective-permute-start | bytes 1179656 | tf_op jit(solution)/shard_map/ppermute | solution.py:307
  30.9 5.0 %copy-start.6 = (f32[2,8,16,1024]{3,2,1,0:T(8,128)S(1)}, f32[2,8,16,1024]{3,2,1,0:T(8,128)}, u32[]{:S(2)}) copy-start(f32[2,8,16,1024]{3,2,1,0:T(8,128)} %draw.1) | copy-start | bytes 3145732
  31.0 5.0 %collective-permute-start.4 = (f32[4,16,1024]{2,1,0:T(8,128)S(1)}, f32[4,16,1024]{2,1,0:T(8,128)S(1)}, u32[]{:S(2)}, u32[]{:S(2)}) collective-permute-start(f32[4,16,1024]{2,1,0:T(8,128)S(1)} %mass.1.mine), channel_id=1, source_target_pairs={{0,32},{32,0},{64,96},{96,64},{1,33},{33,1},{65,97},{97,65},{2,34}... | collective-permute-start | bytes 786440 | tf_op jit(solution)/shard_map/ppermute | solution.py:316
  36.6 13.0 %collective-permute-start.5 = (f32[4,16,1024]{2,1,0:T(8,128)S(1)}, f32[4,16,1024]{2,1,0:T(8,128)S(1)}, u32[]{:S(2)}, u32[]{:S(2)}) collective-permute-start(f32[4,16,1024]{2,1,0:T(8,128)S(1)} %get-tuple-element.29), channel_id=1, source_target_pairs={{0,1},{1,2},{2,3},{3,4},{4,5},{5,6},{6,7},{7,8},{8,9},{9,10},{10,1... | collective-permute-start | bytes 786440 | tf_op jit(solution)/shard_map/ppermute | solution.py:321
  36.6 12.9 %collective-permute-start.6 = (f32[4,16,1024]{2,1,0:T(8,128)S(1)}, f32[4,16,1024]{2,1,0:T(8,128)S(1)}, u32[]{:S(2)}, u32[]{:S(2)}) collective-permute-start(f32[4,16,1024]{2,1,0:T(8,128)S(1)} %get-tuple-element.30), channel_id=1, source_target_pairs={{0,31},{1,0},{2,1},{3,2},{4,3},{5,4},{6,5},{7,6},{8,7},{9,8},{10,9... | collective-permute-start | bytes 786440 | tf_op jit(solution)/shard_map/ppermute | solution.py:322
  55.6 12.1 %collective-permute-start.7 = (f32[4,16,1024]{2,1,0:T(8,128)S(1)}, f32[4,16,1024]{2,1,0:T(8,128)S(1)}, u32[]{:S(2)}, u32[]{:S(2)}) collective-permute-start(f32[4,16,1024]{2,1,0:T(8,128)S(1)} %get-tuple-element.36), channel_id=1, source_target_pairs={{0,1},{1,2},{2,3},{3,4},{4,5},{5,6},{6,7},{7,8},{8,9},{9,10},{10,1... | collective-permute-start | bytes 786440 | tf_op jit(solution)/shard_map/ppermute | solution.py:326
  55.6 12.1 %collective-permute-start.8 = (f32[4,16,1024]{2,1,0:T(8,128)S(1)}, f32[4,16,1024]{2,1,0:T(8,128)S(1)}, u32[]{:S(2)}, u32[]{:S(2)}) collective-permute-start(f32[4,16,1024]{2,1,0:T(8,128)S(1)} %get-tuple-element.37), channel_id=1, source_target_pairs={{0,31},{1,0},{2,1},{3,2},{4,3},{5,4},{6,5},{7,6},{8,7},{9,8},{10,9... | collective-permute-start | bytes 786440 | tf_op jit(solution)/shard_map/ppermute | solution.py:327
  67.7 1.2 %copy-start.7 = (f32[2,8,16,1024]{3,2,1,0:T(8,128)S(1)}, f32[2,8,16,1024]{3,2,1,0:T(8,128)}, u32[]{:S(2)}) copy-start(f32[2,8,16,1024]{3,2,1,0:T(8,128)} %get-tuple-element.20.q) | copy-start | bytes 3145732

commit v3 on v0

v3 whole, which is shorter than its diff:
```python
import jax
import jax.numpy as jnp
from jax import lax
from jax.experimental import pallas as pl
from jax.experimental.pallas import tpu as pltpu
from jax.sharding import PartitionSpec as P

LEAPS = 2

unit = -0.05
inv_noise = 0.25
prior_weight = 0.5
step_size = 0.05
LANES = 128
WIDE = 2


def call(kernel, out_shapes, scratch, name, work, ins=None):
    spec = pl.BlockSpec(memory_space=pltpu.VMEM)
    more = {} if ins is None else {"in_specs": ins}
    return pl.pallas_call(
        kernel,
        out_shape=[jax.ShapeDtypeStruct(shape, jnp.float32) for shape in out_shapes],
        out_specs=[spec] * len(out_shapes),
        scratch_shapes=[
            pltpu.VMEM(shape, jnp.float32) if isinstance(shape, tuple) else shape
            for shape in scratch
        ],
        compiler_params=pltpu.CompilerParams(vmem_limit_bytes=32 << 20),
        cost_estimate=pl.CostEstimate(flops=work, bytes_accessed=work // 8, transcendentals=0),
        name=name,
        **more,
    )


def tiles(width):
    return [slice(j * LANES, (j + 1) * LANES) for j in range(width // LANES)]


def depth_sum(v):
    depth = v.shape[0]
    row = lax.broadcasted_iota(jnp.int32, v.shape, 0)
    below = jnp.where(row == 0, 0.0, pltpu.roll(v, 1, 0))
    above = jnp.where(row == depth - 1, 0.0, pltpu.roll(v, depth - 1, 0))
    return below + above


def stencil(planes, deeps):
    cuts = tiles(planes[1].shape[-1])
    edge_terms, own_terms = [], []
    for cut in cuts:
        v = planes[1][:, cut]
        w = deeps[1][:, cut] + (planes[0][:, cut] + planes[2][:, cut])
        corner = deeps[0][:, cut] + deeps[2][:, cut]
        t = 6.0 * v + (2.0 * w + corner)
        d = t + w
        edge_terms.append(t)
        own_terms.append((d + d) - 92.0 * v)
    lane = lax.broadcasted_iota(jnp.int32, edge_terms[0].shape, 1)
    ups = [pltpu.roll(t, 1, 1) for t in edge_terms]
    downs = [pltpu.roll(t, LANES - 1, 1) for t in edge_terms]
    result = []
    for j in range(len(cuts)):
        before = ups[j - 1] if j else 0.0
        after = downs[j + 1] if j + 1 < len(cuts) else 0.0
        left = jnp.where(lane == 0, before, ups[j])
        right = jnp.where(lane == LANES - 1, after, downs[j])
        result.append(own_terms[j] + (left + right))
    return list(zip(cuts, result, strict=True))


def deepen(deep, source):
    for cut in tiles(source.shape[-1]):
        deep[:, cut] = depth_sum(source[:, cut])


def weigh(view, deep, nu, target, out, out_deep):
    total = 0.0
    for cut, k in stencil(view, deep):
        n = nu[:, cut]
        misfit = (unit * n) * k - target[:, cut]
        s = n * misfit
        out[:, cut] = s
        out_deep[:, cut] = depth_sum(s)
        total = total + misfit * misfit
    return total


def fold(total):
    return total[:8] + total[8:]


def interior(q, nu, obs, scaled, deep, scaled_deep, use):
    chains, planes = q.shape[:2]
    totals = []
    for chain in range(chains):
        for x in range(planes):
            deepen(deep.at[chain, x], q.at[chain, x])
    for chain in range(chains):
        total = 0.0
        for x in range(1, planes - 1):
            near = range(x - 1, x + 2)
            total = total + weigh(
                [q.at[chain, i] for i in near],
                [deep.at[chain, i] for i in near],
                nu.at[x],
                obs.at[x],
                scaled.at[chain, x - 1],
                scaled_deep.at[chain, x - 1],
            )
        totals.append(total)
    for chain in range(chains):
        for x in range(2, planes - 2):
            near = range(x - 2, x + 1)
            view = [scaled.at[chain, i] for i in near]
            for cut, k in stencil(view, [scaled_deep.at[chain, i] for i in near]):
                slope = (inv_noise * unit) * k + prior_weight * q[chain, x, :, cut]
                use(chain, x, cut, slope)
    return totals


def parity():
    return lax.rem(lax.axis_index("gx"), 2)


def place_halo(halo, from_a, from_b):
    odd = parity()
    chains = halo.shape[1]
    for chain in range(chains):
        for i in range(WIDE):
            halo[1 - odd, chain, i] = from_a[chain * WIDE + i]
            halo[odd, chain, i] = from_b[chain * WIDE + i]


def rims(q, halo, nu, obs, nu_halo, obs_halo, scaled, deep, rim_scaled, scaled_deep, use):
    chains, planes = q.shape[:2]

    def at(chain, x):
        if x < 0:
            return halo.at[0, chain, WIDE + x]
        if x >= planes:
            return halo.at[1, chain, x - planes]
        return q.at[chain, x]

    def scaled_at(chain, x):
        if x in (-1, 0):
            return rim_scaled.at[chain, x + 1]
        if x in (planes - 1, planes):
            return rim_scaled.at[chain, x - planes + 3]
        return scaled.at[chain, x - 1]

    sides = ((-2, -1, 0, 1), (planes + 1, planes, planes - 1, planes - 2))
    totals = []
    for chain in range(chains):
        for side in sides:
            for x in side:
                deepen(deep.at[chain, x + WIDE], at(chain, x))
    for chain in range(chains):
        total = 0.0
        for s, side in enumerate(sides):
            for x in side[1:3]:
                outer = x == side[1]
                near = range(x - 1, x + 2)
                squares = weigh(
                    [at(chain, i) for i in near],
                    [deep.at[chain, i + WIDE] for i in near],
                    nu_halo.at[s] if outer else nu.at[x],
                    obs_halo.at[s] if outer else obs.at[x],
                    scaled_at(chain, x),
                    scaled_deep.at[chain, x + 1],
                )
                total = total if outer else total + squares
            for x in (1, 2) if s == 0 else (planes - 2, planes - 3):
                deepen(scaled_deep.at[chain, x + 1], scaled_at(chain, x))
        totals.append(total)
    for chain in range(chains):
        for x in (0, 1, planes - 2, planes - 1):
            near = range(x - 1, x + 2)
            view = [scaled_at(chain, i) for i in near]
            for cut, k in stencil(view, [scaled_deep.at[chain, i + 1] for i in near]):
                slope = (inv_noise * unit) * k + prior_weight * q[chain, x, :, cut]
                use(chain, x, cut, slope)
    return totals


def fetch_kernel(q, nu, obs, to_a, to_b, sems):
    odd = parity()
    chains, planes = q.shape[:2]
    copies = []
    for out, low in ((to_a, odd), (to_b, 1 - odd)):
        start = (1 - low) * (planes - WIDE)
        edge = (1 - low) * (planes - 1)
        for chain in range(chains):
            copies.append((q.at[chain, pl.ds(start, WIDE)], out.at[pl.ds(chain * WIDE, WIDE)]))
        copies.append((nu.at[edge], out.at[chains * WIDE]))
        copies.append((obs.at[edge], out.at[chains * WIDE + 1]))
    started = [
        pltpu.make_async_copy(source, target, sems.at[i])
        for i, (source, target) in enumerate(copies)
    ]
    for copy in started:
        copy.start()
    for copy in started:
        copy.wait()


def sums_kernel(q, keep, send):
    core = lax.rem(lax.axis_index("chain"), 2)
    chains, planes = q.shape[:2]
    half = planes // 2
    for x in range(half):
        for out, base in ((keep, core * half), (send, (1 - core) * half)):
            for cut in tiles(q.shape[-1]):
                first = q[0, base + x, :, cut]
                second = first * first
                for chain in range(1, chains):
                    v = q[chain, base + x, :, cut]
                    first = first + v
                    second = second + v * v
                out[x, 0, :, cut] = first
                out[x, 1, :, cut] = second


def add_kernel(a, b, rim, inner):
    core = lax.rem(lax.axis_index("chain"), 2)
    count = rim.shape[0]
    for x in range(count):
        at = core * count + x
        rim[x] = a[at] + b[at]
        at = (1 - core) * count + x
        inner[x] = a[at] + b[at]


def mass_kernel(count, a, b, out):
    for x in range(a.shape[0]):
        mean = (a[x, 0] + b[x, 0]) / count
        out[x] = 0.5 + (a[x, 1] + b[x, 1]) / count - mean * mean


def first_inner_kernel(q, nu, obs, scaled, slope, potential, deep, scaled_deep):
    chains, planes = q.shape[:2]

    def use(chain, x, cut, value):
        slope[chain, x - 2, :, cut] = value

    misfits = interior(q, nu, obs, scaled, deep, scaled_deep, use)
    for chain in range(chains):
        squares = 0.0
        for x in range(planes):
            for cut in tiles(q.shape[-1]):
                v = q[chain, x, :, cut]
                squares = squares + v * v
        potential[chain] = fold(
            (0.5 * inv_noise) * misfits[chain] + (0.5 * prior_weight) * squares
        )


def first_rim_kernel(
    q, from_a, from_b, nu, obs, scaled, before,
    slope, nu_halo, obs_halo, potential, halo, deep, rim_scaled, scaled_deep,
):
    odd = parity()
    chains, planes = q.shape[:2]
    place_halo(halo, from_a, from_b)
    for out, at in ((nu_halo, chains * WIDE), (obs_halo, chains * WIDE + 1)):
        out[1 - odd] = from_a[at]
        out[odd] = from_b[at]

    def use(chain, x, cut, value):
        slope[chain, x if x < 2 else x - planes + 4, :, cut] = value

    misfits = rims(
        q, halo, nu, obs, nu_halo, obs_halo, scaled, deep, rim_scaled, scaled_deep, use
    )
    for chain in range(chains):
        potential[chain] = before[chain] + fold((0.5 * inv_noise) * misfits[chain])


def launch(q, draw, slope, mine, other, base, new_q, new_p, mass, totals, where_q):
    chains = q.shape[0]
    for part, (start, offset) in ((mine, base[0]), (other, base[1])):
        for i in range(part.shape[0]):
            for cut in tiles(q.shape[-1]):
                im = part[i, :, cut]
                mass[offset + i, :, cut] = im
                inverse_root = 1.0 / jnp.sqrt(im)
                for chain in range(chains):
                    p = draw[chain, start + i, :, cut] * inverse_root
                    totals[chain] = totals[chain] + im * p * p
                    p = p - (0.5 * step_size) * slope[chain, offset + i, :, cut]
                    new_p[chain, offset + i, :, cut] = p
                    new_q[chain, offset + i, :, cut] = (
                        q[chain, start + i, :, cut] + step_size * im * p
                    )


def send_rims(source, to_a, to_b):
    odd = parity()
    for chain in range(source.shape[0]):
        for i in range(WIDE):
            to_a[chain * WIDE + i] = source[chain, (1 - odd) * WIDE + i]
            to_b[chain * WIDE + i] = source[chain, odd * WIDE + i]


def launch_rim_kernel(q, draw, slope, mine, other, new_q, new_p, mass, kinetic, to_a, to_b):
    core = lax.rem(lax.axis_index("chain"), 2)
    chains, planes = q.shape[:2]
    far = planes - WIDE
    totals = [0.0] * chains
    base = ((core * far, core * WIDE), ((1 - core) * far, (1 - core) * WIDE))
    launch(q, draw, slope, mine, other, base, new_q, new_p, mass, totals, None)
    for chain in range(chains):
        kinetic[chain] = fold(0.5 * totals[chain])
    send_rims(new_q, to_a, to_b)


def launch_inner_kernel(
    q, draw, slope, mine, other, rim_q, before, new_q, new_p, mass, kinetic, own_q, own_p
):
    core = lax.rem(lax.axis_index("chain"), 2)
    chains, planes = q.shape[:2]
    half = planes // 2 - WIDE
    totals = [0.0] * chains
    base = tuple((WIDE + c * half, c * half) for c in (core, 1 - core))
    launch(q, draw, slope, mine, other, base, own_q, new_p, mass, totals, None)
    for chain in range(chains):
        kinetic[chain] = before[chain] + fold(0.5 * totals[chain])
    join(new_q, own_q, rim_q)


def join(whole, inner, rim):
    chains, planes = whole.shape[:2]
    for chain in range(chains):
        for x in range(planes):
            if x < WIDE:
                whole[chain, x] = rim[chain, x]
            elif x >= planes - WIDE:
                whole[chain, x] = rim[chain, x - planes + 2 * WIDE]
            else:
                whole[chain, x] = inner[chain, x - WIDE]


def leap_inner_kernel(q, nu, obs, p, mass, scaled, new_q, new_p, deep, scaled_deep):
    def use(chain, x, cut, slope):
        moment = p[chain, x - WIDE, :, cut] - step_size * slope
        new_p[chain, x - WIDE, :, cut] = moment
        new_q[chain, x - WIDE, :, cut] = (
            q[chain, x, :, cut] + step_size * mass[x - WIDE, :, cut] * moment
        )

    interior(q, nu, obs, scaled, deep, scaled_deep, use)


def leap_rim_kernel(
    q, from_a, from_b, nu, obs, nu_halo, obs_halo, p, mass, scaled, inner_q,
    new_q, new_p, to_a, to_b, halo, deep, rim_scaled, scaled_deep, rim_q,
):
    planes = q.shape[1]
    place_halo(halo, from_a, from_b)

    def use(chain, x, cut, slope):
        at = x if x < WIDE else x - planes + 2 * WIDE
        moment = p[chain, at, :, cut] - step_size * slope
        new_p[chain, at, :, cut] = moment
        rim_q[chain, at, :, cut] = q[chain, x, :, cut] + step_size * mass[at, :, cut] * moment

    rims(q, halo, nu, obs, nu_halo, obs_halo, scaled, deep, rim_scaled, scaled_deep, use)
    send_rims(rim_q, to_a, to_b)
    join(new_q, inner_q, rim_q)


def last_inner_kernel(q, nu, obs, p, mass, scaled, new_p, energy, deep, scaled_deep):
    chains, planes = q.shape[:2]
    totals = [0.0] * chains

    def use(chain, x, cut, slope):
        moment = p[chain, x - WIDE, :, cut] - (0.5 * step_size) * slope
        new_p[chain, x - WIDE, :, cut] = moment
        totals[chain] = totals[chain] + (0.5 * mass[x - WIDE, :, cut]) * (moment * moment)

    misfits = interior(q, nu, obs, scaled, deep, scaled_deep, use)
    for chain in range(chains):
        squares = 0.0
        for x in range(planes):
            for cut in tiles(q.shape[-1]):
                v = q[chain, x, :, cut]
                squares = squares + v * v
        energy[chain] = fold(
            (0.5 * inv_noise) * misfits[chain] + (0.5 * prior_weight) * squares + totals[chain]
        )


def last_rim_kernel(
    q, from_a, from_b, nu, obs, nu_halo, obs_halo, p, mass, scaled, inner_p, energy,
    potential, kinetic, new_p, rows, halo, deep, rim_scaled, scaled_deep, rim_p,
):
    chains, planes = q.shape[:2]
    totals = [0.0] * chains
    place_halo(halo, from_a, from_b)

    def use(chain, x, cut, slope):
        at = x if x < WIDE else x - planes + 2 * WIDE
        moment = p[chain, at, :, cut] - (0.5 * step_size) * slope
        rim_p[chain, at, :, cut] = moment
        totals[chain] = totals[chain] + (0.5 * mass[at, :, cut]) * (moment * moment)

    misfits = rims(
        q, halo, nu, obs, nu_halo, obs_halo, scaled, deep, rim_scaled, scaled_deep, use
    )
    join(new_p, inner_p, rim_p)
    sub = lax.broadcasted_iota(jnp.int32, (8, LANES), 0)
    lane = lax.broadcasted_iota(jnp.int32, (8, LANES), 1)
    mark = jnp.zeros((8, LANES), jnp.float32)
    for chain in range(chains):
        end = energy[chain] + fold((0.5 * inv_noise) * misfits[chain] + totals[chain])
        start = potential[chain] + kinetic[chain]
        for row, tile in enumerate((start, end)):
            mark = jnp.where((sub == row) & (lane == chain), jnp.sum(tile), mark)
    for i in range(rows.shape[0]):
        rows[i] = mark


def local(position, momentum_draw, viscosity, observed):
    chains, planes, depth, across = position.shape
    groups, slabs = lax.axis_size("chain"), lax.axis_size("gx")
    cells = planes * slabs * depth * across
    near = [(i, i ^ 1) for i in range(groups)]
    far = [(i, i ^ 2) for i in range(groups)]
    pair_a = [(i, i ^ 1) for i in range(slabs)]
    pair_b = [(i, (i + 1 if i % 2 else i - 1) % slabs) for i in range(slabs)]
    half = planes // 2
    plane = (depth, across)
    rest = planes - 2 * WIDE
    block = (chains, planes, *plane)
    rim_block = (chains, 2 * WIDE, *plane)
    inner_block = (chains, rest, *plane)
    halo = (2, chains, WIDE, *plane)
    edge = (chains * WIDE, *plane)
    sides = (2, *plane)
    tile = (chains, 8, LANES)
    scaled_shape = (chains, planes - 2, *plane)
    field = (chains, planes + 2 * WIDE, *plane)
    inner_scratch = [block, scaled_shape]
    rim_scratch = [halo, field, rim_block, (chains, planes + 2, *plane)]
    work = chains * planes * depth * across * 30

    def swap(to_a, to_b):
        return lax.ppermute(to_a, "gx", pair_a), lax.ppermute(to_b, "gx", pair_b)

    memory = pl.BlockSpec(memory_space=pl.ANY)
    first_edge = (chains * WIDE + 2, *plane)
    to_a, to_b = call(
        fetch_kernel, [first_edge, first_edge], [pltpu.SemaphoreType.DMA((2 * (chains + 2),))],
        "fetch", work // 16, [memory] * 3,
    )(position, viscosity, observed)
    from_a, from_b = swap(to_a, to_b)
    sums = (half, 2, *plane)
    keep, send = call(sums_kernel, [sums, sums], [], "sums", work // 16)(position)
    got = lax.ppermute(send, "chain", near)
    part, inner_part = call(
        add_kernel, [(WIDE, 2, *plane), (half - WIDE, 2, *plane)], [], "add", work // 16
    )(keep, got)
    far_part = lax.ppermute(part, "chain", far)
    far_inner = lax.ppermute(inner_part, "chain", far)
    scaled, inner_slope, potential = call(
        first_inner_kernel, [scaled_shape, inner_block, tile], inner_scratch, "first_inner", work
    )(position, viscosity, observed)
    slope, nu_halo, obs_halo, potential = call(
        first_rim_kernel, [rim_block, sides, sides, tile], rim_scratch, "first_rim", work
    )(position, from_a, from_b, viscosity, observed, scaled, potential)

    def mass_body(*refs):
        mass_kernel(chains * groups, *refs)

    def mass_of(own, remote, name):
        shape = (own.shape[0], *plane)
        mine = call(mass_body, [shape], [], name, work // 16)(own, remote)[0]
        return mine, lax.ppermute(mine, "chain", near)

    mine, other = mass_of(part, far_part, "mass_rim")
    rim_q, rim_p, rim_mass, kinetic, to_a, to_b = call(
        launch_rim_kernel,
        [rim_block, rim_block, (2 * WIDE, *plane), tile, edge, edge],
        [], "launch_rim", work // 4,
    )(position, momentum_draw, slope, mine, other)
    from_a, from_b = swap(to_a, to_b)
    mine, other = mass_of(inner_part, far_inner, "mass_inner")
    q, inner_p, inner_mass, kinetic = call(
        launch_inner_kernel,
        [block, inner_block, (rest, *plane), tile],
        [inner_block, inner_block], "launch_inner", work // 4,
    )(position, momentum_draw, inner_slope, mine, other, rim_q, kinetic)
    for _ in range(LEAPS - 1):
        scaled, inner_q, inner_p = call(
            leap_inner_kernel, [scaled_shape, inner_block, inner_block], inner_scratch, "leap_inner", work
        )(q, viscosity, observed, inner_p, inner_mass)
        q, rim_p, to_a, to_b = call(
            leap_rim_kernel, [block, rim_block, edge, edge], [*rim_scratch, rim_block], "leap_rim", work
        )(q, from_a, from_b, viscosity, observed, nu_halo, obs_halo, rim_p, rim_mass, scaled, inner_q)
        from_a, from_b = swap(to_a, to_b)
    scaled, inner_p, energy = call(
        last_inner_kernel, [scaled_shape, inner_block, tile], inner_scratch, "last_inner", work
    )(q, viscosity, observed, inner_p, inner_mass)
    p, rows = call(
        last_rim_kernel, [block, (slabs, 8, LANES)], [*rim_scratch, rim_block], "last_rim", work
    )(
        q, from_a, from_b, viscosity, observed, nu_halo, obs_halo, rim_p, rim_mass,
        scaled, inner_p, energy, potential, kinetic,
    )
    rows = lax.all_to_all(rows, "gx", 0, 0, tiled=True)
    energies = jnp.sum(rows[:, :2, :chains], axis=0) / cells
    return (q, p, energies)


def solution(mesh):
    in_specs = (
        P("chain", "gx", None, None),
        P("chain", "gx", None, None),
        P("gx", None, None),
        P("gx", None, None),
    )
    out_specs = (P("chain", "gx", None, None), P("chain", "gx", None, None), P(None, "chain"))
    return jax.shard_map(local, mesh=mesh, in_specs=in_specs, out_specs=out_specs, check_vma=False)
```

time: 222 us -> 75.3 us (0.34)
  blocking collectives: 83.3 us -> 13.9 us
  other arithmetic: 38.3 us -> 0.61 us
  waiting for transfers between devices: 45.7 us -> 25.1 us
  starting transfers between devices: 38.8 us -> 19.3 us
  between operations: 14.3 us -> 0.78 us
  Pallas kernels: 0 us -> 11.7 us
    psum x1 -> x0, blocking collectives: 83.3 us -> none  [local(): end_potential, end_kinetic = lax.psum((end_potential, end_kinetic), 'gx')]
    psum x1 -> x0, waiting for transfers between devices: 29.9 us -> none  [local(): first, second = lax.psum((local_first, local_second), 'chain')]
    reduce_sum x5 -> x1, other arithmetic: 22.1 us -> 0.04 us  [local(): energies = jnp.sum(rows[:, :2, :chains], axis=0) / cells]
    ppermute x12 -> x11, starting transfers between devices: 38.8 us -> 19.3 us  [the longest x6 15.1 us: swap(): return (lax.ppermute(to_a, 'gx', pair_a), lax.ppermute(to_b, 'gx', pair_b))]
    all_to_all x0 -> x1, blocking collectives: none -> 13.9 us  [local(): rows = lax.all_to_all(rows, 'gx', 0, 0, tiled=True)]
    pallas_call x0 -> x13, Pallas kernels: none -> 11.7 us  [the longest x1 2.29 us: local(): call(leap_rim_kernel, [block, rim_block, edge, edge], [*rim_scratch, rim_...]
    ppermute x12 -> x11, waiting for transfers between devices: 15.8 us -> 25.1 us  [the longest x1 12.2 us: local(): far_part = lax.ppermute(part, 'chain', far)]
    mul x4 -> x0, other arithmetic: 6.15 us -> none  [the longest x3 4.68 us: gradient_narrow(): scaled = viscosity * misfit]
  transfers between devices with their start and end apart: 13 -> 11, of which waited for: 7 -> 6; matrix products, arithmetic and copies ran while one was open for 4% -> 0% of each run, Pallas kernels for 0% -> 9%
where the time goes in v3:
time: 75.3 us; the launch traced here: 75 us
  waiting for transfers between devices  25.1 us (33%)
  starting transfers between devices  19.3 us (26%)
  blocking collectives  13.9 us (18%)
  Pallas kernels  11.7 us (16%)
  local copies, waits for them, and re-layouts  3.52 us (5%)
  between operations  0.78 us (1%)
    ppermute x6, starting transfers between devices, swap(): return (lax.ppermute(to_a, 'gx', pair_a), lax.ppermute(to_b, 'gx', pair_b))  15.1 us
    all_to_all x1, blocking collectives, local(): rows = lax.all_to_all(rows, 'gx', 0, 0, tiled=True)  13.9 us
    ppermute x1, waiting for transfers between devices, local(): far_part = lax.ppermute(part, 'chain', far)  12.2 us
    ppermute x6, waiting for transfers between devices, swap(): return (lax.ppermute(to_a, 'gx', pair_a), lax.ppermute(to_b, 'gx', pair_b))  11.8 us
    ppermute x1, starting transfers between devices, local(): far_part = lax.ppermute(part, 'chain', far)  3.66 us
    unnamed x12, local copies, waits for them, and re-layouts  3.52 us
    pallas_call x1, Pallas kernels, local(): call(leap_rim_kernel, [block, rim_block, edge, edge], [*rim_scratch, rim_...  2.29 us
    pallas_call x1, Pallas kernels, local(): call(last_rim_kernel, [block, (slabs, 8, LANES)], [*rim_scratch, rim_bloc...  2.22 us
  transfers between devices with their start and end apart: 11, of which 6 were waited for; matrix products, arithmetic and copies ran while one was open for 0% of the time, Pallas kernels for 9%

profile of v3, /device:TPU:0, one launch (start us, length us, event | category | flops | bytes accessed | tf_op | source)
XLA Modules:
  0.0 75.0 jit_solution(8599464406007596502)
XLA Ops:
  0.6 1.2 %copy-done = f32[2,8,16,1024]{3,2,1,0:T(8,128)S(1)} copy-done((f32[2,8,16,1024]{3,2,1,0:T(8,128)S(1)}, f32[2,8,16,1024]{3,2,1,0:T(8,128)}, u32[]{:S(2)}) %copy-start) | copy-done | bytes 1048600
  2.0 0.9 %copy-done.2 = f32[8,16,1024]{2,1,0:T(8,128)S(1)} copy-done((f32[8,16,1024]{2,1,0:T(8,128)S(1)}, f32[8,16,1024]{2,1,0:T(8,128)}, u32[]{:S(2)}) %copy-start.2) | copy-done | bytes 524312
  3.1 1.1 %fetch.1 = (f32[6,16,1024]{2,1,0:T(8,128)S(1)}, f32[6,16,1024]{2,1,0:T(8,128)S(1)}) custom-call(f32[2,8,16,1024]{3,2,1,0:T(8,128)S(1)} %copy-done, f32[8,16,1024]{2,1,0:T(8,128)S(1)} %copy-done.2, f32[8,16,1024]{2,1,0:T(8,128)S(1)} %copy-done.3), custom_call_target="tpu_custom_call" | custom-call | flops 491520 | bytes 61440 | tf_op jit(solution)/shard_map/fetch/pallas_call | solution.py:452
  4.1 1.7 %collective-permute-start.3 = (f32[6,16,1024]{2,1,0:T(8,128)S(1)}, f32[6,16,1024]{2,1,0:T(8,128)S(1)}, u32[]{:S(2)}, u32[]{:S(2)}) collective-permute-start(f32[6,16,1024]{2,1,0:T(8,128)S(1)} %get-tuple-element.42), channel_id=1, source_target_pairs={{0,1},{1,0},{2,3},{3,2},{4,5},{5,4},{6,7},{7,6},{8,9},{9,8},{10,11... | collective-permute-start | bytes 1179656 | tf_op jit(solution)/shard_map/ppermute | solution.py:448
  5.8 5.9 %collective-permute-start.4 = (f32[6,16,1024]{2,1,0:T(8,128)S(1)}, f32[6,16,1024]{2,1,0:T(8,128)S(1)}, u32[]{:S(2)}, u32[]{:S(2)}) collective-permute-start(f32[6,16,1024]{2,1,0:T(8,128)S(1)} %get-tuple-element.43), channel_id=1, source_target_pairs={{0,31},{1,2},{2,1},{3,4},{4,3},{5,6},{6,5},{7,8},{8,7},{9,10},{10,... | collective-permute-start | bytes 1179656 | tf_op jit(solution)/shard_map/ppermute | solution.py:448
  11.8 3.7 %collective-permute-start.5 = (f32[2,2,16,1024]{3,2,1,0:T(8,128)S(1)}, f32[2,2,16,1024]{3,2,1,0:T(8,128)S(1)}, u32[]{:S(2)}, u32[]{:S(2)}) collective-permute-start(f32[2,2,16,1024]{3,2,1,0:T(8,128)S(1)} %get-tuple-element.47.refs_0_), channel_id=1, source_target_pairs={{0,64},{32,96},{64,0},{96,32},{1,65},{33,97},{65,1},{97,33},{2,66}... | collective-permute-start | bytes 786440 | tf_op jit(solution)/shard_map/ppermute | solution.py:463
  15.5 12.2 %collective-permute-done.5.refs_1_ = f32[2,2,16,1024]{3,2,1,0:T(8,128)S(1)} collective-permute-done((f32[2,2,16,1024]{3,2,1,0:T(8,128)S(1)}, f32[2,2,16,1024]{3,2,1,0:T(8,128)S(1)}, u32[]{:S(2)}, u32[]{:S(2)}) %collective-permute-start.5) | collective-permute-done | bytes 262176 | tf_op jit(solution)/shard_map/ppermute | solution.py:463
  27.8 1.4 %first_inner.1 = (f32[2,6,16,1024]{3,2,1,0:T(8,128)S(1)}, f32[2,4,16,1024]{3,2,1,0:T(8,128)S(1)}, f32[2,8,128]{2,1,0:T(8,128)S(1)}) custom-call(f32[2,8,16,1024]{3,2,1,0:T(8,128)S(1)} %copy-done.1, f32[8,16,1024]{2,1,0:T(8,128)S(1)} %copy-done.2, f32[8,16,1024]{2,1,0:T(8,128)S(1)} %copy-done.3), custom_call_target="tpu_custom_call" | custom-call | flops 7864320 | bytes 983040 | tf_op jit(solution)/shard_map/first_inner/pallas_call | solution.py:465
  29.2 1.1 %first_rim.1 = (f32[2,4,16,1024]{3,2,1,0:T(8,128)S(1)}, f32[2,16,1024]{2,1,0:T(8,128)S(1)}, f32[2,16,1024]{2,1,0:T(8,128)S(1)}, f32[2,8,128]{2,1,0:T(8,128)S(1)}) custom-call(f32[2,8,16,1024]{3,2,1,0:T(8,128)S(1)} %copy-done.1, f32[6,16,1024]{2,1,0:T(8,128)S(1)} %collective-permute-done.3.from_a, f32[6,16,1024]{2,1,0:T(8,128)S(1)} %collective-permute-done.4.from_b, ...), custom_call_target="tpu_custom_call" | custom-call | flops 7864320 | bytes 983040 | tf_op jit(solution)/shard_map/first_rim/pallas_call | solution.py:468
  30.8 3.8 %collective-permute-start.8 = (f32[4,16,1024]{2,1,0:T(8,128)S(1)}, f32[4,16,1024]{2,1,0:T(8,128)S(1)}, u32[]{:S(2)}, u32[]{:S(2)}) collective-permute-start(f32[4,16,1024]{2,1,0:T(8,128)S(1)} %get-tuple-element.52), channel_id=1, source_target_pairs={{0,31},{1,2},{2,1},{3,4},{4,3},{5,6},{6,5},{7,8},{8,7},{9,10},{10,... | collective-permute-start | bytes 786440 | tf_op jit(solution)/shard_map/ppermute | solution.py:448
  34.9 1.1 %collective-permute-done.2.other = f32[2,16,1024]{2,1,0:T(8,128)S(1)} collective-permute-done((f32[2,16,1024]{2,1,0:T(8,128)S(1)}, f32[2,16,1024]{2,1,0:T(8,128)S(1)}, u32[]{:S(2)}, u32[]{:S(2)}) %collective-permute-start.2) | collective-permute-done | bytes 131104 | tf_op jit(solution)/shard_map/ppermute | solution.py:478
  36.1 0.3 launch_inner.1
  36.4 1.4 %leap_inner.1 = (f32[2,6,16,1024]{3,2,1,0:T(8,128)S(1)}, f32[2,4,16,1024]{3,2,1,0:T(8,128)S(1)}, f32[2,4,16,1024]{3,2,1,0:T(8,128)S(1)}) custom-call(f32[2,8,16,1024]{3,2,1,0:T(8,128)S(1)} %get-tuple-element.50.q, f32[8,16,1024]{2,1,0:T(8,128)S(1)} %copy-done.2, f32[8,16,1024]{2,1,0:T(8,128)S(1)} %copy-done.3, f32[2,4,16,1024]{3,2,1,0:T(8,128)S(1)} %get-tuple-element.57.p, ...), custom_call_target="tpu_custom_call" | custom-call | flops 7864320 | bytes 983040 | tf_op jit(solution)/shard_map/leap_inner/pallas_call | solution.py:494
  37.7 1.8 %collective-permute-done.7.from_a = f32[4,16,1024]{2,1,0:T(8,128)S(1)} collective-permute-done((f32[4,16,1024]{2,1,0:T(8,128)S(1)}, f32[4,16,1024]{2,1,0:T(8,128)S(1)}, u32[]{:S(2)}, u32[]{:S(2)}) %collective-permute-start.7) | collective-permute-done | bytes 262176 | tf_op jit(solution)/shard_map/ppermute | solution.py:448
  39.5 4.3 %collective-permute-done.8.from_b = f32[4,16,1024]{2,1,0:T(8,128)S(1)} collective-permute-done((f32[4,16,1024]{2,1,0:T(8,128)S(1)}, f32[4,16,1024]{2,1,0:T(8,128)S(1)}, u32[]{:S(2)}, u32[]{:S(2)}) %collective-permute-start.8) | collective-permute-done | bytes 262176 | tf_op jit(solution)/shard_map/ppermute | solution.py:448
  43.8 2.3 %leap_rim.1 = (f32[2,8,16,1024]{3,2,1,0:T(8,128)}, f32[2,4,16,1024]{3,2,1,0:T(8,128)S(1)}, f32[4,16,1024]{2,1,0:T(8,128)S(1)}, f32[4,16,1024]{2,1,0:T(8,128)S(1)}) custom-call(f32[2,8,16,1024]{3,2,1,0:T(8,128)S(1)} %get-tuple-element.50.q, f32[4,16,1024]{2,1,0:T(8,128)S(1)} %collective-permute-done.7.from_a, ...), custom_call_target="tpu_custom_call" | custom-call | flops 7864320 | bytes 983040 | tf_op jit(solution)/shard_map/leap_rim/pallas_call | solution.py:497
  46.1 3.7 %collective-permute-start.10 = (f32[4,16,1024]{2,1,0:T(8,128)S(1)}, f32[4,16,1024]{2,1,0:T(8,128)S(1)}, u32[]{:S(2)}, u32[]{:S(2)}) collective-permute-start(f32[4,16,1024]{2,1,0:T(8,128)S(1)} %get-tuple-element.63), channel_id=1, source_target_pairs={{0,31},{1,2},{2,1},{3,4},{4,3},{5,6},{6,5},{7,8},{8,7},{9,10},{10,... | collective-permute-start | bytes 786440 | tf_op jit(solution)/shard_map/ppermute | solution.py:448
  49.8 1.2 %copy-done.4 = f32[2,8,16,1024]{3,2,1,0:T(8,128)S(1)} copy-done((f32[2,8,16,1024]{3,2,1,0:T(8,128)S(1)}, f32[2,8,16,1024]{3,2,1,0:T(8,128)}, u32[]{:S(2)}) %copy-start.4) | copy-done | bytes 1048600
  51.1 1.5 %last_inner.1 = (f32[2,6,16,1024]{3,2,1,0:T(8,128)S(1)}, f32[2,4,16,1024]{3,2,1,0:T(8,128)S(1)}, f32[2,8,128]{2,1,0:T(8,128)S(1)}) custom-call(f32[2,8,16,1024]{3,2,1,0:T(8,128)S(1)} %copy-done.4, f32[8,16,1024]{2,1,0:T(8,128)S(1)} %copy-done.2, f32[8,16,1024]{2,1,0:T(8,128)S(1)} %copy-done.3, f32[2,4,16,1024]{3,2,1,0:T(8,128)S(1)} %get-tuple-element.65.p, ...), custom_call_target="tpu_custom_call" | custom-call | flops 7864320 | bytes 983040 | tf_op jit(solution)/shard_map/last_inner/pallas_call | solution.py:501
  52.5 1.5 %collective-permute-done.9.from_a = f32[4,16,1024]{2,1,0:T(8,128)S(1)} collective-permute-done((f32[4,16,1024]{2,1,0:T(8,128)S(1)}, f32[4,16,1024]{2,1,0:T(8,128)S(1)}, u32[]{:S(2)}, u32[]{:S(2)}) %collective-permute-start.9) | collective-permute-done | bytes 262176 | tf_op jit(solution)/shard_map/ppermute | solution.py:448
  54.0 4.2 %collective-permute-done.10.from_b = f32[4,16,1024]{2,1,0:T(8,128)S(1)} collective-permute-done((f32[4,16,1024]{2,1,0:T(8,128)S(1)}, f32[4,16,1024]{2,1,0:T(8,128)S(1)}, u32[]{:S(2)}, u32[]{:S(2)}) %collective-permute-start.10) | collective-permute-done | bytes 262176 | tf_op jit(solution)/shard_map/ppermute | solution.py:448
  58.3 2.2 %last_rim.1 = (f32[2,8,16,1024]{3,2,1,0:T(8,128)}, f32[32,8,128]{2,1,0:T(8,128)S(1)}) custom-call(f32[2,8,16,1024]{3,2,1,0:T(8,128)S(1)} %copy-done.4, f32[4,16,1024]{2,1,0:T(8,128)S(1)} %collective-permute-done.9.from_a, f32[4,16,1024]{2,1,0:T(8,128)S(1)} %collective-permute-done.10.from_b, f32[8,16,1024]{2,1,0:T(8,128)S(1)} %copy-done.2, ...), custom_call_target="tpu_custom_call" | custom-call | flops 7864320 | bytes 983040 | tf_op jit(solution)/shard_map/last_rim/pallas_call | solution.py:504
  60.5 13.9 %all_to_all.5 = f32[32,8,128]{2,1,0:T(8,128)S(1)} all-to-all(f32[32,8,128]{2,1,0:T(8,128)S(1)} %get-tuple-element.72), channel_id=1, replica_groups=mesh['chain'=4,'gx'=32] {'gx'}, dimensions={0} | all-to-all | bytes 262144 | tf_op jit(solution)/shard_map/all_to_all | solution.py:510
  74.4 0.6 broadcast_multiply_fusion
  (26 shorter events, 1.4 us)
Async XLA Ops:
  0.6 1.2 %copy-start = (f32[2,8,16,1024]{3,2,1,0:T(8,128)S(1)}, f32[2,8,16,1024]{3,2,1,0:T(8,128)}, u32[]{:S(2)}) copy-start(f32[2,8,16,1024]{3,2,1,0:T(8,128)} %q.11) | copy-start | bytes 3145732
  1.9 1.0 %copy-start.2 = (f32[8,16,1024]{2,1,0:T(8,128)S(1)}, f32[8,16,1024]{2,1,0:T(8,128)}, u32[]{:S(2)}) copy-start(f32[8,16,1024]{2,1,0:T(8,128)} %nu.13) | copy-start | bytes 1572868
  1.9 1.2 %copy-start.3 = (f32[8,16,1024]{2,1,0:T(8,128)S(1)}, f32[8,16,1024]{2,1,0:T(8,128)}, u32[]{:S(2)}) copy-start(f32[8,16,1024]{2,1,0:T(8,128)} %obs.13) | copy-start | bytes 1572868
  1.9 9.8 %collective-permute-start = (f32[4,2,16,1024]{3,2,1,0:T(8,128)S(1)}, f32[4,2,16,1024]{3,2,1,0:T(8,128)S(1)}, u32[]{:S(2)}, u32[]{:S(2)}) collective-permute-start(f32[4,2,16,1024]{3,2,1,0:T(8,128)S(1)} %get-tuple-element.40), channel_id=1, source_target_pairs={{0,32},{32,0},{64,96},{96,64},{1,33},{33,1},{65,97},{97,65},{2,34}... | collective-permute-start | bytes 1572872 | tf_op jit(solution)/shard_map/ppermute | solution.py:459
  4.1 23.7 %copy-start.1 = (f32[2,8,16,1024]{3,2,1,0:T(8,128)S(1)}, f32[2,8,16,1024]{3,2,1,0:T(8,128)}, u32[]{:S(2)}) copy-start(f32[2,8,16,1024]{3,2,1,0:T(8,128)} %q.11) | copy-start | bytes 3145732
  4.1 25.1 %collective-permute-start.3 = (f32[6,16,1024]{2,1,0:T(8,128)S(1)}, f32[6,16,1024]{2,1,0:T(8,128)S(1)}, u32[]{:S(2)}, u32[]{:S(2)}) collective-permute-start(f32[6,16,1024]{2,1,0:T(8,128)S(1)} %get-tuple-element.42), channel_id=1, source_target_pairs={{0,1},{1,0},{2,3},{3,2},{4,5},{5,4},{6,7},{7,6},{8,9},{9,8},{10,11... | collective-permute-start | bytes 1179656 | tf_op jit(solution)/shard_map/ppermute | solution.py:448
  5.8 23.4 %collective-permute-start.4 = (f32[6,16,1024]{2,1,0:T(8,128)S(1)}, f32[6,16,1024]{2,1,0:T(8,128)S(1)}, u32[]{:S(2)}, u32[]{:S(2)}) collective-permute-start(f32[6,16,1024]{2,1,0:T(8,128)S(1)} %get-tuple-element.43), channel_id=1, source_target_pairs={{0,31},{1,2},{2,1},{3,4},{4,3},{5,6},{6,5},{7,8},{8,7},{9,10},{10,... | collective-permute-start | bytes 1179656 | tf_op jit(solution)/shard_map/ppermute | solution.py:448
  11.8 15.9 %collective-permute-start.5 = (f32[2,2,16,1024]{3,2,1,0:T(8,128)S(1)}, f32[2,2,16,1024]{3,2,1,0:T(8,128)S(1)}, u32[]{:S(2)}, u32[]{:S(2)}) collective-permute-start(f32[2,2,16,1024]{3,2,1,0:T(8,128)S(1)} %get-tuple-element.47.refs_0_), channel_id=1, source_target_pairs={{0,64},{32,96},{64,0},{96,32},{1,65},{33,97},{65,1},{97,33},{2,66}... | collective-permute-start | bytes 786440 | tf_op jit(solution)/shard_map/ppermute | solution.py:463
  15.4 19.2 %collective-permute-start.1 = (f32[2,2,16,1024]{3,2,1,0:T(8,128)S(1)}, f32[2,2,16,1024]{3,2,1,0:T(8,128)S(1)}, u32[]{:S(2)}, u32[]{:S(2)}) collective-permute-start(f32[2,2,16,1024]{3,2,1,0:T(8,128)S(1)} %get-tuple-element.41.refs_0_), channel_id=1, source_target_pairs={{0,64},{32,96},{64,0},{96,32},{1,65},{33,97},{65,1},{97,33},{2,66}... | collective-permute-start | bytes 786440 | tf_op jit(solution)/shard_map/ppermute | solution.py:464
  27.7 2.7 %collective-permute-start.6 = (f32[2,16,1024]{2,1,0:T(8,128)S(1)}, f32[2,16,1024]{2,1,0:T(8,128)S(1)}, u32[]{:S(2)}, u32[]{:S(2)}) collective-permute-start(f32[2,16,1024]{2,1,0:T(8,128)S(1)} %mass_rim.1.mine), channel_id=1, source_target_pairs={{0,32},{32,0},{64,96},{96,64},{1,33},{33,1},{65,97},{97,65},{2,34}... | collective-permute-start | bytes 393224 | tf_op jit(solution)/shard_map/ppermute | solution.py:478
  29.2 1.2 %copy-start.5 = (f32[2,8,16,1024]{3,2,1,0:T(8,128)S(1)}, f32[2,8,16,1024]{3,2,1,0:T(8,128)}, u32[]{:S(2)}) copy-start(f32[2,8,16,1024]{3,2,1,0:T(8,128)} %draw.3) | copy-start | bytes 3145732
  30.7 8.8 %collective-permute-start.7 = (f32[4,16,1024]{2,1,0:T(8,128)S(1)}, f32[4,16,1024]{2,1,0:T(8,128)S(1)}, u32[]{:S(2)}, u32[]{:S(2)}) collective-permute-start(f32[4,16,1024]{2,1,0:T(8,128)S(1)} %get-tuple-element.51), channel_id=1, source_target_pairs={{0,1},{1,0},{2,3},{3,2},{4,5},{5,4},{6,7},{7,6},{8,9},{9,8},{10,11... | collective-permute-start | bytes 786440 | tf_op jit(solution)/shard_map/ppermute | solution.py:448
  30.8 13.0 %collective-permute-start.8 = (f32[4,16,1024]{2,1,0:T(8,128)S(1)}, f32[4,16,1024]{2,1,0:T(8,128)S(1)}, u32[]{:S(2)}, u32[]{:S(2)}) collective-permute-start(f32[4,16,1024]{2,1,0:T(8,128)S(1)} %get-tuple-element.52), channel_id=1, source_target_pairs={{0,31},{1,2},{2,1},{3,4},{4,3},{5,6},{6,5},{7,8},{8,7},{9,10},{10,... | collective-permute-start | bytes 786440 | tf_op jit(solution)/shard_map/ppermute | solution.py:448
  34.6 1.4 %collective-permute-start.2 = (f32[2,16,1024]{2,1,0:T(8,128)S(1)}, f32[2,16,1024]{2,1,0:T(8,128)S(1)}, u32[]{:S(2)}, u32[]{:S(2)}) collective-permute-start(f32[2,16,1024]{2,1,0:T(8,128)S(1)} %mass_inner.1.mine), channel_id=1, source_target_pairs={{0,32},{32,0},{64,96},{96,64},{1,33},{33,1},{65,97},{97,65},{2,34}... | collective-permute-start | bytes 393224 | tf_op jit(solution)/shard_map/ppermute | solution.py:478
  46.1 7.9 %collective-permute-start.9 = (f32[4,16,1024]{2,1,0:T(8,128)S(1)}, f32[4,16,1024]{2,1,0:T(8,128)S(1)}, u32[]{:S(2)}, u32[]{:S(2)}) collective-permute-start(f32[4,16,1024]{2,1,0:T(8,128)S(1)} %get-tuple-element.62), channel_id=1, source_target_pairs={{0,1},{1,0},{2,3},{3,2},{4,5},{5,4},{6,7},{7,6},{8,9},{9,8},{10,11... | collective-permute-start | bytes 786440 | tf_op jit(solution)/shard_map/ppermute | solution.py:448
  46.1 12.1 %collective-permute-start.10 = (f32[4,16,1024]{2,1,0:T(8,128)S(1)}, f32[4,16,1024]{2,1,0:T(8,128)S(1)}, u32[]{:S(2)}, u32[]{:S(2)}) collective-permute-start(f32[4,16,1024]{2,1,0:T(8,128)S(1)} %get-tuple-element.63), channel_id=1, source_target_pairs={{0,31},{1,2},{2,1},{3,4},{4,3},{5,6},{6,5},{7,8},{8,7},{9,10},{10,... | collective-permute-start | bytes 786440 | tf_op jit(solution)/shard_map/ppermute | solution.py:448
  49.8 1.2 %copy-start.4 = (f32[2,8,16,1024]{3,2,1,0:T(8,128)S(1)}, f32[2,8,16,1024]{3,2,1,0:T(8,128)}, u32[]{:S(2)}) copy-start(f32[2,8,16,1024]{3,2,1,0:T(8,128)} %get-tuple-element.35.q) | copy-start | bytes 3145732

commit v4 on v3

v4 whole, which is shorter than its diff:
```python
import jax
import jax.numpy as jnp
from jax import lax
from jax.experimental import pallas as pl
from jax.experimental.pallas import tpu as pltpu
from jax.sharding import PartitionSpec as P

LEAPS = 2

unit = -0.05
inv_noise = 0.25
prior_weight = 0.5
step_size = 0.05
LANES = 128
WIDE = 2


VECTOR = pl.BlockSpec(memory_space=pltpu.VMEM)
MEMORY = pl.BlockSpec(memory_space=pltpu.HBM)


def call(kernel, out_shapes, scratch, name, work, ins=None, outs=None, aliases=None, limit=32):
    more = {} if ins is None else {"in_specs": ins}
    if aliases:
        more["input_output_aliases"] = aliases
    return pl.pallas_call(
        kernel,
        out_shape=[jax.ShapeDtypeStruct(shape, jnp.float32) for shape in out_shapes],
        out_specs=outs or [VECTOR] * len(out_shapes),
        scratch_shapes=[
            pltpu.VMEM(shape, jnp.float32) if isinstance(shape, tuple) else shape
            for shape in scratch
        ],
        compiler_params=pltpu.CompilerParams(vmem_limit_bytes=limit << 20),
        cost_estimate=pl.CostEstimate(flops=work, bytes_accessed=work // 8, transcendentals=0),
        name=name,
        **more,
    )


def tiles(width):
    return [slice(j * LANES, (j + 1) * LANES) for j in range(width // LANES)]


def depth_sum(v):
    depth = v.shape[0]
    row = lax.broadcasted_iota(jnp.int32, v.shape, 0)
    below = jnp.where(row == 0, 0.0, pltpu.roll(v, 1, 0))
    above = jnp.where(row == depth - 1, 0.0, pltpu.roll(v, depth - 1, 0))
    return below + above


def stencil(planes, deeps):
    cuts = tiles(planes[1].shape[-1])
    edge_terms, own_terms = [], []
    for cut in cuts:
        v = planes[1][:, cut]
        w = deeps[1][:, cut] + (planes[0][:, cut] + planes[2][:, cut])
        corner = deeps[0][:, cut] + deeps[2][:, cut]
        t = 6.0 * v + (2.0 * w + corner)
        d = t + w
        edge_terms.append(t)
        own_terms.append((d + d) - 92.0 * v)
    lane = lax.broadcasted_iota(jnp.int32, edge_terms[0].shape, 1)
    ups = [pltpu.roll(t, 1, 1) for t in edge_terms]
    downs = [pltpu.roll(t, LANES - 1, 1) for t in edge_terms]
    result = []
    for j in range(len(cuts)):
        before = ups[j - 1] if j else 0.0
        after = downs[j + 1] if j + 1 < len(cuts) else 0.0
        left = jnp.where(lane == 0, before, ups[j])
        right = jnp.where(lane == LANES - 1, after, downs[j])
        result.append(own_terms[j] + (left + right))
    return list(zip(cuts, result, strict=True))


def deepen(deep, source):
    for cut in tiles(source.shape[-1]):
        deep[:, cut] = depth_sum(source[:, cut])


def weigh(view, deep, nu, target, out, out_deep):
    total = 0.0
    for cut, k in stencil(view, deep):
        n = nu[:, cut]
        misfit = (unit * n) * k - target[:, cut]
        s = n * misfit
        out[:, cut] = s
        out_deep[:, cut] = depth_sum(s)
        total = total + misfit * misfit
    return total


def fold(total):
    return total[:8] + total[8:]


def whole(q):
    return lambda chain, x: q.at[chain, x]


def parts(rim, inner):
    planes = inner.shape[1] + 2 * WIDE

    def at(chain, x):
        if x < WIDE:
            return rim.at[chain, x]
        if x >= planes - WIDE:
            return rim.at[chain, x - planes + 2 * WIDE]
        return inner.at[chain, x - WIDE]

    return at


def interior(q_at, nu, obs, scaled, deep, scaled_deep, use):
    chains, planes = deep.shape[:2]
    totals = []
    for chain in range(chains):
        for x in range(planes):
            deepen(deep.at[chain, x], q_at(chain, x))
    for chain in range(chains):
        total = 0.0
        for x in range(1, planes - 1):
            near = range(x - 1, x + 2)
            total = total + weigh(
                [q_at(chain, i) for i in near],
                [deep.at[chain, i] for i in near],
                nu.at[x],
                obs.at[x],
                scaled.at[chain, x - 1],
                scaled_deep.at[chain, x - 1],
            )
        totals.append(total)
    for chain in range(chains):
        for x in range(2, planes - 2):
            near = range(x - 2, x + 1)
            view = [scaled.at[chain, i] for i in near]
            for cut, k in stencil(view, [scaled_deep.at[chain, i] for i in near]):
                v = q_at(chain, x)[:, cut]
                use(chain, x, cut, v, (inv_noise * unit) * k + prior_weight * v)
    return totals


def parity():
    return lax.rem(lax.axis_index("gx"), 2)


def place_halo(halo, from_a, from_b):
    odd = parity()
    chains = halo.shape[1]
    for chain in range(chains):
        for i in range(WIDE):
            halo[1 - odd, chain, i] = from_a[chain * WIDE + i]
            halo[odd, chain, i] = from_b[chain * WIDE + i]


def rims(q_at, halo, nu, obs, nu_halo, obs_halo, scaled, deep, rim_scaled, scaled_deep, use):
    chains, planes = scaled.shape[0], scaled.shape[1] + 2

    def at(chain, x):
        if x < 0:
            return halo.at[0, chain, WIDE + x]
        if x >= planes:
            return halo.at[1, chain, x - planes]
        return q_at(chain, x)

    def scaled_at(chain, x):
        if x in (-1, 0):
            return rim_scaled.at[chain, x + 1]
        if x in (planes - 1, planes):
            return rim_scaled.at[chain, x - planes + 3]
        return scaled.at[chain, x - 1]

    sides = ((-2, -1, 0, 1), (planes + 1, planes, planes - 1, planes - 2))
    totals = []
    for chain in range(chains):
        for side in sides:
            for x in side:
                deepen(deep.at[chain, x + WIDE], at(chain, x))
    for chain in range(chains):
        total = 0.0
        for s, side in enumerate(sides):
            for x in side[1:3]:
                outer = x == side[1]
                near = range(x - 1, x + 2)
                squares = weigh(
                    [at(chain, i) for i in near],
                    [deep.at[chain, i + WIDE] for i in near],
                    nu_halo.at[s] if outer else nu.at[x],
                    obs_halo.at[s] if outer else obs.at[x],
                    scaled_at(chain, x),
                    scaled_deep.at[chain, x + 1],
                )
                total = total if outer else total + squares
            for x in (1, 2) if s == 0 else (planes - 2, planes - 3):
                deepen(scaled_deep.at[chain, x + 1], scaled_at(chain, x))
        totals.append(total)
    for chain in range(chains):
        for x in (0, 1, planes - 2, planes - 1):
            near = range(x - 1, x + 2)
            view = [scaled_at(chain, i) for i in near]
            for cut, k in stencil(view, [scaled_deep.at[chain, i + 1] for i in near]):
                v = q_at(chain, x)[:, cut]
                use(chain, x, cut, v, (inv_noise * unit) * k + prior_weight * v)
    return totals


def entry_kernel(q, nu, obs, own, keep, send, to_a, to_b, sems):
    core, odd = lax.rem(lax.axis_index("chain"), 2), parity()
    chains, planes = own.shape[:2]
    half = planes // 2
    load = [pltpu.make_async_copy(q.at[chain], own.at[chain], sems.at[chain]) for chain in range(chains)]
    edges = []
    for i, (source, at) in enumerate(((nu, chains * WIDE), (obs, chains * WIDE + 1))):
        for k, (out, low) in enumerate(((to_a, odd), (to_b, 1 - odd))):
            edges.append(
                pltpu.make_async_copy(
                    source.at[(1 - low) * (planes - 1)], out.at[at], sems.at[chains + 2 * i + k]
                )
            )
    for copy in load + edges:
        copy.start()
    for copy in load:
        copy.wait()
    for chain in range(chains):
        for i in range(WIDE):
            to_a[chain * WIDE + i] = own[chain, (1 - odd) * (planes - WIDE) + i]
            to_b[chain * WIDE + i] = own[chain, odd * (planes - WIDE) + i]
    for x in range(half):
        for out, base in ((keep, core * half), (send, (1 - core) * half)):
            for cut in tiles(own.shape[-1]):
                first = own[0, base + x, :, cut]
                second = first * first
                for chain in range(1, chains):
                    v = own[chain, base + x, :, cut]
                    first = first + v
                    second = second + v * v
                out[x, 0, :, cut] = first
                out[x, 1, :, cut] = second
    for copy in edges:
        copy.wait()


def add_kernel(rim, a, b, *rest):
    core = lax.rem(lax.axis_index("chain"), 2)
    out = rest[-1]
    count = out.shape[0]
    for x in range(count):
        at = (core if rim else 1 - core) * count + x
        out[x] = a[at] + b[at]


def mass_kernel(count, a, b, *rest):
    out = rest[-1]
    for x in range(a.shape[0]):
        mean = (a[x, 0] + b[x, 0]) / count
        out[x] = 0.5 + (a[x, 1] + b[x, 1]) / count - mean * mean


def first_inner_kernel(q, nu, obs, scaled, slope, potential, deep, scaled_deep):
    chains, planes = q.shape[:2]

    def use(chain, x, cut, v, value):
        slope[chain, x - 2, :, cut] = value

    misfits = interior(whole(q), nu, obs, scaled, deep, scaled_deep, use)
    for chain in range(chains):
        squares = 0.0
        for x in range(planes):
            for cut in tiles(q.shape[-1]):
                v = q[chain, x, :, cut]
                squares = squares + v * v
        potential[chain] = fold(
            (0.5 * inv_noise) * misfits[chain] + (0.5 * prior_weight) * squares
        )


def first_rim_kernel(
    q, from_a, from_b, nu, obs, scaled, before,
    slope, nu_halo, obs_halo, potential, halo, deep, rim_scaled, scaled_deep,
):
    odd = parity()
    chains, planes = q.shape[:2]
    place_halo(halo, from_a, from_b)
    for out, at in ((nu_halo, chains * WIDE), (obs_halo, chains * WIDE + 1)):
        out[1 - odd] = from_a[at]
        out[odd] = from_b[at]

    def use(chain, x, cut, v, value):
        slope[chain, x if x < 2 else x - planes + 4, :, cut] = value

    misfits = rims(
        whole(q), halo, nu, obs, nu_halo, obs_halo, scaled, deep, rim_scaled, scaled_deep, use
    )
    for chain in range(chains):
        potential[chain] = before[chain] + fold((0.5 * inv_noise) * misfits[chain])


def launch(q, draw, slope, mine, other, base, new_q, new_p, mass, totals):
    chains = q.shape[0]
    for part, (start, offset) in ((mine, base[0]), (other, base[1])):
        for i in range(part.shape[0]):
            for cut in tiles(q.shape[-1]):
                im = part[i, :, cut]
                mass[offset + i, :, cut] = im
                inverse_root = 1.0 / jnp.sqrt(im)
                for chain in range(chains):
                    p = draw[chain, start + i, :, cut] * inverse_root
                    totals[chain] = totals[chain] + im * p * p
                    p = p - (0.5 * step_size) * slope[chain, offset + i, :, cut]
                    new_p[chain, offset + i, :, cut] = p
                    new_q[chain, offset + i, :, cut] = (
                        q[chain, start + i, :, cut] + step_size * im * p
                    )


def send_rims(source, to_a, to_b):
    odd = parity()
    for chain in range(source.shape[0]):
        for i in range(WIDE):
            to_a[chain * WIDE + i] = source[chain, (1 - odd) * WIDE + i]
            to_b[chain * WIDE + i] = source[chain, odd * WIDE + i]


def launch_rim_kernel(q, draw, slope, mine, other, new_q, new_p, mass, kinetic, to_a, to_b):
    core = lax.rem(lax.axis_index("chain"), 2)
    chains, planes = q.shape[:2]
    far = planes - WIDE
    totals = [0.0] * chains
    base = ((core * far, core * WIDE), ((1 - core) * far, (1 - core) * WIDE))
    launch(q, draw, slope, mine, other, base, new_q, new_p, mass, totals)
    for chain in range(chains):
        kinetic[chain] = fold(0.5 * totals[chain])
    send_rims(new_q, to_a, to_b)


def launch_inner_kernel(q, draw, slope, mine, other, before, new_q, new_p, mass, kinetic):
    core = lax.rem(lax.axis_index("chain"), 2)
    chains, planes = q.shape[:2]
    half = planes // 2 - WIDE
    totals = [0.0] * chains
    base = tuple((WIDE + c * half, c * half) for c in (core, 1 - core))
    launch(q, draw, slope, mine, other, base, new_q, new_p, mass, totals)
    for chain in range(chains):
        kinetic[chain] = before[chain] + fold(0.5 * totals[chain])


def leap_inner_kernel(q_rim, q_inner, nu, obs, p, mass, scaled, new_q, new_p, deep, scaled_deep):
    def use(chain, x, cut, v, slope):
        at = x - WIDE
        moment = p[chain, at, :, cut] - step_size * slope
        new_p[chain, at, :, cut] = moment
        new_q[chain, at, :, cut] = v + step_size * mass[at, :, cut] * moment

    interior(parts(q_rim, q_inner), nu, obs, scaled, deep, scaled_deep, use)


def rim_index(x, planes):
    return x if x < WIDE else x - planes + 2 * WIDE


def leap_rim_kernel(
    q_rim, q_inner, from_a, from_b, nu, obs, nu_halo, obs_halo, p, mass, scaled,
    new_q, new_p, to_a, to_b, halo, deep, rim_scaled, scaled_deep,
):
    planes = q_inner.shape[1] + 2 * WIDE
    place_halo(halo, from_a, from_b)

    def use(chain, x, cut, v, slope):
        at = rim_index(x, planes)
        moment = p[chain, at, :, cut] - step_size * slope
        new_p[chain, at, :, cut] = moment
        new_q[chain, at, :, cut] = v + step_size * mass[at, :, cut] * moment

    rims(
        parts(q_rim, q_inner), halo, nu, obs, nu_halo, obs_halo,
        scaled, deep, rim_scaled, scaled_deep, use,
    )
    send_rims(new_q, to_a, to_b)


def run(copies):
    for copy in copies:
        copy.start()
    for copy in copies:
        copy.wait()


def rim_copies(rim, out, sems):
    chains, planes = out.shape[:2]
    copies = []
    for chain in range(chains):
        for side, start in enumerate((0, planes - WIDE)):
            copies.append(
                pltpu.make_async_copy(
                    rim.at[chain, pl.ds(side * WIDE, WIDE)],
                    out.at[chain, pl.ds(start, WIDE)],
                    sems.at[2 * chain + side],
                )
            )
    return copies


def inner_copies(inner, out, sems):
    chains, planes = out.shape[:2]
    return [
        pltpu.make_async_copy(
            inner.at[chain], out.at[chain, pl.ds(WIDE, planes - 2 * WIDE)], sems.at[2 * chains + chain]
        )
        for chain in range(chains)
    ]


def store_kernel(rim, inner, out, token, sems):
    token[...] = jnp.zeros_like(token)
    run(rim_copies(rim, out, sems) + inner_copies(inner, out, sems))


def store_inner_kernel(inner, out, sems):
    run(inner_copies(inner, out, sems))


def last_inner_kernel(q_rim, q_inner, nu, obs, p, mass, scaled, new_p, energy, deep, scaled_deep):
    chains, planes = deep.shape[:2]
    q_at = parts(q_rim, q_inner)
    totals = [0.0] * chains

    def use(chain, x, cut, v, slope):
        at = x - WIDE
        moment = p[chain, at, :, cut] - (0.5 * step_size) * slope
        new_p[chain, at, :, cut] = moment
        totals[chain] = totals[chain] + (0.5 * mass[at, :, cut]) * (moment * moment)

    misfits = interior(q_at, nu, obs, scaled, deep, scaled_deep, use)
    for chain in range(chains):
        squares = 0.0
        for x in range(planes):
            view = q_at(chain, x)
            for cut in tiles(view.shape[-1]):
                v = view[:, cut]
                squares = squares + v * v
        energy[chain] = fold(
            (0.5 * inv_noise) * misfits[chain] + (0.5 * prior_weight) * squares + totals[chain]
        )


def last_rim_kernel(
    q_rim, q_inner, from_a, from_b, nu, obs, nu_halo, obs_halo, p, mass, scaled, energy,
    potential, kinetic, stored, partial_p,
    new_p, rows, halo, deep, rim_scaled, scaled_deep, rim_p, sems,
):
    chains, planes = new_p.shape[:2]
    totals = [0.0] * chains
    place_halo(halo, from_a, from_b)

    def use(chain, x, cut, v, slope):
        at = rim_index(x, planes)
        moment = p[chain, at, :, cut] - (0.5 * step_size) * slope
        rim_p[chain, at, :, cut] = moment
        totals[chain] = totals[chain] + (0.5 * mass[at, :, cut]) * (moment * moment)

    misfits = rims(
        parts(q_rim, q_inner), halo, nu, obs, nu_halo, obs_halo,
        scaled, deep, rim_scaled, scaled_deep, use,
    )
    copies = rim_copies(rim_p, new_p, sems)
    for copy in copies:
        copy.start()
    sub = lax.broadcasted_iota(jnp.int32, (8, LANES), 0)
    lane = lax.broadcasted_iota(jnp.int32, (8, LANES), 1)
    mark = jnp.zeros((8, LANES), jnp.float32)
    for chain in range(chains):
        end = energy[chain] + fold((0.5 * inv_noise) * misfits[chain] + totals[chain])
        start = potential[chain] + kinetic[chain]
        for row, tile in enumerate((start, end)):
            mark = jnp.where((sub == row) & (lane == chain), jnp.sum(tile), mark)
    for i in range(rows.shape[0]):
        rows[i] = mark
    for copy in copies:
        copy.wait()


def local(position, momentum_draw, viscosity, observed):
    chains, planes, depth, across = position.shape
    groups, slabs = lax.axis_size("chain"), lax.axis_size("gx")
    cells = planes * slabs * depth * across
    near = [(i, i ^ 1) for i in range(groups)]
    far = [(i, i ^ 2) for i in range(groups)]
    pair_a = [(i, i ^ 1) for i in range(slabs)]
    pair_b = [(i, (i + 1 if i % 2 else i - 1) % slabs) for i in range(slabs)]
    half = planes // 2
    plane = (depth, across)
    rest = planes - 2 * WIDE
    block = (chains, planes, *plane)
    rim_block = (chains, 2 * WIDE, *plane)
    inner_block = (chains, rest, *plane)
    halo = (2, chains, WIDE, *plane)
    edge = (chains * WIDE, *plane)
    sides = (2, *plane)
    tile = (chains, 8, LANES)
    scaled_shape = (chains, planes - 2, *plane)
    field = (chains, planes + 2 * WIDE, *plane)
    inner_scratch = [block, scaled_shape]
    rim_scratch = [halo, field, rim_block, (chains, planes + 2, *plane)]
    work = chains * planes * depth * across * 30

    def swap(to_a, to_b):
        return lax.ppermute(to_a, "gx", pair_a), lax.ppermute(to_b, "gx", pair_b)

    first_edge = (chains * WIDE + 2, *plane)
    sums = (half, 2, *plane)
    position, keep, send, to_a, to_b = call(
        entry_kernel, [block, sums, sums, first_edge, first_edge],
        [pltpu.SemaphoreType.DMA((chains + 4,))], "entry", work // 16, [MEMORY] * 3,
    )(*(pltpu.with_memory_space_constraint(a, pltpu.HBM) for a in (position, viscosity, observed)))
    from_a, from_b = swap(to_a, to_b)
    got = lax.ppermute(send, "chain", near)

    def mass_body(*refs):
        mass_kernel(chains * groups, *refs)

    def mass_of(count, rim, after, before_mass, name):
        def add_body(*refs):
            add_kernel(rim, *refs)

        part = call(add_body, [(count, 2, *plane)], [], name + "_add", work // 16)(keep, got, *after)[0]
        remote = lax.ppermute(part, "chain", far)
        mine = call(mass_body, [(count, *plane)], [], name, work // 16)(part, remote, *before_mass)[0]
        return mine, lax.ppermute(mine, "chain", near)

    scaled, inner_slope, potential = call(
        first_inner_kernel, [scaled_shape, inner_block, tile], inner_scratch, "first_inner", work
    )(position, viscosity, observed)
    mine, other = mass_of(WIDE, True, (), (potential,), "mass_rim")
    inner_mine, inner_other = mass_of(half - WIDE, False, (mine,), (), "mass_inner")
    slope, nu_halo, obs_halo, potential = call(
        first_rim_kernel, [rim_block, sides, sides, tile], rim_scratch, "first_rim", work
    )(position, from_a, from_b, viscosity, observed, scaled, potential)
    rim_q, rim_p, rim_mass, kinetic, to_a, to_b = call(
        launch_rim_kernel,
        [rim_block, rim_block, (2 * WIDE, *plane), tile, edge, edge],
        [], "launch_rim", work // 4,
    )(position, momentum_draw, slope, mine, other)
    from_a, from_b = swap(to_a, to_b)
    inner_q, inner_p, inner_mass, kinetic = call(
        launch_inner_kernel,
        [inner_block, inner_block, (rest, *plane), tile],
        [], "launch_inner", work // 4,
    )(position, momentum_draw, inner_slope, inner_mine, inner_other, kinetic)
    for _ in range(LEAPS - 1):
        old_rim, old_inner = rim_q, inner_q
        scaled, inner_q, inner_p = call(
            leap_inner_kernel, [scaled_shape, inner_block, inner_block], inner_scratch, "leap_inner", work
        )(old_rim, old_inner, viscosity, observed, inner_p, inner_mass)
        rim_q, rim_p, to_a, to_b = call(
            leap_rim_kernel, [rim_block, rim_block, edge, edge], rim_scratch, "leap_rim", work
        )(
            old_rim, old_inner, from_a, from_b, viscosity, observed, nu_halo, obs_halo,
            rim_p, rim_mass, scaled,
        )
        from_a, from_b = swap(to_a, to_b)
    copy_sems = pltpu.SemaphoreType.DMA((3 * chains,))
    q, stored = call(
        store_kernel, [block, (8, LANES)], [copy_sems], "store_q", work // 8, outs=[MEMORY, VECTOR]
    )(rim_q, inner_q)
    scaled, inner_p, energy = call(
        last_inner_kernel, [scaled_shape, inner_block, tile], inner_scratch, "last_inner", work
    )(rim_q, inner_q, viscosity, observed, inner_p, inner_mass)
    partial_p = call(
        store_inner_kernel, [block], [copy_sems], "store_p", work // 16, outs=[MEMORY]
    )(inner_p)[0]
    operands = (
        rim_q, inner_q, from_a, from_b, viscosity, observed, nu_halo, obs_halo, rim_p, rim_mass,
        scaled, energy, potential, kinetic, stored, partial_p,
    )
    p, rows = call(
        last_rim_kernel, [block, (slabs, 8, LANES)], [*rim_scratch, rim_block, copy_sems], "last_rim", work,
        [VECTOR] * (len(operands) - 1) + [MEMORY], [MEMORY, VECTOR], {len(operands) - 1: 0},
    )(*operands)
    rows = lax.all_to_all(rows, "gx", 0, 0, tiled=True)
    energies = jnp.sum(rows[:, :2, :chains], axis=0) / cells
    return (q, p, energies)


def solution(mesh):
    in_specs = (
        P("chain", "gx", None, None),
        P("chain", "gx", None, None),
        P("gx", None, None),
        P("gx", None, None),
    )
    out_specs = (P("chain", "gx", None, None), P("chain", "gx", None, None), P(None, "chain"))
    return jax.shard_map(local, mesh=mesh, in_specs=in_specs, out_specs=out_specs, check_vma=False)
```

time: 75.3 us -> 74.3 us (0.987)
  waiting for transfers between devices: 25.1 us -> 17.7 us
  starting transfers between devices: 19.3 us -> 26.1 us
  local copies, waits for them, and re-layouts: 3.52 us -> 0.01 us
  blocking collectives: 13.9 us -> 16.2 us
  Pallas kernels: 11.7 us -> 12.8 us
    ppermute x2, waiting for transfers between devices: 12.2 us -> 7.08 us  [mass_of(): remote = lax.ppermute(part, 'chain', far)]
    ppermute x6, waiting for transfers between devices: 11.8 us -> 7.27 us  [swap(): return (lax.ppermute(to_a, 'gx', pair_a), lax.ppermute(to_b, 'gx', pair_b))]
    ppermute x2, starting transfers between devices: 3.75 us -> 7.36 us  [mass_of(): remote = lax.ppermute(part, 'chain', far)]
    unnamed x12 -> x6, local copies, waits for them, and re-layouts: 3.52 us -> 0.01 us
    ppermute x6, starting transfers between devices: 15.1 us -> 18.5 us  [swap(): return (lax.ppermute(to_a, 'gx', pair_a), lax.ppermute(to_b, 'gx', pair_b))]
    all_to_all x1, blocking collectives: 13.9 us -> 16.2 us  [local(): rows = lax.all_to_all(rows, 'gx', 0, 0, tiled=True)]
    ppermute x1, waiting for transfers between devices: 0.01 us -> 1.9 us  [local(): got = lax.ppermute(send, 'chain', near)]
    pallas_call x7 -> x9, Pallas kernels: 3.87 us -> 4.99 us  [the longest x1 1.38 us: local(): call(entry_kernel, [block, sums, sums, first_edge, first_edge], [pltpu.Se...]
  transfers between devices with their start and end apart: 11 -> 11, of which waited for: 6 -> 6; matrix products, arithmetic and copies ran while one was open for 0% -> 0% of each run, Pallas kernels for 9% -> 11%
where the time goes in v4:
time: 74.3 us; the launch traced here: 74.1 us
  starting transfers between devices  26.1 us (35%)
  waiting for transfers between devices  17.7 us (24%)
  blocking collectives  16.2 us (22%)
  Pallas kernels  12.8 us (17%)
  between operations  0.77 us (1%)
    ppermute x6, starting transfers between devices, swap(): return (lax.ppermute(to_a, 'gx', pair_a), lax.ppermute(to_b, 'gx', pair_b))  18.5 us
    all_to_all x1, blocking collectives, local(): rows = lax.all_to_all(rows, 'gx', 0, 0, tiled=True)  16.2 us
    ppermute x2, starting transfers between devices, mass_of(): remote = lax.ppermute(part, 'chain', far)  7.36 us
    ppermute x6, waiting for transfers between devices, swap(): return (lax.ppermute(to_a, 'gx', pair_a), lax.ppermute(to_b, 'gx', pair_b))  7.27 us
    ppermute x2, waiting for transfers between devices, mass_of(): remote = lax.ppermute(part, 'chain', far)  7.08 us
    pallas_call x1, Pallas kernels, local(): call(last_rim_kernel, [block, (slabs, 8, LANES)], [*rim_scratch, rim_bloc...  2.07 us
    ppermute x1, waiting for transfers between devices, local(): got = lax.ppermute(send, 'chain', near)  1.9 us
    pallas_call x1, Pallas kernels, local(): call(last_inner_kernel, [scaled_shape, inner_block, tile], inner_scratch,...  1.52 us
  transfers between devices with their start and end apart: 11, of which 6 were waited for; matrix products, arithmetic and copies ran while one was open for 0% of the time, Pallas kernels for 11%

profile of v4, /device:TPU:0, one launch (start us, length us, event | category | flops | bytes accessed | tf_op | source)
XLA Modules:
  0.0 74.1 jit_solution(9334078742684032337)
XLA Ops:
  0.6 1.4 %entry.1 = (f32[2,8,16,1024]{3,2,1,0:T(8,128)S(1)}, f32[4,2,16,1024]{3,2,1,0:T(8,128)S(1)}, f32[4,2,16,1024]{3,2,1,0:T(8,128)S(1)}, f32[6,16,1024]{2,1,0:T(8,128)S(1)}, f32[6,16,1024]{2,1,0:T(8,128)S(1)}) custom-call(f32[2,8,16,1024]{3,2,1,0:T(8,128)} %q.1, f32[8,16,1024]{2,1,0:T(8,128)} %nu.13, f32[8,16,1024]{2,1,0:T(8,128)} %obs.13), custom_call_target="tpu_custom_call" | custom-call | flops 491520 | bytes 61440 | tf_op jit(solution)/shard_map/entry/pallas_call | solution.py:512
  2.1 1.9 %collective-permute-done.2.refs_1_ = f32[4,2,16,1024]{3,2,1,0:T(8,128)S(1)} collective-permute-done((f32[4,2,16,1024]{3,2,1,0:T(8,128)S(1)}, f32[4,2,16,1024]{3,2,1,0:T(8,128)S(1)}, u32[]{:S(2)}, u32[]{:S(2)}) %collective-permute-start.2) | collective-permute-done | bytes 524320 | tf_op jit(solution)/shard_map/ppermute | solution.py:517
  4.0 4.0 %collective-permute-start.3 = (f32[2,2,16,1024]{3,2,1,0:T(8,128)S(1)}, f32[2,2,16,1024]{3,2,1,0:T(8,128)S(1)}, u32[]{:S(2)}, u32[]{:S(2)}) collective-permute-start(f32[2,2,16,1024]{3,2,1,0:T(8,128)S(1)} %mass_rim_add.1.refs_0_), channel_id=1, source_target_pairs={{0,64},{32,96},{64,0},{96,32},{1,65},{33,97},{65,1},{97,33},{2,66}... | collective-permute-start | bytes 786440 | tf_op jit(solution)/shard_map/ppermute | solution.py:527
  8.1 1.5 %collective-permute-start = (f32[6,16,1024]{2,1,0:T(8,128)S(1)}, f32[6,16,1024]{2,1,0:T(8,128)S(1)}, u32[]{:S(2)}, u32[]{:S(2)}) collective-permute-start(f32[6,16,1024]{2,1,0:T(8,128)S(1)} %get-tuple-element.40), channel_id=1, source_target_pairs={{0,1},{1,0},{2,3},{3,2},{4,5},{5,4},{6,7},{7,6},{8,9},{9,8},{10,11... | collective-permute-start | bytes 1179656 | tf_op jit(solution)/shard_map/ppermute | solution.py:508
  9.6 5.0 %collective-permute-start.1 = (f32[6,16,1024]{2,1,0:T(8,128)S(1)}, f32[6,16,1024]{2,1,0:T(8,128)S(1)}, u32[]{:S(2)}, u32[]{:S(2)}) collective-permute-start(f32[6,16,1024]{2,1,0:T(8,128)S(1)} %get-tuple-element.41), channel_id=1, source_target_pairs={{0,31},{1,2},{2,1},{3,4},{4,3},{5,6},{6,5},{7,8},{8,7},{9,10},{10,... | collective-permute-start | bytes 1179656 | tf_op jit(solution)/shard_map/ppermute | solution.py:508
  14.6 1.4 %first_inner.1 = (f32[2,6,16,1024]{3,2,1,0:T(8,128)S(1)}, f32[2,4,16,1024]{3,2,1,0:T(8,128)S(1)}, f32[2,8,128]{2,1,0:T(8,128)S(1)}) custom-call(f32[2,8,16,1024]{3,2,1,0:T(8,128)S(1)} %get-tuple-element.39.q, f32[8,16,1024]{2,1,0:T(8,128)S(1)} %copy-done, f32[8,16,1024]{2,1,0:T(8,128)S(1)} %copy-done.1), custom_call_target="tpu_custom_call" | custom-call | flops 7864320 | bytes 983040 | tf_op jit(solution)/shard_map/first_inner/pallas_call | solution.py:531
  16.0 7.1 %collective-permute-done.3.refs_1_ = f32[2,2,16,1024]{3,2,1,0:T(8,128)S(1)} collective-permute-done((f32[2,2,16,1024]{3,2,1,0:T(8,128)S(1)}, f32[2,2,16,1024]{3,2,1,0:T(8,128)S(1)}, u32[]{:S(2)}, u32[]{:S(2)}) %collective-permute-start.3) | collective-permute-done | bytes 262176 | tf_op jit(solution)/shard_map/ppermute | solution.py:527
  23.2 3.3 %collective-permute-start.5 = (f32[2,2,16,1024]{3,2,1,0:T(8,128)S(1)}, f32[2,2,16,1024]{3,2,1,0:T(8,128)S(1)}, u32[]{:S(2)}, u32[]{:S(2)}) collective-permute-start(f32[2,2,16,1024]{3,2,1,0:T(8,128)S(1)} %mass_inner_add.1.refs_0_), channel_id=1, source_target_pairs={{0,64},{32,96},{64,0},{96,32},{1,65},{33,97},{65,1},{97,33},{2,66}... | collective-permute-start | bytes 786440 | tf_op jit(solution)/shard_map/ppermute | solution.py:527
  26.6 1.2 %first_rim.1 = (f32[2,4,16,1024]{3,2,1,0:T(8,128)S(1)}, f32[2,16,1024]{2,1,0:T(8,128)S(1)}, f32[2,16,1024]{2,1,0:T(8,128)S(1)}, f32[2,8,128]{2,1,0:T(8,128)S(1)}) custom-call(f32[2,8,16,1024]{3,2,1,0:T(8,128)S(1)} %get-tuple-element.39.q, f32[6,16,1024]{2,1,0:T(8,128)S(1)} %collective-permute-done.from_a, f32[6,16,1024]{2,1,0:T(8,128)S(1)} %collective-permute-done.1.from_b, ...), custom_call_target="tpu_custom_call" | custom-call | flops 7864320 | bytes 983040 | tf_op jit(solution)/shard_map/first_rim/pallas_call | solution.py:536
  27.9 0.3 launch_rim.1
  28.3 5.8 %collective-permute-start.8 = (f32[4,16,1024]{2,1,0:T(8,128)S(1)}, f32[4,16,1024]{2,1,0:T(8,128)S(1)}, u32[]{:S(2)}, u32[]{:S(2)}) collective-permute-start(f32[4,16,1024]{2,1,0:T(8,128)S(1)} %get-tuple-element.52), channel_id=1, source_target_pairs={{0,31},{1,2},{2,1},{3,4},{4,3},{5,6},{6,5},{7,8},{8,7},{9,10},{10,... | collective-permute-start | bytes 786440 | tf_op jit(solution)/shard_map/ppermute | solution.py:508
  34.2 1.3 %collective-permute-done.6.other = f32[2,16,1024]{2,1,0:T(8,128)S(1)} collective-permute-done((f32[2,16,1024]{2,1,0:T(8,128)S(1)}, f32[2,16,1024]{2,1,0:T(8,128)S(1)}, u32[]{:S(2)}, u32[]{:S(2)}) %collective-permute-start.6) | collective-permute-done | bytes 131104 | tf_op jit(solution)/shard_map/ppermute | solution.py:529
  35.5 0.3 launch_inner.1
  35.8 1.3 %leap_inner.1 = (f32[2,6,16,1024]{3,2,1,0:T(8,128)S(1)}, f32[2,4,16,1024]{3,2,1,0:T(8,128)S(1)}, f32[2,4,16,1024]{3,2,1,0:T(8,128)S(1)}) custom-call(f32[2,4,16,1024]{3,2,1,0:T(8,128)S(1)} %get-tuple-element.47.q_rim, f32[2,4,16,1024]{3,2,1,0:T(8,128)S(1)} %get-tuple-element.50.q_inner, f32[8,16,1024]{2,1,0:T(8,128)S(1)} %copy-done, ...), custom_call_target="tpu_custom_call" | custom-call | flops 7864320 | bytes 983040 | tf_op jit(solution)/shard_map/leap_inner/pallas_call | solution.py:552
  37.1 4.0 %collective-permute-done.8.from_b = f32[4,16,1024]{2,1,0:T(8,128)S(1)} collective-permute-done((f32[4,16,1024]{2,1,0:T(8,128)S(1)}, f32[4,16,1024]{2,1,0:T(8,128)S(1)}, u32[]{:S(2)}, u32[]{:S(2)}) %collective-permute-start.8) | collective-permute-done | bytes 262176 | tf_op jit(solution)/shard_map/ppermute | solution.py:508
  41.2 1.3 %leap_rim.1 = (f32[2,4,16,1024]{3,2,1,0:T(8,128)S(1)}, f32[2,4,16,1024]{3,2,1,0:T(8,128)S(1)}, f32[4,16,1024]{2,1,0:T(8,128)S(1)}, f32[4,16,1024]{2,1,0:T(8,128)S(1)}) custom-call(f32[2,4,16,1024]{3,2,1,0:T(8,128)S(1)} %get-tuple-element.47.q_rim, f32[2,4,16,1024]{3,2,1,0:T(8,128)S(1)} %get-tuple-element.50.q_inner, ...), custom_call_target="tpu_custom_call" | custom-call | flops 7864320 | bytes 983040 | tf_op jit(solution)/shard_map/leap_rim/pallas_call | solution.py:555
  42.6 6.0 %collective-permute-start.10 = (f32[4,16,1024]{2,1,0:T(8,128)S(1)}, f32[4,16,1024]{2,1,0:T(8,128)S(1)}, u32[]{:S(2)}, u32[]{:S(2)}) collective-permute-start(f32[4,16,1024]{2,1,0:T(8,128)S(1)} %get-tuple-element.64), channel_id=1, source_target_pairs={{0,31},{1,2},{2,1},{3,4},{4,3},{5,6},{6,5},{7,8},{8,7},{9,10},{10,... | collective-permute-start | bytes 786440 | tf_op jit(solution)/shard_map/ppermute | solution.py:508
  48.7 1.5 %last_inner.1 = (f32[2,6,16,1024]{3,2,1,0:T(8,128)S(1)}, f32[2,4,16,1024]{3,2,1,0:T(8,128)S(1)}, f32[2,8,128]{2,1,0:T(8,128)S(1)}) custom-call(f32[2,4,16,1024]{3,2,1,0:T(8,128)S(1)} %get-tuple-element.60.rim.q_rim, f32[2,4,16,1024]{3,2,1,0:T(8,128)S(1)} %get-tuple-element.61.inner.q_inner, f32[8,16,1024]{2,1,0:T(8,128)S(1)} %copy-done, ...), custom_call_target="tpu_custom_call" | custom-call | flops 7864320 | bytes 983040 | tf_op jit(solution)/shard_map/last_inner/pallas_call | solution.py:566
  50.2 0.8 %store_p.1.partial_p = f32[2,8,16,1024]{3,2,1,0:T(8,128)} custom-call(f32[2,4,16,1024]{3,2,1,0:T(8,128)S(1)} %get-tuple-element.72.inner), custom_call_target="tpu_custom_call" | custom-call | flops 491520 | bytes 61440 | tf_op jit(solution)/shard_map/store_p/pallas_call | solution.py:569
  51.0 1.0 %store_q.1 = (f32[2,8,16,1024]{3,2,1,0:T(8,128)}, f32[8,128]{1,0:T(8,128)S(1)}) custom-call(f32[2,4,16,1024]{3,2,1,0:T(8,128)S(1)} %get-tuple-element.60.rim.q_rim, f32[2,4,16,1024]{3,2,1,0:T(8,128)S(1)} %get-tuple-element.61.inner.q_inner), custom_call_target="tpu_custom_call" | custom-call | flops 983040 | bytes 122880 | tf_op jit(solution)/shard_map/store_q/pallas_call | solution.py:563
  52.1 3.2 %collective-permute-done.10.from_b = f32[4,16,1024]{2,1,0:T(8,128)S(1)} collective-permute-done((f32[4,16,1024]{2,1,0:T(8,128)S(1)}, f32[4,16,1024]{2,1,0:T(8,128)S(1)}, u32[]{:S(2)}, u32[]{:S(2)}) %collective-permute-start.10) | collective-permute-done | bytes 262176 | tf_op jit(solution)/shard_map/ppermute | solution.py:508
  55.3 2.1 %last_rim.1 = (f32[2,8,16,1024]{3,2,1,0:T(8,128)}, f32[32,8,128]{2,1,0:T(8,128)S(1)}) custom-call(f32[2,4,16,1024]{3,2,1,0:T(8,128)S(1)} %get-tuple-element.60.rim.q_rim, f32[2,4,16,1024]{3,2,1,0:T(8,128)S(1)} %get-tuple-element.61.inner.q_inner, f32[4,16,1024]{2,1,0:T(8,128)S(1)} %collective-permute-done.9.from_a, ...), custom_call_target="tpu_custom_call", output_to_operand_aliasing={{0}: (15, {})} | custom-call | flops 7864320 | bytes 983040 | tf_op jit(solution)/shard_map/last_rim/pallas_call | solution.py:576
  57.4 16.2 %all_to_all.5 = f32[32,8,128]{2,1,0:T(8,128)S(1)} all-to-all(f32[32,8,128]{2,1,0:T(8,128)S(1)} %get-tuple-element.74), channel_id=1, replica_groups=mesh['chain'=4,'gx'=32] {'gx'}, dimensions={0} | all-to-all | bytes 262144 | tf_op jit(solution)/shard_map/all_to_all | solution.py:580
  73.6 0.6 broadcast_multiply_fusion
  (22 shorter events, 0.8 us)
Async XLA Ops:
  2.0 2.0 %collective-permute-start.2 = (f32[4,2,16,1024]{3,2,1,0:T(8,128)S(1)}, f32[4,2,16,1024]{3,2,1,0:T(8,128)S(1)}, u32[]{:S(2)}, u32[]{:S(2)}) collective-permute-start(f32[4,2,16,1024]{3,2,1,0:T(8,128)S(1)} %get-tuple-element.46), channel_id=1, source_target_pairs={{0,32},{32,0},{64,96},{96,64},{1,33},{33,1},{65,97},{97,65},{2,34}... | collective-permute-start | bytes 1572872 | tf_op jit(solution)/shard_map/ppermute | solution.py:517
  4.0 10.6 %copy-start = (f32[8,16,1024]{2,1,0:T(8,128)S(1)}, f32[8,16,1024]{2,1,0:T(8,128)}, u32[]{:S(2)}) copy-start(f32[8,16,1024]{2,1,0:T(8,128)} %nu.13) | copy-start | bytes 1572868
  4.0 10.6 %copy-start.1 = (f32[8,16,1024]{2,1,0:T(8,128)S(1)}, f32[8,16,1024]{2,1,0:T(8,128)}, u32[]{:S(2)}) copy-start(f32[8,16,1024]{2,1,0:T(8,128)} %obs.13) | copy-start | bytes 1572868
  4.0 19.1 %collective-permute-start.3 = (f32[2,2,16,1024]{3,2,1,0:T(8,128)S(1)}, f32[2,2,16,1024]{3,2,1,0:T(8,128)S(1)}, u32[]{:S(2)}, u32[]{:S(2)}) collective-permute-start(f32[2,2,16,1024]{3,2,1,0:T(8,128)S(1)} %mass_rim_add.1.refs_0_), channel_id=1, source_target_pairs={{0,64},{32,96},{64,0},{96,32},{1,65},{33,97},{65,1},{97,33},{2,66}... | collective-permute-start | bytes 786440 | tf_op jit(solution)/shard_map/ppermute | solution.py:527
  8.1 18.5 %collective-permute-start = (f32[6,16,1024]{2,1,0:T(8,128)S(1)}, f32[6,16,1024]{2,1,0:T(8,128)S(1)}, u32[]{:S(2)}, u32[]{:S(2)}) collective-permute-start(f32[6,16,1024]{2,1,0:T(8,128)S(1)} %get-tuple-element.40), channel_id=1, source_target_pairs={{0,1},{1,0},{2,3},{3,2},{4,5},{5,4},{6,7},{7,6},{8,9},{9,8},{10,11... | collective-permute-start | bytes 1179656 | tf_op jit(solution)/shard_map/ppermute | solution.py:508
  9.6 17.0 %collective-permute-start.1 = (f32[6,16,1024]{2,1,0:T(8,128)S(1)}, f32[6,16,1024]{2,1,0:T(8,128)S(1)}, u32[]{:S(2)}, u32[]{:S(2)}) collective-permute-start(f32[6,16,1024]{2,1,0:T(8,128)S(1)} %get-tuple-element.41), channel_id=1, source_target_pairs={{0,31},{1,2},{2,1},{3,4},{4,3},{5,6},{6,5},{7,8},{8,7},{9,10},{10,... | collective-permute-start | bytes 1179656 | tf_op jit(solution)/shard_map/ppermute | solution.py:508
  23.2 10.8 %collective-permute-start.5 = (f32[2,2,16,1024]{3,2,1,0:T(8,128)S(1)}, f32[2,2,16,1024]{3,2,1,0:T(8,128)S(1)}, u32[]{:S(2)}, u32[]{:S(2)}) collective-permute-start(f32[2,2,16,1024]{3,2,1,0:T(8,128)S(1)} %mass_inner_add.1.refs_0_), channel_id=1, source_target_pairs={{0,64},{32,96},{64,0},{96,32},{1,65},{33,97},{65,1},{97,33},{2,66}... | collective-permute-start | bytes 786440 | tf_op jit(solution)/shard_map/ppermute | solution.py:527
  26.5 1.3 %collective-permute-start.4 = (f32[2,16,1024]{2,1,0:T(8,128)S(1)}, f32[2,16,1024]{2,1,0:T(8,128)S(1)}, u32[]{:S(2)}, u32[]{:S(2)}) collective-permute-start(f32[2,16,1024]{2,1,0:T(8,128)S(1)} %mass_rim.1.mine.refs_2_), channel_id=1, source_target_pairs={{0,32},{32,0},{64,96},{96,64},{1,33},{33,1},{65,97},{97,65},{2,34}... | collective-permute-start | bytes 393224 | tf_op jit(solution)/shard_map/ppermute | solution.py:529
  26.5 1.3 %copy-start.2 = (f32[2,8,16,1024]{3,2,1,0:T(8,128)S(1)}, f32[2,8,16,1024]{3,2,1,0:T(8,128)}, u32[]{:S(2)}) copy-start(f32[2,8,16,1024]{3,2,1,0:T(8,128)} %draw.3) | copy-start | bytes 3145732
  28.2 8.9 %collective-permute-start.7 = (f32[4,16,1024]{2,1,0:T(8,128)S(1)}, f32[4,16,1024]{2,1,0:T(8,128)S(1)}, u32[]{:S(2)}, u32[]{:S(2)}) collective-permute-start(f32[4,16,1024]{2,1,0:T(8,128)S(1)} %get-tuple-element.51), channel_id=1, source_target_pairs={{0,1},{1,0},{2,3},{3,2},{4,5},{5,4},{6,7},{7,6},{8,9},{9,8},{10,11... | collective-permute-start | bytes 786440 | tf_op jit(solution)/shard_map/ppermute | solution.py:508
  28.3 12.9 %collective-permute-start.8 = (f32[4,16,1024]{2,1,0:T(8,128)S(1)}, f32[4,16,1024]{2,1,0:T(8,128)S(1)}, u32[]{:S(2)}, u32[]{:S(2)}) collective-permute-start(f32[4,16,1024]{2,1,0:T(8,128)S(1)} %get-tuple-element.52), channel_id=1, source_target_pairs={{0,31},{1,2},{2,1},{3,4},{4,3},{5,6},{6,5},{7,8},{8,7},{9,10},{10,... | collective-permute-start | bytes 786440 | tf_op jit(solution)/shard_map/ppermute | solution.py:508
  34.1 1.4 %collective-permute-start.6 = (f32[2,16,1024]{2,1,0:T(8,128)S(1)}, f32[2,16,1024]{2,1,0:T(8,128)S(1)}, u32[]{:S(2)}, u32[]{:S(2)}) collective-permute-start(f32[2,16,1024]{2,1,0:T(8,128)S(1)} %mass_inner.1.mine), channel_id=1, source_target_pairs={{0,32},{32,0},{64,96},{96,64},{1,33},{33,1},{65,97},{97,65},{2,34}... | collective-permute-start | bytes 393224 | tf_op jit(solution)/shard_map/ppermute | solution.py:529
  42.5 9.5 %collective-permute-start.9 = (f32[4,16,1024]{2,1,0:T(8,128)S(1)}, f32[4,16,1024]{2,1,0:T(8,128)S(1)}, u32[]{:S(2)}, u32[]{:S(2)}) collective-permute-start(f32[4,16,1024]{2,1,0:T(8,128)S(1)} %get-tuple-element.63), channel_id=1, source_target_pairs={{0,1},{1,0},{2,3},{3,2},{4,5},{5,4},{6,7},{7,6},{8,9},{9,8},{10,11... | collective-permute-start | bytes 786440 | tf_op jit(solution)/shard_map/ppermute | solution.py:508
  42.6 12.7 %collective-permute-start.10 = (f32[4,16,1024]{2,1,0:T(8,128)S(1)}, f32[4,16,1024]{2,1,0:T(8,128)S(1)}, u32[]{:S(2)}, u32[]{:S(2)}) collective-permute-start(f32[4,16,1024]{2,1,0:T(8,128)S(1)} %get-tuple-element.64), channel_id=1, source_target_pairs={{0,31},{1,2},{2,1},{3,4},{4,3},{5,6},{6,5},{7,8},{8,7},{9,10},{10,... | collective-permute-start | bytes 786440 | tf_op jit(solution)/shard_map/ppermute | solution.py:508

commit v5 on v4

--- a/solution.py
+++ b/solution.py
@@ -154,7 +154,9 @@
             halo[odd, chain, i] = from_b[chain * WIDE + i]
 
 
-def rims(q_at, halo, nu, obs, nu_halo, obs_halo, scaled, deep, rim_scaled, scaled_deep, use):
+def rims(
+    q_at, halo, nu, obs, nu_halo, obs_halo, scaled, deep, rim_scaled, scaled_deep, use, ready=None
+):
     chains, planes = scaled.shape[0], scaled.shape[1] + 2
 
     def at(chain, x):
@@ -202,6 +204,8 @@
             for cut, k in stencil(view, [scaled_deep.at[chain, i + 1] for i in near]):
                 v = q_at(chain, x)[:, cut]
                 use(chain, x, cut, v, (inv_noise * unit) * k + prior_weight * v)
+            if ready and x in (1, planes - 1):
+                ready(chain, x > 1)
     return totals
 
 
@@ -445,7 +449,7 @@
 
 
 def last_rim_kernel(
-    q_rim, q_inner, from_a, from_b, nu, obs, nu_halo, obs_halo, p, mass, scaled, energy,
+    cells, q_rim, q_inner, from_a, from_b, nu, obs, nu_halo, obs_halo, p, mass, scaled, energy,
     potential, kinetic, stored, partial_p,
     new_p, rows, halo, deep, rim_scaled, scaled_deep, rim_p, sems,
 ):
@@ -459,13 +463,12 @@
         rim_p[chain, at, :, cut] = moment
         totals[chain] = totals[chain] + (0.5 * mass[at, :, cut]) * (moment * moment)
 
+    copies = rim_copies(rim_p, new_p, sems)
     misfits = rims(
         parts(q_rim, q_inner), halo, nu, obs, nu_halo, obs_halo,
         scaled, deep, rim_scaled, scaled_deep, use,
+        lambda chain, high: copies[2 * chain + high].start(),
     )
-    copies = rim_copies(rim_p, new_p, sems)
-    for copy in copies:
-        copy.start()
     sub = lax.broadcasted_iota(jnp.int32, (8, LANES), 0)
     lane = lax.broadcasted_iota(jnp.int32, (8, LANES), 1)
     mark = jnp.zeros((8, LANES), jnp.float32)
@@ -473,7 +476,7 @@
         end = energy[chain] + fold((0.5 * inv_noise) * misfits[chain] + totals[chain])
         start = potential[chain] + kinetic[chain]
         for row, tile in enumerate((start, end)):
-            mark = jnp.where((sub == row) & (lane == chain), jnp.sum(tile), mark)
+            mark = jnp.where((sub == row) & (lane == chain), jnp.sum(tile) / cells, mark)
     for i in range(rows.shape[0]):
         rows[i] = mark
     for copy in copies:
@@ -532,7 +535,7 @@
         first_inner_kernel, [scaled_shape, inner_block, tile], inner_scratch, "first_inner", work
     )(position, viscosity, observed)
     mine, other = mass_of(WIDE, True, (), (potential,), "mass_rim")
-    inner_mine, inner_other = mass_of(half - WIDE, False, (mine,), (), "mass_inner")
+    inner_mine, inner_other = mass_of(half - WIDE, False, (), (), "mass_inner")
     slope, nu_halo, obs_halo, potential = call(
         first_rim_kernel, [rim_block, sides, sides, tile], rim_scratch, "first_rim", work
     )(position, from_a, from_b, viscosity, observed, scaled, potential)
@@ -569,16 +572,20 @@
     partial_p = call(
         store_inner_kernel, [block], [copy_sems], "store_p", work // 16, outs=[MEMORY]
     )(inner_p)[0]
+
+    def last_body(*refs):
+        last_rim_kernel(cells, *refs)
+
     operands = (
         rim_q, inner_q, from_a, from_b, viscosity, observed, nu_halo, obs_halo, rim_p, rim_mass,
         scaled, energy, potential, kinetic, stored, partial_p,
     )
     p, rows = call(
-        last_rim_kernel, [block, (slabs, 8, LANES)], [*rim_scratch, rim_block, copy_sems], "last_rim", work,
+        last_body, [block, (slabs, 8, LANES)], [*rim_scratch, rim_block, copy_sems], "last_rim", work,
         [VECTOR] * (len(operands) - 1) + [MEMORY], [MEMORY, VECTOR], {len(operands) - 1: 0},
     )(*operands)
     rows = lax.all_to_all(rows, "gx", 0, 0, tiled=True)
-    energies = jnp.sum(rows[:, :2, :chains], axis=0) / cells
+    energies = jnp.sum(rows[:, :2, :chains], axis=0)
     return (q, p, energies)
 
 

time: 74.3 us -> 71.3 us (0.960)
  starting transfers between devices: 26.1 us -> 19.5 us
  waiting for transfers between devices: 17.7 us -> 23.6 us
  blocking collectives: 16.2 us -> 13.9 us
    ppermute x2, waiting for transfers between devices: 7.08 us -> 11.2 us  [mass_of(): remote = lax.ppermute(part, 'chain', far)]
    ppermute x6, waiting for transfers between devices: 7.27 us -> 11 us  [swap(): return (lax.ppermute(to_a, 'gx', pair_a), lax.ppermute(to_b, 'gx', pair_b))]
    ppermute x2, starting transfers between devices: 7.36 us -> 3.77 us  [mass_of(): remote = lax.ppermute(part, 'chain', far)]
    ppermute x6, starting transfers between devices: 18.5 us -> 15.4 us  [swap(): return (lax.ppermute(to_a, 'gx', pair_a), lax.ppermute(to_b, 'gx', pair_b))]
    all_to_all x1, blocking collectives: 16.2 us -> 13.9 us  [local(): rows = lax.all_to_all(rows, 'gx', 0, 0, tiled=True)]
    ppermute x1, waiting for transfers between devices: 1.9 us -> 0.01 us  [local(): got = lax.ppermute(send, 'chain', near)]
  transfers between devices with their start and end apart: 11 -> 11, of which waited for: 6 -> 7; matrix products, arithmetic and copies ran while one was open for 0% -> 0% of each run, Pallas kernels for 11% -> 11%
where the time goes in v5:
time: 71.3 us; the launch traced here: 71.1 us
  waiting for transfers between devices  23.6 us (33%)
  starting transfers between devices  19.5 us (27%)
  blocking collectives  13.9 us (19%)
  Pallas kernels  12.8 us (18%)
  between operations  0.79 us (1%)
    ppermute x6, starting transfers between devices, swap(): return (lax.ppermute(to_a, 'gx', pair_a), lax.ppermute(to_b, 'gx', pair_b))  15.4 us
    all_to_all x1, blocking collectives, local(): rows = lax.all_to_all(rows, 'gx', 0, 0, tiled=True)  13.9 us
    ppermute x2, waiting for transfers between devices, mass_of(): remote = lax.ppermute(part, 'chain', far)  11.2 us
    ppermute x6, waiting for transfers between devices, swap(): return (lax.ppermute(to_a, 'gx', pair_a), lax.ppermute(to_b, 'gx', pair_b))  11 us
    ppermute x2, starting transfers between devices, mass_of(): remote = lax.ppermute(part, 'chain', far)  3.77 us
    pallas_call x1, Pallas kernels, local(): call(last_body, [block, (slabs, 8, LANES)], [*rim_scratch, rim_block, cop...  2.02 us
    pallas_call x1, Pallas kernels, local(): call(last_inner_kernel, [scaled_shape, inner_block, tile], inner_scratch,...  1.52 us
    pallas_call x1, Pallas kernels, local(): call(first_inner_kernel, [scaled_shape, inner_block, tile], inner_scratch...  1.45 us
  transfers between devices with their start and end apart: 11, of which 7 were waited for; matrix products, arithmetic and copies ran while one was open for 0% of the time, Pallas kernels for 11%

profile of v5, /device:TPU:0, one launch (start us, length us, event | category | flops | bytes accessed | tf_op | source)
XLA Modules:
  0.0 71.1 jit_solution(11321470735111644405)
XLA Ops:
  0.6 1.4 %entry.1 = (f32[2,8,16,1024]{3,2,1,0:T(8,128)S(1)}, f32[4,2,16,1024]{3,2,1,0:T(8,128)S(1)}, f32[4,2,16,1024]{3,2,1,0:T(8,128)S(1)}, f32[6,16,1024]{2,1,0:T(8,128)S(1)}, f32[6,16,1024]{2,1,0:T(8,128)S(1)}) custom-call(f32[2,8,16,1024]{3,2,1,0:T(8,128)} %q.1, f32[8,16,1024]{2,1,0:T(8,128)} %refs_4_.1, f32[8,16,1024]{2,1,0:T(8,128)} %refs_5_.1), custom_call_target="tpu_custom_call" | custom-call | flops 491520 | bytes 61440 | tf_op jit(solution)/shard_map/entry/pallas_call | solution.py:515
  2.1 1.7 %collective-permute-start = (f32[6,16,1024]{2,1,0:T(8,128)S(1)}, f32[6,16,1024]{2,1,0:T(8,128)S(1)}, u32[]{:S(2)}, u32[]{:S(2)}) collective-permute-start(f32[6,16,1024]{2,1,0:T(8,128)S(1)} %get-tuple-element.40), channel_id=1, source_target_pairs={{0,1},{1,0},{2,3},{3,2},{4,5},{5,4},{6,7},{7,6},{8,9},{9,8},{10,11... | collective-permute-start | bytes 1179656 | tf_op jit(solution)/shard_map/ppermute | solution.py:511
  3.8 5.9 %collective-permute-start.1 = (f32[6,16,1024]{2,1,0:T(8,128)S(1)}, f32[6,16,1024]{2,1,0:T(8,128)S(1)}, u32[]{:S(2)}, u32[]{:S(2)}) collective-permute-start(f32[6,16,1024]{2,1,0:T(8,128)S(1)} %get-tuple-element.41), channel_id=1, source_target_pairs={{0,31},{1,2},{2,1},{3,4},{4,3},{5,6},{6,5},{7,8},{8,7},{9,10},{10,... | collective-permute-start | bytes 1179656 | tf_op jit(solution)/shard_map/ppermute | solution.py:511
  9.7 3.7 %collective-permute-start.3 = (f32[2,2,16,1024]{3,2,1,0:T(8,128)S(1)}, f32[2,2,16,1024]{3,2,1,0:T(8,128)S(1)}, u32[]{:S(2)}, u32[]{:S(2)}) collective-permute-start(f32[2,2,16,1024]{3,2,1,0:T(8,128)S(1)} %mass_rim_add.1.refs_0_), channel_id=1, source_target_pairs={{0,64},{32,96},{64,0},{96,32},{1,65},{33,97},{65,1},{97,33},{2,66}... | collective-permute-start | bytes 786440 | tf_op jit(solution)/shard_map/ppermute | solution.py:530
  13.5 1.4 %first_inner.1 = (f32[2,6,16,1024]{3,2,1,0:T(8,128)S(1)}, f32[2,4,16,1024]{3,2,1,0:T(8,128)S(1)}, f32[2,8,128]{2,1,0:T(8,128)S(1)}) custom-call(f32[2,8,16,1024]{3,2,1,0:T(8,128)S(1)} %get-tuple-element.39.q, f32[8,16,1024]{2,1,0:T(8,128)S(1)} %copy-done, f32[8,16,1024]{2,1,0:T(8,128)S(1)} %copy-done.1), custom_call_target="tpu_custom_call" | custom-call | flops 7864320 | bytes 983040 | tf_op jit(solution)/shard_map/first_inner/pallas_call | solution.py:534
  15.0 11.2 %collective-permute-done.3.refs_1_ = f32[2,2,16,1024]{3,2,1,0:T(8,128)S(1)} collective-permute-done((f32[2,2,16,1024]{3,2,1,0:T(8,128)S(1)}, f32[2,2,16,1024]{3,2,1,0:T(8,128)S(1)}, u32[]{:S(2)}, u32[]{:S(2)}) %collective-permute-start.3) | collective-permute-done | bytes 262176 | tf_op jit(solution)/shard_map/ppermute | solution.py:530
  26.4 1.2 %first_rim.1 = (f32[2,4,16,1024]{3,2,1,0:T(8,128)S(1)}, f32[2,16,1024]{2,1,0:T(8,128)S(1)}, f32[2,16,1024]{2,1,0:T(8,128)S(1)}, f32[2,8,128]{2,1,0:T(8,128)S(1)}) custom-call(f32[2,8,16,1024]{3,2,1,0:T(8,128)S(1)} %get-tuple-element.39.q, f32[6,16,1024]{2,1,0:T(8,128)S(1)} %collective-permute-done.from_a, f32[6,16,1024]{2,1,0:T(8,128)S(1)} %collective-permute-done.1.from_b, ...), custom_call_target="tpu_custom_call" | custom-call | flops 7864320 | bytes 983040 | tf_op jit(solution)/shard_map/first_rim/pallas_call | solution.py:539
  27.7 0.3 launch_rim.1
  28.1 3.8 %collective-permute-start.8 = (f32[4,16,1024]{2,1,0:T(8,128)S(1)}, f32[4,16,1024]{2,1,0:T(8,128)S(1)}, u32[]{:S(2)}, u32[]{:S(2)}) collective-permute-start(f32[4,16,1024]{2,1,0:T(8,128)S(1)} %get-tuple-element.52), channel_id=1, source_target_pairs={{0,31},{1,2},{2,1},{3,4},{4,3},{5,6},{6,5},{7,8},{8,7},{9,10},{10,... | collective-permute-start | bytes 786440 | tf_op jit(solution)/shard_map/ppermute | solution.py:511
  32.0 1.3 %collective-permute-done.6.other = f32[2,16,1024]{2,1,0:T(8,128)S(1)} collective-permute-done((f32[2,16,1024]{2,1,0:T(8,128)S(1)}, f32[2,16,1024]{2,1,0:T(8,128)S(1)}, u32[]{:S(2)}, u32[]{:S(2)}) %collective-permute-start.6) | collective-permute-done | bytes 131104 | tf_op jit(solution)/shard_map/ppermute | solution.py:532
  33.3 0.3 launch_inner.1
  33.6 1.3 %leap_inner.1 = (f32[2,6,16,1024]{3,2,1,0:T(8,128)S(1)}, f32[2,4,16,1024]{3,2,1,0:T(8,128)S(1)}, f32[2,4,16,1024]{3,2,1,0:T(8,128)S(1)}) custom-call(f32[2,4,16,1024]{3,2,1,0:T(8,128)S(1)} %get-tuple-element.47.q_rim, f32[2,4,16,1024]{3,2,1,0:T(8,128)S(1)} %get-tuple-element.50.q_inner, f32[8,16,1024]{2,1,0:T(8,128)S(1)} %copy-done, ...), custom_call_target="tpu_custom_call" | custom-call | flops 7864320 | bytes 983040 | tf_op jit(solution)/shard_map/leap_inner/pallas_call | solution.py:555
  34.9 1.7 %collective-permute-done.7.from_a = f32[4,16,1024]{2,1,0:T(8,128)S(1)} collective-permute-done((f32[4,16,1024]{2,1,0:T(8,128)S(1)}, f32[4,16,1024]{2,1,0:T(8,128)S(1)}, u32[]{:S(2)}, u32[]{:S(2)}) %collective-permute-start.7) | collective-permute-done | bytes 262176 | tf_op jit(solution)/shard_map/ppermute | solution.py:511
  36.7 4.3 %collective-permute-done.8.from_b = f32[4,16,1024]{2,1,0:T(8,128)S(1)} collective-permute-done((f32[4,16,1024]{2,1,0:T(8,128)S(1)}, f32[4,16,1024]{2,1,0:T(8,128)S(1)}, u32[]{:S(2)}, u32[]{:S(2)}) %collective-permute-start.8) | collective-permute-done | bytes 262176 | tf_op jit(solution)/shard_map/ppermute | solution.py:511
  41.0 1.3 %leap_rim.1 = (f32[2,4,16,1024]{3,2,1,0:T(8,128)S(1)}, f32[2,4,16,1024]{3,2,1,0:T(8,128)S(1)}, f32[4,16,1024]{2,1,0:T(8,128)S(1)}, f32[4,16,1024]{2,1,0:T(8,128)S(1)}) custom-call(f32[2,4,16,1024]{3,2,1,0:T(8,128)S(1)} %get-tuple-element.47.q_rim, f32[2,4,16,1024]{3,2,1,0:T(8,128)S(1)} %get-tuple-element.50.q_inner, ...), custom_call_target="tpu_custom_call" | custom-call | flops 7864320 | bytes 983040 | tf_op jit(solution)/shard_map/leap_rim/pallas_call | solution.py:558
  42.4 3.9 %collective-permute-start.10 = (f32[4,16,1024]{2,1,0:T(8,128)S(1)}, f32[4,16,1024]{2,1,0:T(8,128)S(1)}, u32[]{:S(2)}, u32[]{:S(2)}) collective-permute-start(f32[4,16,1024]{2,1,0:T(8,128)S(1)} %get-tuple-element.64), channel_id=1, source_target_pairs={{0,31},{1,2},{2,1},{3,4},{4,3},{5,6},{6,5},{7,8},{8,7},{9,10},{10,... | collective-permute-start | bytes 786440 | tf_op jit(solution)/shard_map/ppermute | solution.py:511
  46.3 1.5 %last_inner.1 = (f32[2,6,16,1024]{3,2,1,0:T(8,128)S(1)}, f32[2,4,16,1024]{3,2,1,0:T(8,128)S(1)}, f32[2,8,128]{2,1,0:T(8,128)S(1)}) custom-call(f32[2,4,16,1024]{3,2,1,0:T(8,128)S(1)} %get-tuple-element.60.rim.q_rim.refs_0_, f32[2,4,16,1024]{3,2,1,0:T(8,128)S(1)} %get-tuple-element.61.inner.q_inner.refs_1_, f32[8,16,1024]{2,1,0:T(8,128)S(1)} %copy-done, ...), custom_call_target="tpu_custom_call" | custom-call | flops 7864320 | bytes 983040 | tf_op jit(solution)/shard_map/last_inner/pallas_call | solution.py:569
  47.8 0.8 %store_p.1.refs_15_ = f32[2,8,16,1024]{3,2,1,0:T(8,128)} custom-call(f32[2,4,16,1024]{3,2,1,0:T(8,128)S(1)} %get-tuple-element.72.inner), custom_call_target="tpu_custom_call" | custom-call | flops 491520 | bytes 61440 | tf_op jit(solution)/shard_map/store_p/pallas_call | solution.py:572
  48.7 1.0 %store_q.1 = (f32[2,8,16,1024]{3,2,1,0:T(8,128)}, f32[8,128]{1,0:T(8,128)S(1)}) custom-call(f32[2,4,16,1024]{3,2,1,0:T(8,128)S(1)} %get-tuple-element.60.rim.q_rim.refs_0_, f32[2,4,16,1024]{3,2,1,0:T(8,128)S(1)} %get-tuple-element.61.inner.q_inner.refs_1_), custom_call_target="tpu_custom_call" | custom-call | flops 983040 | bytes 122880 | tf_op jit(solution)/shard_map/store_q/pallas_call | solution.py:566
  49.7 0.4 collective-permute-done.9.refs_2_
  50.2 4.5 %collective-permute-done.10.refs_3_ = f32[4,16,1024]{2,1,0:T(8,128)S(1)} collective-permute-done((f32[4,16,1024]{2,1,0:T(8,128)S(1)}, f32[4,16,1024]{2,1,0:T(8,128)S(1)}, u32[]{:S(2)}, u32[]{:S(2)}) %collective-permute-start.10) | collective-permute-done | bytes 262176 | tf_op jit(solution)/shard_map/ppermute | solution.py:511
  54.6 2.0 %last_rim.1 = (f32[2,8,16,1024]{3,2,1,0:T(8,128)}, f32[32,8,128]{2,1,0:T(8,128)S(1)}) custom-call(f32[2,4,16,1024]{3,2,1,0:T(8,128)S(1)} %get-tuple-element.60.rim.q_rim.refs_0_, f32[2,4,16,1024]{3,2,1,0:T(8,128)S(1)} %get-tuple-element.61.inner.q_inner.refs_1_, f32[4,16,1024]{2,1,0:T(8,128)S(1)} %collective-permute-done.9.refs_2_, ...), custom_call_target="tpu_custom_call", output_to_operand_aliasing={{0}: (15, {})} | custom-call | flops 7864320 | bytes 983040 | tf_op jit(solution)/shard_map/last_rim/pallas_call | solution.py:583
  56.7 13.9 %all_to_all.5 = f32[32,8,128]{2,1,0:T(8,128)S(1)} all-to-all(f32[32,8,128]{2,1,0:T(8,128)S(1)} %get-tuple-element.74), channel_id=1, replica_groups=mesh['chain'=4,'gx'=32] {'gx'}, dimensions={0} | all-to-all | bytes 262144 | tf_op jit(solution)/shard_map/all_to_all | solution.py:587
  70.5 0.6 slice_reduce_fusion
  (21 shorter events, 0.9 us)
Async XLA Ops:
  2.0 7.7 %collective-permute-start.2 = (f32[4,2,16,1024]{3,2,1,0:T(8,128)S(1)}, f32[4,2,16,1024]{3,2,1,0:T(8,128)S(1)}, u32[]{:S(2)}, u32[]{:S(2)}) collective-permute-start(f32[4,2,16,1024]{3,2,1,0:T(8,128)S(1)} %get-tuple-element.46), channel_id=1, source_target_pairs={{0,32},{32,0},{64,96},{96,64},{1,33},{33,1},{65,97},{97,65},{2,34}... | collective-permute-start | bytes 1572872 | tf_op jit(solution)/shard_map/ppermute | solution.py:520
  2.1 24.2 %collective-permute-start = (f32[6,16,1024]{2,1,0:T(8,128)S(1)}, f32[6,16,1024]{2,1,0:T(8,128)S(1)}, u32[]{:S(2)}, u32[]{:S(2)}) collective-permute-start(f32[6,16,1024]{2,1,0:T(8,128)S(1)} %get-tuple-element.40), channel_id=1, source_target_pairs={{0,1},{1,0},{2,3},{3,2},{4,5},{5,4},{6,7},{7,6},{8,9},{9,8},{10,11... | collective-permute-start | bytes 1179656 | tf_op jit(solution)/shard_map/ppermute | solution.py:511
  3.8 22.6 %collective-permute-start.1 = (f32[6,16,1024]{2,1,0:T(8,128)S(1)}, f32[6,16,1024]{2,1,0:T(8,128)S(1)}, u32[]{:S(2)}, u32[]{:S(2)}) collective-permute-start(f32[6,16,1024]{2,1,0:T(8,128)S(1)} %get-tuple-element.41), channel_id=1, source_target_pairs={{0,31},{1,2},{2,1},{3,4},{4,3},{5,6},{6,5},{7,8},{8,7},{9,10},{10,... | collective-permute-start | bytes 1179656 | tf_op jit(solution)/shard_map/ppermute | solution.py:511
  9.7 3.8 %copy-start = (f32[8,16,1024]{2,1,0:T(8,128)S(1)}, f32[8,16,1024]{2,1,0:T(8,128)}, u32[]{:S(2)}) copy-start(f32[8,16,1024]{2,1,0:T(8,128)} %refs_4_.1) | copy-start | bytes 1572868
  9.7 3.8 %copy-start.1 = (f32[8,16,1024]{2,1,0:T(8,128)S(1)}, f32[8,16,1024]{2,1,0:T(8,128)}, u32[]{:S(2)}) copy-start(f32[8,16,1024]{2,1,0:T(8,128)} %refs_5_.1) | copy-start | bytes 1572868
  9.7 16.5 %collective-permute-start.3 = (f32[2,2,16,1024]{3,2,1,0:T(8,128)S(1)}, f32[2,2,16,1024]{3,2,1,0:T(8,128)S(1)}, u32[]{:S(2)}, u32[]{:S(2)}) collective-permute-start(f32[2,2,16,1024]{3,2,1,0:T(8,128)S(1)} %mass_rim_add.1.refs_0_), channel_id=1, source_target_pairs={{0,64},{32,96},{64,0},{96,32},{1,65},{33,97},{65,1},{97,33},{2,66}... | collective-permute-start | bytes 786440 | tf_op jit(solution)/shard_map/ppermute | solution.py:530
  13.4 18.4 %collective-permute-start.5 = (f32[2,2,16,1024]{3,2,1,0:T(8,128)S(1)}, f32[2,2,16,1024]{3,2,1,0:T(8,128)S(1)}, u32[]{:S(2)}, u32[]{:S(2)}) collective-permute-start(f32[2,2,16,1024]{3,2,1,0:T(8,128)S(1)} %mass_inner_add.1.refs_0_), channel_id=1, source_target_pairs={{0,64},{32,96},{64,0},{96,32},{1,65},{33,97},{65,1},{97,33},{2,66}... | collective-permute-start | bytes 786440 | tf_op jit(solution)/shard_map/ppermute | solution.py:530
  26.2 1.4 %collective-permute-start.4 = (f32[2,16,1024]{2,1,0:T(8,128)S(1)}, f32[2,16,1024]{2,1,0:T(8,128)S(1)}, u32[]{:S(2)}, u32[]{:S(2)}) collective-permute-start(f32[2,16,1024]{2,1,0:T(8,128)S(1)} %mass_rim.1.mine), channel_id=1, source_target_pairs={{0,32},{32,0},{64,96},{96,64},{1,33},{33,1},{65,97},{97,65},{2,34}... | collective-permute-start | bytes 393224 | tf_op jit(solution)/shard_map/ppermute | solution.py:532
  26.4 1.3 %copy-start.2 = (f32[2,8,16,1024]{3,2,1,0:T(8,128)S(1)}, f32[2,8,16,1024]{3,2,1,0:T(8,128)}, u32[]{:S(2)}) copy-start(f32[2,8,16,1024]{3,2,1,0:T(8,128)} %draw.3) | copy-start | bytes 3145732
  28.0 8.7 %collective-permute-start.7 = (f32[4,16,1024]{2,1,0:T(8,128)S(1)}, f32[4,16,1024]{2,1,0:T(8,128)S(1)}, u32[]{:S(2)}, u32[]{:S(2)}) collective-permute-start(f32[4,16,1024]{2,1,0:T(8,128)S(1)} %get-tuple-element.51), channel_id=1, source_target_pairs={{0,1},{1,0},{2,3},{3,2},{4,5},{5,4},{6,7},{7,6},{8,9},{9,8},{10,11... | collective-permute-start | bytes 786440 | tf_op jit(solution)/shard_map/ppermute | solution.py:511
  28.1 12.9 %collective-permute-start.8 = (f32[4,16,1024]{2,1,0:T(8,128)S(1)}, f32[4,16,1024]{2,1,0:T(8,128)S(1)}, u32[]{:S(2)}, u32[]{:S(2)}) collective-permute-start(f32[4,16,1024]{2,1,0:T(8,128)S(1)} %get-tuple-element.52), channel_id=1, source_target_pairs={{0,31},{1,2},{2,1},{3,4},{4,3},{5,6},{6,5},{7,8},{8,7},{9,10},{10,... | collective-permute-start | bytes 786440 | tf_op jit(solution)/shard_map/ppermute | solution.py:511
  31.9 1.4 %collective-permute-start.6 = (f32[2,16,1024]{2,1,0:T(8,128)S(1)}, f32[2,16,1024]{2,1,0:T(8,128)S(1)}, u32[]{:S(2)}, u32[]{:S(2)}) collective-permute-start(f32[2,16,1024]{2,1,0:T(8,128)S(1)} %mass_inner.1.mine), channel_id=1, source_target_pairs={{0,32},{32,0},{64,96},{96,64},{1,33},{33,1},{65,97},{97,65},{2,34}... | collective-permute-start | bytes 393224 | tf_op jit(solution)/shard_map/ppermute | solution.py:532
  42.3 7.8 %collective-permute-start.9 = (f32[4,16,1024]{2,1,0:T(8,128)S(1)}, f32[4,16,1024]{2,1,0:T(8,128)S(1)}, u32[]{:S(2)}, u32[]{:S(2)}) collective-permute-start(f32[4,16,1024]{2,1,0:T(8,128)S(1)} %get-tuple-element.63), channel_id=1, source_target_pairs={{0,1},{1,0},{2,3},{3,2},{4,5},{5,4},{6,7},{7,6},{8,9},{9,8},{10,11... | collective-permute-start | bytes 786440 | tf_op jit(solution)/shard_map/ppermute | solution.py:511
  42.4 12.3 %collective-permute-start.10 = (f32[4,16,1024]{2,1,0:T(8,128)S(1)}, f32[4,16,1024]{2,1,0:T(8,128)S(1)}, u32[]{:S(2)}, u32[]{:S(2)}) collective-permute-start(f32[4,16,1024]{2,1,0:T(8,128)S(1)} %get-tuple-element.64), channel_id=1, source_target_pairs={{0,31},{1,2},{2,1},{3,4},{4,3},{5,6},{6,5},{7,8},{8,7},{9,10},{10,... | collective-permute-start | bytes 786440 | tf_op jit(solution)/shard_map/ppermute | solution.py:511

commit v6 on v5

--- a/solution.py
+++ b/solution.py
@@ -142,7 +142,7 @@
 
 
 def parity():
-    return lax.rem(lax.axis_index("gx"), 2)
+    return 1 - lax.rem(lax.axis_index("gx"), 2)
 
 
 def place_halo(halo, from_a, from_b):
@@ -469,14 +469,13 @@
         scaled, deep, rim_scaled, scaled_deep, use,
         lambda chain, high: copies[2 * chain + high].start(),
     )
-    sub = lax.broadcasted_iota(jnp.int32, (8, LANES), 0)
-    lane = lax.broadcasted_iota(jnp.int32, (8, LANES), 1)
-    mark = jnp.zeros((8, LANES), jnp.float32)
+    lane = lax.broadcasted_iota(jnp.int32, (1, LANES), 1)
+    mark = jnp.zeros((1, LANES), jnp.float32)
     for chain in range(chains):
         end = energy[chain] + fold((0.5 * inv_noise) * misfits[chain] + totals[chain])
         start = potential[chain] + kinetic[chain]
         for row, tile in enumerate((start, end)):
-            mark = jnp.where((sub == row) & (lane == chain), jnp.sum(tile) / cells, mark)
+            mark = jnp.where(lane == row * chains + chain, jnp.sum(tile) / cells, mark)
     for i in range(rows.shape[0]):
         rows[i] = mark
     for copy in copies:
@@ -489,8 +488,8 @@
     cells = planes * slabs * depth * across
     near = [(i, i ^ 1) for i in range(groups)]
     far = [(i, i ^ 2) for i in range(groups)]
-    pair_a = [(i, i ^ 1) for i in range(slabs)]
-    pair_b = [(i, (i + 1 if i % 2 else i - 1) % slabs) for i in range(slabs)]
+    pair_a = [(i, (i + 1 if i % 2 else i - 1) % slabs) for i in range(slabs)]
+    pair_b = [(i, i ^ 1) for i in range(slabs)]
     half = planes // 2
     plane = (depth, across)
     rest = planes - 2 * WIDE
@@ -535,10 +534,10 @@
         first_inner_kernel, [scaled_shape, inner_block, tile], inner_scratch, "first_inner", work
     )(position, viscosity, observed)
     mine, other = mass_of(WIDE, True, (), (potential,), "mass_rim")
-    inner_mine, inner_other = mass_of(half - WIDE, False, (), (), "mass_inner")
     slope, nu_halo, obs_halo, potential = call(
         first_rim_kernel, [rim_block, sides, sides, tile], rim_scratch, "first_rim", work
     )(position, from_a, from_b, viscosity, observed, scaled, potential)
+    inner_mine, inner_other = mass_of(half - WIDE, False, (slope,), (), "mass_inner")
     rim_q, rim_p, rim_mass, kinetic, to_a, to_b = call(
         launch_rim_kernel,
         [rim_block, rim_block, (2 * WIDE, *plane), tile, edge, edge],
@@ -581,11 +580,11 @@
         scaled, energy, potential, kinetic, stored, partial_p,
     )
     p, rows = call(
-        last_body, [block, (slabs, 8, LANES)], [*rim_scratch, rim_block, copy_sems], "last_rim", work,
+        last_body, [block, (slabs, 1, LANES)], [*rim_scratch, rim_block, copy_sems], "last_rim", work,
         [VECTOR] * (len(operands) - 1) + [MEMORY], [MEMORY, VECTOR], {len(operands) - 1: 0},
     )(*operands)
     rows = lax.all_to_all(rows, "gx", 0, 0, tiled=True)
-    energies = jnp.sum(rows[:, :2, :chains], axis=0)
+    energies = jnp.sum(rows[:, 0, : 2 * chains].reshape(slabs, 2, chains), axis=0)
     return (q, p, energies)
 
 

time: 71.3 us -> 69.3 us (0.972)
  waiting for transfers between devices: 23.6 us -> 18.2 us
  starting transfers between devices: 19.5 us -> 22.8 us
    ppermute x2, waiting for transfers between devices: 11.2 us -> 0.01 us  [mass_of(): remote = lax.ppermute(part, 'chain', far)]
    ppermute x6, waiting for transfers between devices: 11 us -> 15.6 us  [swap(): return (lax.ppermute(to_a, 'gx', pair_a), lax.ppermute(to_b, 'gx', pair_b))]
    ppermute x2, starting transfers between devices: 3.77 us -> 7.33 us  [mass_of(): remote = lax.ppermute(part, 'chain', far)]
    ppermute x2, waiting for transfers between devices: 1.38 us -> 2.62 us  [mass_of(): return (mine, lax.ppermute(mine, 'chain', near))]
  transfers between devices with their start and end apart: 11 -> 11, of which waited for: 7 -> 6; matrix products, arithmetic and copies ran while one was open for 0% -> 0% of each run, Pallas kernels for 11% -> 12%
where the time goes in v6:
time: 69.3 us; the launch traced here: 69.1 us
  starting transfers between devices  22.8 us (33%)
  waiting for transfers between devices  18.2 us (26%)
  blocking collectives  13.9 us (20%)
  Pallas kernels  12.8 us (18%)
  between operations  0.76 us (1%)
    ppermute x6, waiting for transfers between devices, swap(): return (lax.ppermute(to_a, 'gx', pair_a), lax.ppermute(to_b, 'gx', pair_b))  15.6 us
    ppermute x6, starting transfers between devices, swap(): return (lax.ppermute(to_a, 'gx', pair_a), lax.ppermute(to_b, 'gx', pair_b))  15.1 us
    all_to_all x1, blocking collectives, local(): rows = lax.all_to_all(rows, 'gx', 0, 0, tiled=True)  13.9 us
    ppermute x2, starting transfers between devices, mass_of(): remote = lax.ppermute(part, 'chain', far)  7.33 us
    ppermute x2, waiting for transfers between devices, mass_of(): return (mine, lax.ppermute(mine, 'chain', near))  2.62 us
    pallas_call x1, Pallas kernels, local(): call(last_body, [block, (slabs, 1, LANES)], [*rim_scratch, rim_block, cop...  2.03 us
    pallas_call x1, Pallas kernels, local(): call(last_inner_kernel, [scaled_shape, inner_block, tile], inner_scratch,...  1.52 us
    pallas_call x1, Pallas kernels, local(): call(first_inner_kernel, [scaled_shape, inner_block, tile], inner_scratch...  1.45 us
  transfers between devices with their start and end apart: 11, of which 6 were waited for; matrix products, arithmetic and copies ran while one was open for 0% of the time, Pallas kernels for 12%

profile of v6, /device:TPU:0, one launch (start us, length us, event | category | flops | bytes accessed | tf_op | source)
XLA Modules:
  0.0 69.1 jit_solution(16722911802272894544)
XLA Ops:
  0.6 1.4 %entry.1 = (f32[2,8,16,1024]{3,2,1,0:T(8,128)S(1)}, f32[4,2,16,1024]{3,2,1,0:T(8,128)S(1)}, f32[4,2,16,1024]{3,2,1,0:T(8,128)S(1)}, f32[6,16,1024]{2,1,0:T(8,128)S(1)}, f32[6,16,1024]{2,1,0:T(8,128)S(1)}) custom-call(f32[2,8,16,1024]{3,2,1,0:T(8,128)} %q.1, f32[8,16,1024]{2,1,0:T(8,128)} %refs_4_.1, f32[8,16,1024]{2,1,0:T(8,128)} %refs_5_.1), custom_call_target="tpu_custom_call" | custom-call | flops 491520 | bytes 61440 | tf_op jit(solution)/shard_map/entry/pallas_call | solution.py:514
  2.1 6.7 %collective-permute-start = (f32[6,16,1024]{2,1,0:T(8,128)S(1)}, f32[6,16,1024]{2,1,0:T(8,128)S(1)}, u32[]{:S(2)}, u32[]{:S(2)}) collective-permute-start(f32[6,16,1024]{2,1,0:T(8,128)S(1)} %get-tuple-element.40), channel_id=1, source_target_pairs={{0,31},{1,2},{2,1},{3,4},{4,3},{5,6},{6,5},{7,8},{8,7},{9,10},{10,... | collective-permute-start | bytes 1179656 | tf_op jit(solution)/shard_map/ppermute | solution.py:510
  8.9 3.7 %collective-permute-start.3 = (f32[2,2,16,1024]{3,2,1,0:T(8,128)S(1)}, f32[2,2,16,1024]{3,2,1,0:T(8,128)S(1)}, u32[]{:S(2)}, u32[]{:S(2)}) collective-permute-start(f32[2,2,16,1024]{3,2,1,0:T(8,128)S(1)} %mass_rim_add.1.refs_0_), channel_id=1, source_target_pairs={{0,64},{32,96},{64,0},{96,32},{1,65},{33,97},{65,1},{97,33},{2,66}... | collective-permute-start | bytes 786440 | tf_op jit(solution)/shard_map/ppermute | solution.py:529
  12.6 1.4 %first_inner.1 = (f32[2,6,16,1024]{3,2,1,0:T(8,128)S(1)}, f32[2,4,16,1024]{3,2,1,0:T(8,128)S(1)}, f32[2,8,128]{2,1,0:T(8,128)S(1)}) custom-call(f32[2,8,16,1024]{3,2,1,0:T(8,128)S(1)} %get-tuple-element.39.q, f32[8,16,1024]{2,1,0:T(8,128)S(1)} %copy-done, f32[8,16,1024]{2,1,0:T(8,128)S(1)} %copy-done.1), custom_call_target="tpu_custom_call" | custom-call | flops 7864320 | bytes 983040 | tf_op jit(solution)/shard_map/first_inner/pallas_call | solution.py:533
  14.0 4.6 %collective-permute-done.from_a = f32[6,16,1024]{2,1,0:T(8,128)S(1)} collective-permute-done((f32[6,16,1024]{2,1,0:T(8,128)S(1)}, f32[6,16,1024]{2,1,0:T(8,128)S(1)}, u32[]{:S(2)}, u32[]{:S(2)}) %collective-permute-start) | collective-permute-done | bytes 393248 | tf_op jit(solution)/shard_map/ppermute | solution.py:510
  18.6 1.4 %collective-permute-done.1.from_b = f32[6,16,1024]{2,1,0:T(8,128)S(1)} collective-permute-done((f32[6,16,1024]{2,1,0:T(8,128)S(1)}, f32[6,16,1024]{2,1,0:T(8,128)S(1)}, u32[]{:S(2)}, u32[]{:S(2)}) %collective-permute-start.1) | collective-permute-done | bytes 393248 | tf_op jit(solution)/shard_map/ppermute | solution.py:510
  20.0 1.2 %first_rim.1 = (f32[2,4,16,1024]{3,2,1,0:T(8,128)S(1)}, f32[2,16,1024]{2,1,0:T(8,128)S(1)}, f32[2,16,1024]{2,1,0:T(8,128)S(1)}, f32[2,8,128]{2,1,0:T(8,128)S(1)}) custom-call(f32[2,8,16,1024]{3,2,1,0:T(8,128)S(1)} %get-tuple-element.39.q, f32[6,16,1024]{2,1,0:T(8,128)S(1)} %collective-permute-done.from_a, f32[6,16,1024]{2,1,0:T(8,128)S(1)} %collective-permute-done.1.from_b, ...), custom_call_target="tpu_custom_call" | custom-call | flops 7864320 | bytes 983040 | tf_op jit(solution)/shard_map/first_rim/pallas_call | solution.py:537
  21.3 3.7 %collective-permute-start.5 = (f32[2,2,16,1024]{3,2,1,0:T(8,128)S(1)}, f32[2,2,16,1024]{3,2,1,0:T(8,128)S(1)}, u32[]{:S(2)}, u32[]{:S(2)}) collective-permute-start(f32[2,2,16,1024]{3,2,1,0:T(8,128)S(1)} %mass_inner_add.1.refs_0_), channel_id=1, source_target_pairs={{0,64},{32,96},{64,0},{96,32},{1,65},{33,97},{65,1},{97,33},{2,66}... | collective-permute-start | bytes 786440 | tf_op jit(solution)/shard_map/ppermute | solution.py:529
  25.1 1.3 %collective-permute-done.4.other = f32[2,16,1024]{2,1,0:T(8,128)S(1)} collective-permute-done((f32[2,16,1024]{2,1,0:T(8,128)S(1)}, f32[2,16,1024]{2,1,0:T(8,128)S(1)}, u32[]{:S(2)}, u32[]{:S(2)}) %collective-permute-start.4) | collective-permute-done | bytes 131104 | tf_op jit(solution)/shard_map/ppermute | solution.py:531
  26.4 0.3 launch_rim.1
  26.7 4.2 %collective-permute-start.7 = (f32[4,16,1024]{2,1,0:T(8,128)S(1)}, f32[4,16,1024]{2,1,0:T(8,128)S(1)}, u32[]{:S(2)}, u32[]{:S(2)}) collective-permute-start(f32[4,16,1024]{2,1,0:T(8,128)S(1)} %get-tuple-element.51), channel_id=1, source_target_pairs={{0,31},{1,2},{2,1},{3,4},{4,3},{5,6},{6,5},{7,8},{8,7},{9,10},{10,... | collective-permute-start | bytes 786440 | tf_op jit(solution)/shard_map/ppermute | solution.py:510
  31.0 1.3 %collective-permute-done.6.other = f32[2,16,1024]{2,1,0:T(8,128)S(1)} collective-permute-done((f32[2,16,1024]{2,1,0:T(8,128)S(1)}, f32[2,16,1024]{2,1,0:T(8,128)S(1)}, u32[]{:S(2)}, u32[]{:S(2)}) %collective-permute-start.6) | collective-permute-done | bytes 131104 | tf_op jit(solution)/shard_map/ppermute | solution.py:531
  32.4 0.3 launch_inner.1
  32.6 1.3 %leap_inner.1 = (f32[2,6,16,1024]{3,2,1,0:T(8,128)S(1)}, f32[2,4,16,1024]{3,2,1,0:T(8,128)S(1)}, f32[2,4,16,1024]{3,2,1,0:T(8,128)S(1)}) custom-call(f32[2,4,16,1024]{3,2,1,0:T(8,128)S(1)} %get-tuple-element.47.q_rim, f32[2,4,16,1024]{3,2,1,0:T(8,128)S(1)} %get-tuple-element.50.q_inner, f32[8,16,1024]{2,1,0:T(8,128)S(1)} %copy-done, ...), custom_call_target="tpu_custom_call" | custom-call | flops 7864320 | bytes 983040 | tf_op jit(solution)/shard_map/leap_inner/pallas_call | solution.py:554
  34.0 5.4 %collective-permute-done.7.from_a = f32[4,16,1024]{2,1,0:T(8,128)S(1)} collective-permute-done((f32[4,16,1024]{2,1,0:T(8,128)S(1)}, f32[4,16,1024]{2,1,0:T(8,128)S(1)}, u32[]{:S(2)}, u32[]{:S(2)}) %collective-permute-start.7) | collective-permute-done | bytes 262176 | tf_op jit(solution)/shard_map/ppermute | solution.py:510
  39.4 1.3 %leap_rim.1 = (f32[2,4,16,1024]{3,2,1,0:T(8,128)S(1)}, f32[2,4,16,1024]{3,2,1,0:T(8,128)S(1)}, f32[4,16,1024]{2,1,0:T(8,128)S(1)}, f32[4,16,1024]{2,1,0:T(8,128)S(1)}) custom-call(f32[2,4,16,1024]{3,2,1,0:T(8,128)S(1)} %get-tuple-element.47.q_rim, f32[2,4,16,1024]{3,2,1,0:T(8,128)S(1)} %get-tuple-element.50.q_inner, ...), custom_call_target="tpu_custom_call" | custom-call | flops 7864320 | bytes 983040 | tf_op jit(solution)/shard_map/leap_rim/pallas_call | solution.py:557
  40.7 4.2 %collective-permute-start.9 = (f32[4,16,1024]{2,1,0:T(8,128)S(1)}, f32[4,16,1024]{2,1,0:T(8,128)S(1)}, u32[]{:S(2)}, u32[]{:S(2)}) collective-permute-start(f32[4,16,1024]{2,1,0:T(8,128)S(1)} %get-tuple-element.63), channel_id=1, source_target_pairs={{0,31},{1,2},{2,1},{3,4},{4,3},{5,6},{6,5},{7,8},{8,7},{9,10},{10,... | collective-permute-start | bytes 786440 | tf_op jit(solution)/shard_map/ppermute | solution.py:510
  44.9 1.5 %last_inner.1 = (f32[2,6,16,1024]{3,2,1,0:T(8,128)S(1)}, f32[2,4,16,1024]{3,2,1,0:T(8,128)S(1)}, f32[2,8,128]{2,1,0:T(8,128)S(1)}) custom-call(f32[2,4,16,1024]{3,2,1,0:T(8,128)S(1)} %get-tuple-element.60.rim.q_rim.refs_0_, f32[2,4,16,1024]{3,2,1,0:T(8,128)S(1)} %get-tuple-element.61.inner.q_inner.refs_1_, f32[8,16,1024]{2,1,0:T(8,128)S(1)} %copy-done, ...), custom_call_target="tpu_custom_call" | custom-call | flops 7864320 | bytes 983040 | tf_op jit(solution)/shard_map/last_inner/pallas_call | solution.py:568
  46.4 0.8 %store_p.1.refs_15_ = f32[2,8,16,1024]{3,2,1,0:T(8,128)} custom-call(f32[2,4,16,1024]{3,2,1,0:T(8,128)S(1)} %get-tuple-element.72.inner), custom_call_target="tpu_custom_call" | custom-call | flops 491520 | bytes 61440 | tf_op jit(solution)/shard_map/store_p/pallas_call | solution.py:571
  47.3 1.0 %store_q.1 = (f32[2,8,16,1024]{3,2,1,0:T(8,128)}, f32[8,128]{1,0:T(8,128)S(1)}) custom-call(f32[2,4,16,1024]{3,2,1,0:T(8,128)S(1)} %get-tuple-element.60.rim.q_rim.refs_0_, f32[2,4,16,1024]{3,2,1,0:T(8,128)S(1)} %get-tuple-element.61.inner.q_inner.refs_1_), custom_call_target="tpu_custom_call" | custom-call | flops 983040 | bytes 122880 | tf_op jit(solution)/shard_map/store_q/pallas_call | solution.py:565
  48.3 4.2 %collective-permute-done.9.refs_2_ = f32[4,16,1024]{2,1,0:T(8,128)S(1)} collective-permute-done((f32[4,16,1024]{2,1,0:T(8,128)S(1)}, f32[4,16,1024]{2,1,0:T(8,128)S(1)}, u32[]{:S(2)}, u32[]{:S(2)}) %collective-permute-start.9) | collective-permute-done | bytes 262176 | tf_op jit(solution)/shard_map/ppermute | solution.py:510
  52.5 2.0 %last_rim.1 = (f32[2,8,16,1024]{3,2,1,0:T(8,128)}, f32[32,1,128]{2,1,0:T(1,128)S(1)}) custom-call(f32[2,4,16,1024]{3,2,1,0:T(8,128)S(1)} %get-tuple-element.60.rim.q_rim.refs_0_, f32[2,4,16,1024]{3,2,1,0:T(8,128)S(1)} %get-tuple-element.61.inner.q_inner.refs_1_, f32[4,16,1024]{2,1,0:T(8,128)S(1)} %collective-permute-done.9.refs_2_, ...), custom_call_target="tpu_custom_call", output_to_operand_aliasing={{0}: (15, {})} | custom-call | flops 7864320 | bytes 983040 | tf_op jit(solution)/shard_map/last_rim/pallas_call | solution.py:582
  54.6 13.9 %all_to_all.5 = f32[32,1,128]{2,1,0:T(1,128)S(1)} all-to-all(f32[32,1,128]{2,1,0:T(1,128)S(1)} %get-tuple-element.74), channel_id=1, replica_groups=mesh['chain'=4,'gx'=32] {'gx'}, dimensions={0} | all-to-all | bytes 32768 | tf_op jit(solution)/shard_map/all_to_all | solution.py:586
  68.5 0.6 reduce_sum.12
  (22 shorter events, 0.6 us)
Async XLA Ops:
  2.0 6.8 %collective-permute-start.2 = (f32[4,2,16,1024]{3,2,1,0:T(8,128)S(1)}, f32[4,2,16,1024]{3,2,1,0:T(8,128)S(1)}, u32[]{:S(2)}, u32[]{:S(2)}) collective-permute-start(f32[4,2,16,1024]{3,2,1,0:T(8,128)S(1)} %get-tuple-element.46), channel_id=1, source_target_pairs={{0,32},{32,0},{64,96},{96,64},{1,33},{33,1},{65,97},{97,65},{2,34}... | collective-permute-start | bytes 1572872 | tf_op jit(solution)/shard_map/ppermute | solution.py:519
  2.1 16.5 %collective-permute-start = (f32[6,16,1024]{2,1,0:T(8,128)S(1)}, f32[6,16,1024]{2,1,0:T(8,128)S(1)}, u32[]{:S(2)}, u32[]{:S(2)}) collective-permute-start(f32[6,16,1024]{2,1,0:T(8,128)S(1)} %get-tuple-element.40), channel_id=1, source_target_pairs={{0,31},{1,2},{2,1},{3,4},{4,3},{5,6},{6,5},{7,8},{8,7},{9,10},{10,... | collective-permute-start | bytes 1179656 | tf_op jit(solution)/shard_map/ppermute | solution.py:510
  8.8 11.2 %collective-permute-start.1 = (f32[6,16,1024]{2,1,0:T(8,128)S(1)}, f32[6,16,1024]{2,1,0:T(8,128)S(1)}, u32[]{:S(2)}, u32[]{:S(2)}) collective-permute-start(f32[6,16,1024]{2,1,0:T(8,128)S(1)} %get-tuple-element.41), channel_id=1, source_target_pairs={{0,1},{1,0},{2,3},{3,2},{4,5},{5,4},{6,7},{7,6},{8,9},{9,8},{10,11... | collective-permute-start | bytes 1179656 | tf_op jit(solution)/shard_map/ppermute | solution.py:510
  8.8 3.7 %copy-start = (f32[8,16,1024]{2,1,0:T(8,128)S(1)}, f32[8,16,1024]{2,1,0:T(8,128)}, u32[]{:S(2)}) copy-start(f32[8,16,1024]{2,1,0:T(8,128)} %refs_4_.1) | copy-start | bytes 1572868
  8.8 3.7 %copy-start.1 = (f32[8,16,1024]{2,1,0:T(8,128)S(1)}, f32[8,16,1024]{2,1,0:T(8,128)}, u32[]{:S(2)}) copy-start(f32[8,16,1024]{2,1,0:T(8,128)} %refs_5_.1) | copy-start | bytes 1572868
  8.9 16.0 %collective-permute-start.3 = (f32[2,2,16,1024]{3,2,1,0:T(8,128)S(1)}, f32[2,2,16,1024]{3,2,1,0:T(8,128)S(1)}, u32[]{:S(2)}, u32[]{:S(2)}) collective-permute-start(f32[2,2,16,1024]{3,2,1,0:T(8,128)S(1)} %mass_rim_add.1.refs_0_), channel_id=1, source_target_pairs={{0,64},{32,96},{64,0},{96,32},{1,65},{33,97},{65,1},{97,33},{2,66}... | collective-permute-start | bytes 786440 | tf_op jit(solution)/shard_map/ppermute | solution.py:529
  21.2 5.2 %copy-start.2 = (f32[2,8,16,1024]{3,2,1,0:T(8,128)S(1)}, f32[2,8,16,1024]{3,2,1,0:T(8,128)}, u32[]{:S(2)}) copy-start(f32[2,8,16,1024]{3,2,1,0:T(8,128)} %draw.3) | copy-start | bytes 3145732
  21.3 9.7 %collective-permute-start.5 = (f32[2,2,16,1024]{3,2,1,0:T(8,128)S(1)}, f32[2,2,16,1024]{3,2,1,0:T(8,128)S(1)}, u32[]{:S(2)}, u32[]{:S(2)}) collective-permute-start(f32[2,2,16,1024]{3,2,1,0:T(8,128)S(1)} %mass_inner_add.1.refs_0_), channel_id=1, source_target_pairs={{0,64},{32,96},{64,0},{96,32},{1,65},{33,97},{65,1},{97,33},{2,66}... | collective-permute-start | bytes 786440 | tf_op jit(solution)/shard_map/ppermute | solution.py:529
  25.0 1.4 %collective-permute-start.4 = (f32[2,16,1024]{2,1,0:T(8,128)S(1)}, f32[2,16,1024]{2,1,0:T(8,128)S(1)}, u32[]{:S(2)}, u32[]{:S(2)}) collective-permute-start(f32[2,16,1024]{2,1,0:T(8,128)S(1)} %mass_rim.1.mine), channel_id=1, source_target_pairs={{0,32},{32,0},{64,96},{96,64},{1,33},{33,1},{65,97},{97,65},{2,34}... | collective-permute-start | bytes 393224 | tf_op jit(solution)/shard_map/ppermute | solution.py:531
  26.7 12.7 %collective-permute-start.7 = (f32[4,16,1024]{2,1,0:T(8,128)S(1)}, f32[4,16,1024]{2,1,0:T(8,128)S(1)}, u32[]{:S(2)}, u32[]{:S(2)}) collective-permute-start(f32[4,16,1024]{2,1,0:T(8,128)S(1)} %get-tuple-element.51), channel_id=1, source_target_pairs={{0,31},{1,2},{2,1},{3,4},{4,3},{5,6},{6,5},{7,8},{8,7},{9,10},{10,... | collective-permute-start | bytes 786440 | tf_op jit(solution)/shard_map/ppermute | solution.py:510
  30.9 8.5 %collective-permute-start.8 = (f32[4,16,1024]{2,1,0:T(8,128)S(1)}, f32[4,16,1024]{2,1,0:T(8,128)S(1)}, u32[]{:S(2)}, u32[]{:S(2)}) collective-permute-start(f32[4,16,1024]{2,1,0:T(8,128)S(1)} %get-tuple-element.52), channel_id=1, source_target_pairs={{0,1},{1,0},{2,3},{3,2},{4,5},{5,4},{6,7},{7,6},{8,9},{9,8},{10,11... | collective-permute-start | bytes 786440 | tf_op jit(solution)/shard_map/ppermute | solution.py:510
  31.0 1.4 %collective-permute-start.6 = (f32[2,16,1024]{2,1,0:T(8,128)S(1)}, f32[2,16,1024]{2,1,0:T(8,128)S(1)}, u32[]{:S(2)}, u32[]{:S(2)}) collective-permute-start(f32[2,16,1024]{2,1,0:T(8,128)S(1)} %mass_inner.1.mine), channel_id=1, source_target_pairs={{0,32},{32,0},{64,96},{96,64},{1,33},{33,1},{65,97},{97,65},{2,34}... | collective-permute-start | bytes 393224 | tf_op jit(solution)/shard_map/ppermute | solution.py:531
  40.7 11.8 %collective-permute-start.9 = (f32[4,16,1024]{2,1,0:T(8,128)S(1)}, f32[4,16,1024]{2,1,0:T(8,128)S(1)}, u32[]{:S(2)}, u32[]{:S(2)}) collective-permute-start(f32[4,16,1024]{2,1,0:T(8,128)S(1)} %get-tuple-element.63), channel_id=1, source_target_pairs={{0,31},{1,2},{2,1},{3,4},{4,3},{5,6},{6,5},{7,8},{8,7},{9,10},{10,... | collective-permute-start | bytes 786440 | tf_op jit(solution)/shard_map/ppermute | solution.py:510
  44.9 7.6 %collective-permute-start.10 = (f32[4,16,1024]{2,1,0:T(8,128)S(1)}, f32[4,16,1024]{2,1,0:T(8,128)S(1)}, u32[]{:S(2)}, u32[]{:S(2)}) collective-permute-start(f32[4,16,1024]{2,1,0:T(8,128)S(1)} %get-tuple-element.64), channel_id=1, source_target_pairs={{0,1},{1,0},{2,3},{3,2},{4,5},{5,4},{6,7},{7,6},{8,9},{9,8},{10,11... | collective-permute-start | bytes 786440 | tf_op jit(solution)/shard_map/ppermute | solution.py:510

commit v7 on v6

--- a/solution.py
+++ b/solution.py
@@ -50,13 +50,21 @@
     return below + above
 
 
+def present(views, cut):
+    value = None
+    for view in views:
+        if view is not None:
+            value = view[:, cut] if value is None else value + view[:, cut]
+    return value
+
+
 def stencil(planes, deeps):
-    cuts = tiles(planes[1].shape[-1])
+    cuts = tiles(planes[2].shape[-1])
     edge_terms, own_terms = [], []
     for cut in cuts:
-        v = planes[1][:, cut]
-        w = deeps[1][:, cut] + (planes[0][:, cut] + planes[2][:, cut])
-        corner = deeps[0][:, cut] + deeps[2][:, cut]
+        v = 0.0 if planes[1] is None else planes[1][:, cut]
+        w = present([deeps[1], planes[0], planes[2]], cut)
+        corner = present([deeps[0], deeps[2]], cut)
         t = 6.0 * v + (2.0 * w + corner)
         d = t + w
         edge_terms.append(t)
@@ -155,15 +163,15 @@
 
 
 def rims(
-    q_at, halo, nu, obs, nu_halo, obs_halo, scaled, deep, rim_scaled, scaled_deep, use, ready=None
+    q_at, halo, nu, obs, nu_halo, scaled, deep, rim_scaled, scaled_deep, use, ready=None
 ):
     chains, planes = scaled.shape[0], scaled.shape[1] + 2
 
     def at(chain, x):
         if x < 0:
-            return halo.at[0, chain, WIDE + x]
+            return halo.at[0, chain, 0]
         if x >= planes:
-            return halo.at[1, chain, x - planes]
+            return halo.at[1, chain, 0]
         return q_at(chain, x)
 
     def scaled_at(chain, x):
@@ -173,7 +181,7 @@
             return rim_scaled.at[chain, x - planes + 3]
         return scaled.at[chain, x - 1]
 
-    sides = ((-2, -1, 0, 1), (planes + 1, planes, planes - 1, planes - 2))
+    sides = ((-1, 0, 1), (planes, planes - 1, planes - 2))
     totals = []
     for chain in range(chains):
         for side in sides:
@@ -181,19 +189,22 @@
                 deepen(deep.at[chain, x + WIDE], at(chain, x))
     for chain in range(chains):
         total = 0.0
-        for s, side in enumerate(sides):
-            for x in side[1:3]:
-                outer = x == side[1]
-                near = range(x - 1, x + 2)
-                squares = weigh(
-                    [at(chain, i) for i in near],
-                    [deep.at[chain, i + WIDE] for i in near],
-                    nu_halo.at[s] if outer else nu.at[x],
-                    obs_halo.at[s] if outer else obs.at[x],
-                    scaled_at(chain, x),
-                    scaled_deep.at[chain, x + 1],
-                )
-                total = total if outer else total + squares
+        for s, (outer, x, _) in enumerate(sides):
+            view = [None, None, at(chain, x)]
+            for cut, k in stencil(view, [None, None, deep.at[chain, x + WIDE]]):
+                n = nu_halo[s, :, cut]
+                value = (unit * n * n) * k + halo[s, chain, 1, :, cut]
+                scaled_at(chain, outer)[:, cut] = value
+                scaled_deep[chain, outer + 1, :, cut] = depth_sum(value)
+            near = range(x - 1, x + 2)
+            total = total + weigh(
+                [at(chain, i) for i in near],
+                [deep.at[chain, i + WIDE] for i in near],
+                nu.at[x],
+                obs.at[x],
+                scaled_at(chain, x),
+                scaled_deep.at[chain, x + 1],
+            )
             for x in (1, 2) if s == 0 else (planes - 2, planes - 3):
                 deepen(scaled_deep.at[chain, x + 1], scaled_at(chain, x))
         totals.append(total)
@@ -209,27 +220,31 @@
     return totals
 
 
-def entry_kernel(q, nu, obs, own, keep, send, to_a, to_b, sems):
+def entry_kernel(q, nu, obs, own, keep, send, to_a, to_b, edges, deep, known, sems):
     core, odd = lax.rem(lax.axis_index("chain"), 2), parity()
     chains, planes = own.shape[:2]
     half = planes // 2
     load = [pltpu.make_async_copy(q.at[chain], own.at[chain], sems.at[chain]) for chain in range(chains)]
-    edges = []
-    for i, (source, at) in enumerate(((nu, chains * WIDE), (obs, chains * WIDE + 1))):
-        for k, (out, low) in enumerate(((to_a, odd), (to_b, 1 - odd))):
-            edges.append(
-                pltpu.make_async_copy(
-                    source.at[(1 - low) * (planes - 1)], out.at[at], sems.at[chains + 2 * i + k]
-                )
+    for i, source in enumerate((nu, obs)):
+        for side in range(2):
+            at = 2 * i + side
+            load.append(
+                pltpu.make_async_copy(source.at[side * (planes - 1)], edges.at[at], sems.at[chains + at])
             )
-    for copy in load + edges:
+    for copy in load:
         copy.start()
     for copy in load:
         copy.wait()
-    for chain in range(chains):
-        for i in range(WIDE):
-            to_a[chain * WIDE + i] = own[chain, (1 - odd) * (planes - WIDE) + i]
-            to_b[chain * WIDE + i] = own[chain, odd * (planes - WIDE) + i]
+    near = (0, 1, planes - 2, planes - 1)
+    send_rims(
+        lambda chain, i: own.at[chain, near[i]],
+        (edges.at[0], edges.at[1]), (edges.at[2], edges.at[3]), to_a, to_b, deep, known,
+    )
+    for chain in range(chains):
+        to_a[2 * chain] = own[chain, (1 - odd) * (planes - 1)]
+        to_b[2 * chain] = own[chain, odd * (planes - 1)]
+    to_a[2 * chains] = edges[1 - odd]
+    to_b[2 * chains] = edges[odd]
     for x in range(half):
         for out, base in ((keep, core * half), (send, (1 - core) * half)):
             for cut in tiles(own.shape[-1]):
@@ -241,8 +256,6 @@
                     second = second + v * v
                 out[x, 0, :, cut] = first
                 out[x, 1, :, cut] = second
-    for copy in edges:
-        copy.wait()
 
 
 def add_kernel(rim, a, b, *rest):
@@ -281,20 +294,19 @@
 
 def first_rim_kernel(
     q, from_a, from_b, nu, obs, scaled, before,
-    slope, nu_halo, obs_halo, potential, halo, deep, rim_scaled, scaled_deep,
+    slope, nu_halo, potential, halo, deep, rim_scaled, scaled_deep,
 ):
     odd = parity()
     chains, planes = q.shape[:2]
     place_halo(halo, from_a, from_b)
-    for out, at in ((nu_halo, chains * WIDE), (obs_halo, chains * WIDE + 1)):
-        out[1 - odd] = from_a[at]
-        out[odd] = from_b[at]
+    nu_halo[1 - odd] = from_a[chains * WIDE]
+    nu_halo[odd] = from_b[chains * WIDE]
 
     def use(chain, x, cut, v, value):
         slope[chain, x if x < 2 else x - planes + 4, :, cut] = value
 
     misfits = rims(
-        whole(q), halo, nu, obs, nu_halo, obs_halo, scaled, deep, rim_scaled, scaled_deep, use
+        whole(q), halo, nu, obs, nu_halo, scaled, deep, rim_scaled, scaled_deep, use
     )
     for chain in range(chains):
         potential[chain] = before[chain] + fold((0.5 * inv_noise) * misfits[chain])
@@ -318,15 +330,38 @@
                     )
 
 
-def send_rims(source, to_a, to_b):
+def send_rims(rim, nu_edges, obs_edges, to_a, to_b, deep, known):
     odd = parity()
-    for chain in range(source.shape[0]):
-        for i in range(WIDE):
-            to_a[chain * WIDE + i] = source[chain, (1 - odd) * WIDE + i]
-            to_b[chain * WIDE + i] = source[chain, odd * WIDE + i]
-
-
-def launch_rim_kernel(q, draw, slope, mine, other, new_q, new_p, mass, kinetic, to_a, to_b):
+    chains = deep.shape[0]
+    for chain in range(chains):
+        for i in range(2 * WIDE):
+            deepen(deep.at[chain, i], rim(chain, i))
+        for side, (edge, inside) in enumerate(((0, 1), (3, 2))):
+            view = [None, rim(chain, edge), rim(chain, inside)]
+            for cut, k in stencil(view, [None, deep.at[chain, edge], deep.at[chain, inside]]):
+                n = nu_edges[side][:, cut]
+                known[side, chain, :, cut] = n * ((unit * n) * k - obs_edges[side][:, cut])
+        to_a[2 * chain + 1] = known[1 - odd, chain]
+        to_b[2 * chain + 1] = known[odd, chain]
+
+
+def edges_of(field):
+    return field.at[0], field.at[field.shape[0] - 1]
+
+
+def send_new_rims(new_q, nu, obs, to_a, to_b, deep, known):
+    odd = parity()
+    send_rims(
+        lambda chain, i: new_q.at[chain, i], edges_of(nu), edges_of(obs), to_a, to_b, deep, known
+    )
+    for chain in range(deep.shape[0]):
+        to_a[2 * chain] = new_q[chain, (1 - odd) * 3]
+        to_b[2 * chain] = new_q[chain, odd * 3]
+
+
+def launch_rim_kernel(
+    q, draw, slope, mine, other, nu, obs, new_q, new_p, mass, kinetic, to_a, to_b, deep, known
+):
     core = lax.rem(lax.axis_index("chain"), 2)
     chains, planes = q.shape[:2]
     far = planes - WIDE
@@ -335,7 +370,7 @@
     launch(q, draw, slope, mine, other, base, new_q, new_p, mass, totals)
     for chain in range(chains):
         kinetic[chain] = fold(0.5 * totals[chain])
-    send_rims(new_q, to_a, to_b)
+    send_new_rims(new_q, nu, obs, to_a, to_b, deep, known)
 
 
 def launch_inner_kernel(q, draw, slope, mine, other, before, new_q, new_p, mass, kinetic):
@@ -364,8 +399,8 @@
 
 
 def leap_rim_kernel(
-    q_rim, q_inner, from_a, from_b, nu, obs, nu_halo, obs_halo, p, mass, scaled,
-    new_q, new_p, to_a, to_b, halo, deep, rim_scaled, scaled_deep,
+    q_rim, q_inner, from_a, from_b, nu, obs, nu_halo, p, mass, scaled,
+    new_q, new_p, to_a, to_b, halo, deep, rim_scaled, scaled_deep, send_deep, known,
 ):
     planes = q_inner.shape[1] + 2 * WIDE
     place_halo(halo, from_a, from_b)
@@ -377,10 +412,10 @@
         new_q[chain, at, :, cut] = v + step_size * mass[at, :, cut] * moment
 
     rims(
-        parts(q_rim, q_inner), halo, nu, obs, nu_halo, obs_halo,
+        parts(q_rim, q_inner), halo, nu, obs, nu_halo,
         scaled, deep, rim_scaled, scaled_deep, use,
     )
-    send_rims(new_q, to_a, to_b)
+    send_new_rims(new_q, nu, obs, to_a, to_b, send_deep, known)
 
 
 def run(copies):
@@ -449,7 +484,7 @@
 
 
 def last_rim_kernel(
-    cells, q_rim, q_inner, from_a, from_b, nu, obs, nu_halo, obs_halo, p, mass, scaled, energy,
+    cells, q_rim, q_inner, from_a, from_b, nu, obs, nu_halo, p, mass, scaled, energy,
     potential, kinetic, stored, partial_p,
     new_p, rows, halo, deep, rim_scaled, scaled_deep, rim_p, sems,
 ):
@@ -465,7 +500,7 @@
 
     copies = rim_copies(rim_p, new_p, sems)
     misfits = rims(
-        parts(q_rim, q_inner), halo, nu, obs, nu_halo, obs_halo,
+        parts(q_rim, q_inner), halo, nu, obs, nu_halo,
         scaled, deep, rim_scaled, scaled_deep, use,
         lambda chain, high: copies[2 * chain + high].start(),
     )
@@ -502,6 +537,7 @@
     tile = (chains, 8, LANES)
     scaled_shape = (chains, planes - 2, *plane)
     field = (chains, planes + 2 * WIDE, *plane)
+    send_scratch = [rim_block, (2, chains, *plane)]
     inner_scratch = [block, scaled_shape]
     rim_scratch = [halo, field, rim_block, (chains, planes + 2, *plane)]
     work = chains * planes * depth * across * 30
@@ -509,11 +545,11 @@
     def swap(to_a, to_b):
         return lax.ppermute(to_a, "gx", pair_a), lax.ppermute(to_b, "gx", pair_b)
 
-    first_edge = (chains * WIDE + 2, *plane)
+    first_edge = (chains * WIDE + 1, *plane)
     sums = (half, 2, *plane)
     position, keep, send, to_a, to_b = call(
         entry_kernel, [block, sums, sums, first_edge, first_edge],
-        [pltpu.SemaphoreType.DMA((chains + 4,))], "entry", work // 16, [MEMORY] * 3,
+        [(4, *plane), *send_scratch, pltpu.SemaphoreType.DMA((chains + 4,))], "entry", work // 16, [MEMORY] * 3,
     )(*(pltpu.with_memory_space_constraint(a, pltpu.HBM) for a in (position, viscosity, observed)))
     from_a, from_b = swap(to_a, to_b)
     got = lax.ppermute(send, "chain", near)
@@ -534,15 +570,15 @@
         first_inner_kernel, [scaled_shape, inner_block, tile], inner_scratch, "first_inner", work
     )(position, viscosity, observed)
     mine, other = mass_of(WIDE, True, (), (potential,), "mass_rim")
-    slope, nu_halo, obs_halo, potential = call(
-        first_rim_kernel, [rim_block, sides, sides, tile], rim_scratch, "first_rim", work
+    slope, nu_halo, potential = call(
+        first_rim_kernel, [rim_block, sides, tile], rim_scratch, "first_rim", work
     )(position, from_a, from_b, viscosity, observed, scaled, potential)
     inner_mine, inner_other = mass_of(half - WIDE, False, (slope,), (), "mass_inner")
     rim_q, rim_p, rim_mass, kinetic, to_a, to_b = call(
         launch_rim_kernel,
         [rim_block, rim_block, (2 * WIDE, *plane), tile, edge, edge],
-        [], "launch_rim", work // 4,
-    )(position, momentum_draw, slope, mine, other)
+        send_scratch, "launch_rim", work // 4,
+    )(position, momentum_draw, slope, mine, other, viscosity, observed)
     from_a, from_b = swap(to_a, to_b)
     inner_q, inner_p, inner_mass, kinetic = call(
         launch_inner_kernel,
@@ -555,9 +591,9 @@
             leap_inner_kernel, [scaled_shape, inner_block, inner_block], inner_scratch, "leap_inner", work
         )(old_rim, old_inner, viscosity, observed, inner_p, inner_mass)
         rim_q, rim_p, to_a, to_b = call(
-            leap_rim_kernel, [rim_block, rim_block, edge, edge], rim_scratch, "leap_rim", work
+            leap_rim_kernel, [rim_block, rim_block, edge, edge], rim_scratch + send_scratch, "leap_rim", work
         )(
-            old_rim, old_inner, from_a, from_b, viscosity, observed, nu_halo, obs_halo,
+            old_rim, old_inner, from_a, from_b, viscosity, observed, nu_halo,
             rim_p, rim_mass, scaled,
         )
         from_a, from_b = swap(to_a, to_b)
@@ -576,7 +612,7 @@
         last_rim_kernel(cells, *refs)
 
     operands = (
-        rim_q, inner_q, from_a, from_b, viscosity, observed, nu_halo, obs_halo, rim_p, rim_mass,
+        rim_q, inner_q, from_a, from_b, viscosity, observed, nu_halo, rim_p, rim_mass,
         scaled, energy, potential, kinetic, stored, partial_p,
     )
     p, rows = call(

time: 69.3 us -> 68.6 us (0.990)
  waiting for transfers between devices: 18.2 us -> 17.1 us
    ppermute x6, waiting for transfers between devices: 15.6 us -> 14.3 us  [swap(): return (lax.ppermute(to_a, 'gx', pair_a), lax.ppermute(to_b, 'gx', pair_b))]
  transfers between devices with their start and end apart: 11 -> 11, of which waited for: 6 -> 7; matrix products, arithmetic and copies ran while one was open for 0% -> 0% of each run, Pallas kernels for 12% -> 12%
where the time goes in v7:
time: 68.6 us; the launch traced here: 68.5 us
  starting transfers between devices  22.8 us (33%)
  waiting for transfers between devices  17.1 us (25%)
  blocking collectives  13.9 us (20%)
  Pallas kernels  13.2 us (19%)
  between operations  0.76 us (1%)
    ppermute x6, starting transfers between devices, swap(): return (lax.ppermute(to_a, 'gx', pair_a), lax.ppermute(to_b, 'gx', pair_b))  15.2 us
    ppermute x6, waiting for transfers between devices, swap(): return (lax.ppermute(to_a, 'gx', pair_a), lax.ppermute(to_b, 'gx', pair_b))  14.3 us
    all_to_all x1, blocking collectives, local(): rows = lax.all_to_all(rows, 'gx', 0, 0, tiled=True)  13.9 us
    ppermute x2, starting transfers between devices, mass_of(): remote = lax.ppermute(part, 'chain', far)  7.33 us
    ppermute x2, waiting for transfers between devices, mass_of(): return (mine, lax.ppermute(mine, 'chain', near))  2.62 us
    pallas_call x1, Pallas kernels, local(): call(last_body, [block, (slabs, 1, LANES)], [*rim_scratch, rim_block, cop...  1.94 us
    pallas_call x1, Pallas kernels, local(): call(entry_kernel, [block, sums, sums, first_edge, first_edge], [(4, *pla...  1.69 us
    pallas_call x1, Pallas kernels, local(): call(last_inner_kernel, [scaled_shape, inner_block, tile], inner_scratch,...  1.52 us
  transfers between devices with their start and end apart: 11, of which 7 were waited for; matrix products, arithmetic and copies ran while one was open for 0% of the time, Pallas kernels for 12%

profile of v7, /device:TPU:0, one launch (start us, length us, event | category | flops | bytes accessed | tf_op | source)
XLA Modules:
  0.0 68.5 jit_solution(6503887070075573062)
XLA Ops:
  0.6 1.7 %entry.1 = (f32[2,8,16,1024]{3,2,1,0:T(8,128)S(1)}, f32[4,2,16,1024]{3,2,1,0:T(8,128)S(1)}, f32[4,2,16,1024]{3,2,1,0:T(8,128)S(1)}, f32[5,16,1024]{2,1,0:T(8,128)S(1)}, f32[5,16,1024]{2,1,0:T(8,128)S(1)}) custom-call(f32[2,8,16,1024]{3,2,1,0:T(8,128)} %q.1, f32[8,16,1024]{2,1,0:T(8,128)} %refs_4_.1, f32[8,16,1024]{2,1,0:T(8,128)} %refs_5_.1), custom_call_target="tpu_custom_call" | custom-call | flops 491520 | bytes 61440 | tf_op jit(solution)/shard_map/entry/pallas_call | solution.py:550
  2.4 6.7 %collective-permute-start = (f32[5,16,1024]{2,1,0:T(8,128)S(1)}, f32[5,16,1024]{2,1,0:T(8,128)S(1)}, u32[]{:S(2)}, u32[]{:S(2)}) collective-permute-start(f32[5,16,1024]{2,1,0:T(8,128)S(1)} %get-tuple-element.39), channel_id=1, source_target_pairs={{0,31},{1,2},{2,1},{3,4},{4,3},{5,6},{6,5},{7,8},{8,7},{9,10},{10,... | collective-permute-start | bytes 983048 | tf_op jit(solution)/shard_map/ppermute | solution.py:546
  9.2 3.7 %collective-permute-start.3 = (f32[2,2,16,1024]{3,2,1,0:T(8,128)S(1)}, f32[2,2,16,1024]{3,2,1,0:T(8,128)S(1)}, u32[]{:S(2)}, u32[]{:S(2)}) collective-permute-start(f32[2,2,16,1024]{3,2,1,0:T(8,128)S(1)} %mass_rim_add.1.refs_0_), channel_id=1, source_target_pairs={{0,64},{32,96},{64,0},{96,32},{1,65},{33,97},{65,1},{97,33},{2,66}... | collective-permute-start | bytes 786440 | tf_op jit(solution)/shard_map/ppermute | solution.py:565
  12.9 1.4 %first_inner.1 = (f32[2,6,16,1024]{3,2,1,0:T(8,128)S(1)}, f32[2,4,16,1024]{3,2,1,0:T(8,128)S(1)}, f32[2,8,128]{2,1,0:T(8,128)S(1)}) custom-call(f32[2,8,16,1024]{3,2,1,0:T(8,128)S(1)} %get-tuple-element.38.q, f32[8,16,1024]{2,1,0:T(8,128)S(1)} %copy-done, f32[8,16,1024]{2,1,0:T(8,128)S(1)} %copy-done.1), custom_call_target="tpu_custom_call" | custom-call | flops 7864320 | bytes 983040 | tf_op jit(solution)/shard_map/first_inner/pallas_call | solution.py:569
  14.3 3.3 %collective-permute-done.from_a = f32[5,16,1024]{2,1,0:T(8,128)S(1)} collective-permute-done((f32[5,16,1024]{2,1,0:T(8,128)S(1)}, f32[5,16,1024]{2,1,0:T(8,128)S(1)}, u32[]{:S(2)}, u32[]{:S(2)}) %collective-permute-start) | collective-permute-done | bytes 327712 | tf_op jit(solution)/shard_map/ppermute | solution.py:546
  17.5 1.4 %collective-permute-done.1.from_b = f32[5,16,1024]{2,1,0:T(8,128)S(1)} collective-permute-done((f32[5,16,1024]{2,1,0:T(8,128)S(1)}, f32[5,16,1024]{2,1,0:T(8,128)S(1)}, u32[]{:S(2)}, u32[]{:S(2)}) %collective-permute-start.1) | collective-permute-done | bytes 327712 | tf_op jit(solution)/shard_map/ppermute | solution.py:546
  18.9 1.0 %first_rim.1 = (f32[2,4,16,1024]{3,2,1,0:T(8,128)S(1)}, f32[2,16,1024]{2,1,0:T(8,128)S(1)}, f32[2,8,128]{2,1,0:T(8,128)S(1)}) custom-call(f32[2,8,16,1024]{3,2,1,0:T(8,128)S(1)} %get-tuple-element.38.q, f32[5,16,1024]{2,1,0:T(8,128)S(1)} %collective-permute-done.from_a, f32[5,16,1024]{2,1,0:T(8,128)S(1)} %collective-permute-done.1.from_b, ...), custom_call_target="tpu_custom_call" | custom-call | flops 7864320 | bytes 983040 | tf_op jit(solution)/shard_map/first_rim/pallas_call | solution.py:573
  20.0 3.7 %collective-permute-start.5 = (f32[2,2,16,1024]{3,2,1,0:T(8,128)S(1)}, f32[2,2,16,1024]{3,2,1,0:T(8,128)S(1)}, u32[]{:S(2)}, u32[]{:S(2)}) collective-permute-start(f32[2,2,16,1024]{3,2,1,0:T(8,128)S(1)} %mass_inner_add.1.refs_0_), channel_id=1, source_target_pairs={{0,64},{32,96},{64,0},{96,32},{1,65},{33,97},{65,1},{97,33},{2,66}... | collective-permute-start | bytes 786440 | tf_op jit(solution)/shard_map/ppermute | solution.py:565
  24.0 1.3 %collective-permute-done.4.other = f32[2,16,1024]{2,1,0:T(8,128)S(1)} collective-permute-done((f32[2,16,1024]{2,1,0:T(8,128)S(1)}, f32[2,16,1024]{2,1,0:T(8,128)S(1)}, u32[]{:S(2)}, u32[]{:S(2)}) %collective-permute-start.4) | collective-permute-done | bytes 131104 | tf_op jit(solution)/shard_map/ppermute | solution.py:567
  25.3 0.6 launch_rim.1
  25.9 4.2 %collective-permute-start.7 = (f32[4,16,1024]{2,1,0:T(8,128)S(1)}, f32[4,16,1024]{2,1,0:T(8,128)S(1)}, u32[]{:S(2)}, u32[]{:S(2)}) collective-permute-start(f32[4,16,1024]{2,1,0:T(8,128)S(1)} %get-tuple-element.50), channel_id=1, source_target_pairs={{0,31},{1,2},{2,1},{3,4},{4,3},{5,6},{6,5},{7,8},{8,7},{9,10},{10,... | collective-permute-start | bytes 786440 | tf_op jit(solution)/shard_map/ppermute | solution.py:546
  30.3 1.3 %collective-permute-done.6.other = f32[2,16,1024]{2,1,0:T(8,128)S(1)} collective-permute-done((f32[2,16,1024]{2,1,0:T(8,128)S(1)}, f32[2,16,1024]{2,1,0:T(8,128)S(1)}, u32[]{:S(2)}, u32[]{:S(2)}) %collective-permute-start.6) | collective-permute-done | bytes 131104 | tf_op jit(solution)/shard_map/ppermute | solution.py:567
  31.6 0.2 launch_inner.1
  31.9 1.3 %leap_inner.1 = (f32[2,6,16,1024]{3,2,1,0:T(8,128)S(1)}, f32[2,4,16,1024]{3,2,1,0:T(8,128)S(1)}, f32[2,4,16,1024]{3,2,1,0:T(8,128)S(1)}) custom-call(f32[2,4,16,1024]{3,2,1,0:T(8,128)S(1)} %get-tuple-element.46.q_rim, f32[2,4,16,1024]{3,2,1,0:T(8,128)S(1)} %get-tuple-element.49.q_inner, f32[8,16,1024]{2,1,0:T(8,128)S(1)} %copy-done, ...), custom_call_target="tpu_custom_call" | custom-call | flops 7864320 | bytes 983040 | tf_op jit(solution)/shard_map/leap_inner/pallas_call | solution.py:590
  33.2 5.4 %collective-permute-done.7.from_a = f32[4,16,1024]{2,1,0:T(8,128)S(1)} collective-permute-done((f32[4,16,1024]{2,1,0:T(8,128)S(1)}, f32[4,16,1024]{2,1,0:T(8,128)S(1)}, u32[]{:S(2)}, u32[]{:S(2)}) %collective-permute-start.7) | collective-permute-done | bytes 262176 | tf_op jit(solution)/shard_map/ppermute | solution.py:546
  38.6 1.5 %leap_rim.1 = (f32[2,4,16,1024]{3,2,1,0:T(8,128)S(1)}, f32[2,4,16,1024]{3,2,1,0:T(8,128)S(1)}, f32[4,16,1024]{2,1,0:T(8,128)S(1)}, f32[4,16,1024]{2,1,0:T(8,128)S(1)}) custom-call(f32[2,4,16,1024]{3,2,1,0:T(8,128)S(1)} %get-tuple-element.46.q_rim, f32[2,4,16,1024]{3,2,1,0:T(8,128)S(1)} %get-tuple-element.49.q_inner, ...), custom_call_target="tpu_custom_call" | custom-call | flops 7864320 | bytes 983040 | tf_op jit(solution)/shard_map/leap_rim/pallas_call | solution.py:593
  40.1 4.2 %collective-permute-start.9 = (f32[4,16,1024]{2,1,0:T(8,128)S(1)}, f32[4,16,1024]{2,1,0:T(8,128)S(1)}, u32[]{:S(2)}, u32[]{:S(2)}) collective-permute-start(f32[4,16,1024]{2,1,0:T(8,128)S(1)} %get-tuple-element.61), channel_id=1, source_target_pairs={{0,31},{1,2},{2,1},{3,4},{4,3},{5,6},{6,5},{7,8},{8,7},{9,10},{10,... | collective-permute-start | bytes 786440 | tf_op jit(solution)/shard_map/ppermute | solution.py:546
  44.3 1.5 %last_inner.1 = (f32[2,6,16,1024]{3,2,1,0:T(8,128)S(1)}, f32[2,4,16,1024]{3,2,1,0:T(8,128)S(1)}, f32[2,8,128]{2,1,0:T(8,128)S(1)}) custom-call(f32[2,4,16,1024]{3,2,1,0:T(8,128)S(1)} %get-tuple-element.58.rim.q_rim.refs_0_, f32[2,4,16,1024]{3,2,1,0:T(8,128)S(1)} %get-tuple-element.59.inner.q_inner.refs_1_, f32[8,16,1024]{2,1,0:T(8,128)S(1)} %copy-done, ...), custom_call_target="tpu_custom_call" | custom-call | flops 7864320 | bytes 983040 | tf_op jit(solution)/shard_map/last_inner/pallas_call | solution.py:604
  45.8 0.8 %store_p.1.refs_14_ = f32[2,8,16,1024]{3,2,1,0:T(8,128)} custom-call(f32[2,4,16,1024]{3,2,1,0:T(8,128)S(1)} %get-tuple-element.70.inner), custom_call_target="tpu_custom_call" | custom-call | flops 491520 | bytes 61440 | tf_op jit(solution)/shard_map/store_p/pallas_call | solution.py:607
  46.7 1.0 %store_q.1 = (f32[2,8,16,1024]{3,2,1,0:T(8,128)}, f32[8,128]{1,0:T(8,128)S(1)}) custom-call(f32[2,4,16,1024]{3,2,1,0:T(8,128)S(1)} %get-tuple-element.58.rim.q_rim.refs_0_, f32[2,4,16,1024]{3,2,1,0:T(8,128)S(1)} %get-tuple-element.59.inner.q_inner.refs_1_), custom_call_target="tpu_custom_call" | custom-call | flops 983040 | bytes 122880 | tf_op jit(solution)/shard_map/store_q/pallas_call | solution.py:601
  47.7 4.2 %collective-permute-done.9.refs_2_ = f32[4,16,1024]{2,1,0:T(8,128)S(1)} collective-permute-done((f32[4,16,1024]{2,1,0:T(8,128)S(1)}, f32[4,16,1024]{2,1,0:T(8,128)S(1)}, u32[]{:S(2)}, u32[]{:S(2)}) %collective-permute-start.9) | collective-permute-done | bytes 262176 | tf_op jit(solution)/shard_map/ppermute | solution.py:546
  51.9 1.9 %last_rim.1 = (f32[2,8,16,1024]{3,2,1,0:T(8,128)}, f32[32,1,128]{2,1,0:T(1,128)S(1)}) custom-call(f32[2,4,16,1024]{3,2,1,0:T(8,128)S(1)} %get-tuple-element.58.rim.q_rim.refs_0_, f32[2,4,16,1024]{3,2,1,0:T(8,128)S(1)} %get-tuple-element.59.inner.q_inner.refs_1_, f32[4,16,1024]{2,1,0:T(8,128)S(1)} %collective-permute-done.9.refs_2_, ...), custom_call_target="tpu_custom_call", output_to_operand_aliasing={{0}: (14, {})} | custom-call | flops 7864320 | bytes 983040 | tf_op jit(solution)/shard_map/last_rim/pallas_call | solution.py:618
  53.9 13.9 %all_to_all.5 = f32[32,1,128]{2,1,0:T(1,128)S(1)} all-to-all(f32[32,1,128]{2,1,0:T(1,128)S(1)} %get-tuple-element.72), channel_id=1, replica_groups=mesh['chain'=4,'gx'=32] {'gx'}, dimensions={0} | all-to-all | bytes 32768 | tf_op jit(solution)/shard_map/all_to_all | solution.py:622
  67.8 0.6 reduce_sum.12
  (22 shorter events, 0.7 us)
Async XLA Ops:
  2.3 6.8 %collective-permute-start.2 = (f32[4,2,16,1024]{3,2,1,0:T(8,128)S(1)}, f32[4,2,16,1024]{3,2,1,0:T(8,128)S(1)}, u32[]{:S(2)}, u32[]{:S(2)}) collective-permute-start(f32[4,2,16,1024]{3,2,1,0:T(8,128)S(1)} %get-tuple-element.45), channel_id=1, source_target_pairs={{0,32},{32,0},{64,96},{96,64},{1,33},{33,1},{65,97},{97,65},{2,34}... | collective-permute-start | bytes 1572872 | tf_op jit(solution)/shard_map/ppermute | solution.py:555
  2.4 15.1 %collective-permute-start = (f32[5,16,1024]{2,1,0:T(8,128)S(1)}, f32[5,16,1024]{2,1,0:T(8,128)S(1)}, u32[]{:S(2)}, u32[]{:S(2)}) collective-permute-start(f32[5,16,1024]{2,1,0:T(8,128)S(1)} %get-tuple-element.39), channel_id=1, source_target_pairs={{0,31},{1,2},{2,1},{3,4},{4,3},{5,6},{6,5},{7,8},{8,7},{9,10},{10,... | collective-permute-start | bytes 983048 | tf_op jit(solution)/shard_map/ppermute | solution.py:546
  9.1 9.8 %collective-permute-start.1 = (f32[5,16,1024]{2,1,0:T(8,128)S(1)}, f32[5,16,1024]{2,1,0:T(8,128)S(1)}, u32[]{:S(2)}, u32[]{:S(2)}) collective-permute-start(f32[5,16,1024]{2,1,0:T(8,128)S(1)} %get-tuple-element.40), channel_id=1, source_target_pairs={{0,1},{1,0},{2,3},{3,2},{4,5},{5,4},{6,7},{7,6},{8,9},{9,8},{10,11... | collective-permute-start | bytes 983048 | tf_op jit(solution)/shard_map/ppermute | solution.py:546
  9.2 3.7 %copy-start = (f32[8,16,1024]{2,1,0:T(8,128)S(1)}, f32[8,16,1024]{2,1,0:T(8,128)}, u32[]{:S(2)}) copy-start(f32[8,16,1024]{2,1,0:T(8,128)} %refs_4_.1) | copy-start | bytes 1572868
  9.2 3.7 %copy-start.1 = (f32[8,16,1024]{2,1,0:T(8,128)S(1)}, f32[8,16,1024]{2,1,0:T(8,128)}, u32[]{:S(2)}) copy-start(f32[8,16,1024]{2,1,0:T(8,128)} %refs_5_.1) | copy-start | bytes 1572868
  9.2 14.6 %collective-permute-start.3 = (f32[2,2,16,1024]{3,2,1,0:T(8,128)S(1)}, f32[2,2,16,1024]{3,2,1,0:T(8,128)S(1)}, u32[]{:S(2)}, u32[]{:S(2)}) collective-permute-start(f32[2,2,16,1024]{3,2,1,0:T(8,128)S(1)} %mass_rim_add.1.refs_0_), channel_id=1, source_target_pairs={{0,64},{32,96},{64,0},{96,32},{1,65},{33,97},{65,1},{97,33},{2,66}... | collective-permute-start | bytes 786440 | tf_op jit(solution)/shard_map/ppermute | solution.py:565
  19.9 5.3 %copy-start.2 = (f32[2,8,16,1024]{3,2,1,0:T(8,128)S(1)}, f32[2,8,16,1024]{3,2,1,0:T(8,128)}, u32[]{:S(2)}) copy-start(f32[2,8,16,1024]{3,2,1,0:T(8,128)} %draw.3) | copy-start | bytes 3145732
  20.0 10.1 %collective-permute-start.5 = (f32[2,2,16,1024]{3,2,1,0:T(8,128)S(1)}, f32[2,2,16,1024]{3,2,1,0:T(8,128)S(1)}, u32[]{:S(2)}, u32[]{:S(2)}) collective-permute-start(f32[2,2,16,1024]{3,2,1,0:T(8,128)S(1)} %mass_inner_add.1.refs_0_), channel_id=1, source_target_pairs={{0,64},{32,96},{64,0},{96,32},{1,65},{33,97},{65,1},{97,33},{2,66}... | collective-permute-start | bytes 786440 | tf_op jit(solution)/shard_map/ppermute | solution.py:565
  23.9 1.4 %collective-permute-start.4 = (f32[2,16,1024]{2,1,0:T(8,128)S(1)}, f32[2,16,1024]{2,1,0:T(8,128)S(1)}, u32[]{:S(2)}, u32[]{:S(2)}) collective-permute-start(f32[2,16,1024]{2,1,0:T(8,128)S(1)} %mass_rim.1.mine), channel_id=1, source_target_pairs={{0,32},{32,0},{64,96},{96,64},{1,33},{33,1},{65,97},{97,65},{2,34}... | collective-permute-start | bytes 393224 | tf_op jit(solution)/shard_map/ppermute | solution.py:567
  25.9 12.7 %collective-permute-start.7 = (f32[4,16,1024]{2,1,0:T(8,128)S(1)}, f32[4,16,1024]{2,1,0:T(8,128)S(1)}, u32[]{:S(2)}, u32[]{:S(2)}) collective-permute-start(f32[4,16,1024]{2,1,0:T(8,128)S(1)} %get-tuple-element.50), channel_id=1, source_target_pairs={{0,31},{1,2},{2,1},{3,4},{4,3},{5,6},{6,5},{7,8},{8,7},{9,10},{10,... | collective-permute-start | bytes 786440 | tf_op jit(solution)/shard_map/ppermute | solution.py:546
  30.1 8.5 %collective-permute-start.8 = (f32[4,16,1024]{2,1,0:T(8,128)S(1)}, f32[4,16,1024]{2,1,0:T(8,128)S(1)}, u32[]{:S(2)}, u32[]{:S(2)}) collective-permute-start(f32[4,16,1024]{2,1,0:T(8,128)S(1)} %get-tuple-element.51), channel_id=1, source_target_pairs={{0,1},{1,0},{2,3},{3,2},{4,5},{5,4},{6,7},{7,6},{8,9},{9,8},{10,11... | collective-permute-start | bytes 786440 | tf_op jit(solution)/shard_map/ppermute | solution.py:546
  30.2 1.4 %collective-permute-start.6 = (f32[2,16,1024]{2,1,0:T(8,128)S(1)}, f32[2,16,1024]{2,1,0:T(8,128)S(1)}, u32[]{:S(2)}, u32[]{:S(2)}) collective-permute-start(f32[2,16,1024]{2,1,0:T(8,128)S(1)} %mass_inner.1.mine), channel_id=1, source_target_pairs={{0,32},{32,0},{64,96},{96,64},{1,33},{33,1},{65,97},{97,65},{2,34}... | collective-permute-start | bytes 393224 | tf_op jit(solution)/shard_map/ppermute | solution.py:567
  40.1 11.8 %collective-permute-start.9 = (f32[4,16,1024]{2,1,0:T(8,128)S(1)}, f32[4,16,1024]{2,1,0:T(8,128)S(1)}, u32[]{:S(2)}, u32[]{:S(2)}) collective-permute-start(f32[4,16,1024]{2,1,0:T(8,128)S(1)} %get-tuple-element.61), channel_id=1, source_target_pairs={{0,31},{1,2},{2,1},{3,4},{4,3},{5,6},{6,5},{7,8},{8,7},{9,10},{10,... | collective-permute-start | bytes 786440 | tf_op jit(solution)/shard_map/ppermute | solution.py:546
  44.3 7.6 %collective-permute-start.10 = (f32[4,16,1024]{2,1,0:T(8,128)S(1)}, f32[4,16,1024]{2,1,0:T(8,128)S(1)}, u32[]{:S(2)}, u32[]{:S(2)}) collective-permute-start(f32[4,16,1024]{2,1,0:T(8,128)S(1)} %get-tuple-element.62), channel_id=1, source_target_pairs={{0,1},{1,0},{2,3},{3,2},{4,5},{5,4},{6,7},{7,6},{8,9},{9,8},{10,11... | collective-permute-start | bytes 786440 | tf_op jit(solution)/shard_map/ppermute | solution.py:546

commit v8 on v7

--- a/solution.py
+++ b/solution.py
@@ -459,7 +459,17 @@
     run(inner_copies(inner, out, sems))
 
 
-def last_inner_kernel(q_rim, q_inner, nu, obs, p, mass, scaled, new_p, energy, deep, scaled_deep):
+def marked(tiles_of, row, cells, mark):
+    lane = lax.broadcasted_iota(jnp.int32, mark.shape, 1)
+    for chain, tile in enumerate(tiles_of):
+        mark = jnp.where(lane == row * len(tiles_of) + chain, jnp.sum(tile) / cells, mark)
+    return mark
+
+
+def last_inner_kernel(
+    cells, q_rim, q_inner, nu, obs, p, mass, potential, kinetic,
+    scaled, new_p, energy, start, deep, scaled_deep,
+):
     chains, planes = deep.shape[:2]
     q_at = parts(q_rim, q_inner)
     totals = [0.0] * chains
@@ -481,14 +491,16 @@
         energy[chain] = fold(
             (0.5 * inv_noise) * misfits[chain] + (0.5 * prior_weight) * squares + totals[chain]
         )
+    tiles_of = [potential[chain] + kinetic[chain] for chain in range(chains)]
+    start[...] = marked(tiles_of, 0, cells, jnp.zeros(start.shape, jnp.float32))
 
 
 def last_rim_kernel(
     cells, q_rim, q_inner, from_a, from_b, nu, obs, nu_halo, p, mass, scaled, energy,
-    potential, kinetic, stored, partial_p,
-    new_p, rows, halo, deep, rim_scaled, scaled_deep, rim_p, sems,
+    start, stored,
+    rim_p, rows, halo, deep, rim_scaled, scaled_deep,
 ):
-    chains, planes = new_p.shape[:2]
+    chains, planes = rim_p.shape[0], nu.shape[0]
     totals = [0.0] * chains
     place_halo(halo, from_a, from_b)
 
@@ -498,23 +510,17 @@
         rim_p[chain, at, :, cut] = moment
         totals[chain] = totals[chain] + (0.5 * mass[at, :, cut]) * (moment * moment)
 
-    copies = rim_copies(rim_p, new_p, sems)
     misfits = rims(
         parts(q_rim, q_inner), halo, nu, obs, nu_halo,
         scaled, deep, rim_scaled, scaled_deep, use,
-        lambda chain, high: copies[2 * chain + high].start(),
-    )
-    lane = lax.broadcasted_iota(jnp.int32, (1, LANES), 1)
-    mark = jnp.zeros((1, LANES), jnp.float32)
-    for chain in range(chains):
-        end = energy[chain] + fold((0.5 * inv_noise) * misfits[chain] + totals[chain])
-        start = potential[chain] + kinetic[chain]
-        for row, tile in enumerate((start, end)):
-            mark = jnp.where(lane == row * chains + chain, jnp.sum(tile) / cells, mark)
+    )
+    tiles_of = [
+        energy[chain] + fold((0.5 * inv_noise) * misfits[chain] + totals[chain])
+        for chain in range(chains)
+    ]
+    mark = marked(tiles_of, 1, cells, start[...])
     for i in range(rows.shape[0]):
         rows[i] = mark
-    for copy in copies:
-        copy.wait()
 
 
 def local(position, momentum_draw, viscosity, observed):
@@ -601,9 +607,13 @@
     q, stored = call(
         store_kernel, [block, (8, LANES)], [copy_sems], "store_q", work // 8, outs=[MEMORY, VECTOR]
     )(rim_q, inner_q)
-    scaled, inner_p, energy = call(
-        last_inner_kernel, [scaled_shape, inner_block, tile], inner_scratch, "last_inner", work
-    )(rim_q, inner_q, viscosity, observed, inner_p, inner_mass)
+
+    def last_inner_body(*refs):
+        last_inner_kernel(cells, *refs)
+
+    scaled, inner_p, energy, start = call(
+        last_inner_body, [scaled_shape, inner_block, tile, (1, LANES)], inner_scratch, "last_inner", work
+    )(rim_q, inner_q, viscosity, observed, inner_p, inner_mass, potential, kinetic)
     partial_p = call(
         store_inner_kernel, [block], [copy_sems], "store_p", work // 16, outs=[MEMORY]
     )(inner_p)[0]
@@ -613,14 +623,29 @@
 
     operands = (
         rim_q, inner_q, from_a, from_b, viscosity, observed, nu_halo, rim_p, rim_mass,
-        scaled, energy, potential, kinetic, stored, partial_p,
-    )
-    p, rows = call(
-        last_body, [block, (slabs, 1, LANES)], [*rim_scratch, rim_block, copy_sems], "last_rim", work,
-        [VECTOR] * (len(operands) - 1) + [MEMORY], [MEMORY, VECTOR], {len(operands) - 1: 0},
+        scaled, energy, start, stored,
+    )
+    rim_p, rows = call(
+        last_body, [rim_block, (slabs, 1, LANES)], rim_scratch, "last_rim", work
     )(*operands)
     rows = lax.all_to_all(rows, "gx", 0, 0, tiled=True)
-    energies = jnp.sum(rows[:, 0, : 2 * chains].reshape(slabs, 2, chains), axis=0)
+
+    def finish_kernel(rows, rim_p, partial_p, new_p, out, sems):
+        copies = rim_copies(rim_p, new_p, sems)
+        for copy in copies:
+            copy.start()
+        value = rows[0]
+        for i in range(1, slabs):
+            value = value + rows[i]
+        for row in range(2):
+            out[row : row + 1, :] = value[:, row * chains : (row + 1) * chains]
+        for copy in copies:
+            copy.wait()
+
+    p, energies = call(
+        finish_kernel, [block, (2, chains)], [copy_sems], "finish", work // 64,
+        [VECTOR, VECTOR, MEMORY], [MEMORY, VECTOR], {2: 0},
+    )(rows, rim_p, partial_p)
     return (q, p, energies)
 
 

time: 68.6 us -> 69.6 us (1.015)
  blocking collectives: 13.9 us -> 0 us
  waiting for transfers between devices: 17.1 us -> 25.4 us
  starting transfers between devices: 22.8 us -> 28.6 us
  Pallas kernels: 13.2 us -> 14.5 us
    all_to_all x1 -> x0, blocking collectives: 13.9 us -> none  [local(): rows = lax.all_to_all(rows, 'gx', 0, 0, tiled=True)]
    all_to_all x0 -> x1, waiting for transfers between devices: none -> 7.43 us  [local(): rows = lax.all_to_all(rows, 'gx', 0, 0, tiled=True)]
    all_to_all x0 -> x1, starting transfers between devices: none -> 5.79 us  [local(): rows = lax.all_to_all(rows, 'gx', 0, 0, tiled=True)]
    pallas_call x2 -> x3, Pallas kernels: 3.46 us -> 4.72 us  [the longest x1 1.84 us: local(): call(last_body, [rim_block, (slabs, 1, LANES)], rim_scratch, 'last_rim',...]
    ppermute x6, waiting for transfers between devices: 14.3 us -> 15.2 us  [swap(): return (lax.ppermute(to_a, 'gx', pair_a), lax.ppermute(to_b, 'gx', pair_b))]
  transfers between devices with their start and end apart: 11 -> 12, of which waited for: 7 -> 8; matrix products, arithmetic and copies ran while one was open for 0% -> 0% of each run, Pallas kernels for 12% -> 12%
where the time goes in v8:
time: 69.6 us; the launch traced here: 69.4 us
  starting transfers between devices  28.6 us (41%)
  waiting for transfers between devices  25.4 us (36%)
  Pallas kernels  14.5 us (21%)
  between operations  0.92 us (1%)
    ppermute x6, waiting for transfers between devices, swap(): return (lax.ppermute(to_a, 'gx', pair_a), lax.ppermute(to_b, 'gx', pair_b))  15.2 us
    ppermute x6, starting transfers between devices, swap(): return (lax.ppermute(to_a, 'gx', pair_a), lax.ppermute(to_b, 'gx', pair_b))  15.2 us
    all_to_all x1, waiting for transfers between devices, local(): rows = lax.all_to_all(rows, 'gx', 0, 0, tiled=True)  7.43 us
    ppermute x2, starting transfers between devices, mass_of(): remote = lax.ppermute(part, 'chain', far)  7.33 us
    all_to_all x1, starting transfers between devices, local(): rows = lax.all_to_all(rows, 'gx', 0, 0, tiled=True)  5.79 us
    ppermute x2, waiting for transfers between devices, mass_of(): return (mine, lax.ppermute(mine, 'chain', near))  2.62 us
    pallas_call x1, Pallas kernels, local(): call(last_body, [rim_block, (slabs, 1, LANES)], rim_scratch, 'last_rim',...  1.84 us
    pallas_call x1, Pallas kernels, local(): call(entry_kernel, [block, sums, sums, first_edge, first_edge], [(4, *pla...  1.69 us
  transfers between devices with their start and end apart: 12, of which 8 were waited for; matrix products, arithmetic and copies ran while one was open for 0% of the time, Pallas kernels for 12%

profile of v8, /device:TPU:0, one launch (start us, length us, event | category | flops | bytes accessed | tf_op | source)
XLA Modules:
  0.0 69.4 jit_solution(8318641779359105556)
XLA Ops:
  0.6 1.7 %entry.1 = (f32[2,8,16,1024]{3,2,1,0:T(8,128)S(1)}, f32[4,2,16,1024]{3,2,1,0:T(8,128)S(1)}, f32[4,2,16,1024]{3,2,1,0:T(8,128)S(1)}, f32[5,16,1024]{2,1,0:T(8,128)S(1)}, f32[5,16,1024]{2,1,0:T(8,128)S(1)}) custom-call(f32[2,8,16,1024]{3,2,1,0:T(8,128)} %q.1, f32[8,16,1024]{2,1,0:T(8,128)} %refs_4_.1, f32[8,16,1024]{2,1,0:T(8,128)} %refs_5_.1), custom_call_target="tpu_custom_call" | custom-call | flops 491520 | bytes 61440 | tf_op jit(solution)/shard_map/entry/pallas_call | solution.py:556
  2.4 6.7 %collective-permute-start = (f32[5,16,1024]{2,1,0:T(8,128)S(1)}, f32[5,16,1024]{2,1,0:T(8,128)S(1)}, u32[]{:S(2)}, u32[]{:S(2)}) collective-permute-start(f32[5,16,1024]{2,1,0:T(8,128)S(1)} %get-tuple-element.42), channel_id=1, source_target_pairs={{0,31},{1,2},{2,1},{3,4},{4,3},{5,6},{6,5},{7,8},{8,7},{9,10},{10,... | collective-permute-start | bytes 983048 | tf_op jit(solution)/shard_map/ppermute | solution.py:552
  9.2 3.7 %collective-permute-start.3 = (f32[2,2,16,1024]{3,2,1,0:T(8,128)S(1)}, f32[2,2,16,1024]{3,2,1,0:T(8,128)S(1)}, u32[]{:S(2)}, u32[]{:S(2)}) collective-permute-start(f32[2,2,16,1024]{3,2,1,0:T(8,128)S(1)} %mass_rim_add.1.refs_0_), channel_id=1, source_target_pairs={{0,64},{32,96},{64,0},{96,32},{1,65},{33,97},{65,1},{97,33},{2,66}... | collective-permute-start | bytes 786440 | tf_op jit(solution)/shard_map/ppermute | solution.py:571
  12.9 1.4 %first_inner.1 = (f32[2,6,16,1024]{3,2,1,0:T(8,128)S(1)}, f32[2,4,16,1024]{3,2,1,0:T(8,128)S(1)}, f32[2,8,128]{2,1,0:T(8,128)S(1)}) custom-call(f32[2,8,16,1024]{3,2,1,0:T(8,128)S(1)} %get-tuple-element.41.q, f32[8,16,1024]{2,1,0:T(8,128)S(1)} %copy-done, f32[8,16,1024]{2,1,0:T(8,128)S(1)} %copy-done.1), custom_call_target="tpu_custom_call" | custom-call | flops 7864320 | bytes 983040 | tf_op jit(solution)/shard_map/first_inner/pallas_call | solution.py:575
  14.3 3.3 %collective-permute-done.from_a = f32[5,16,1024]{2,1,0:T(8,128)S(1)} collective-permute-done((f32[5,16,1024]{2,1,0:T(8,128)S(1)}, f32[5,16,1024]{2,1,0:T(8,128)S(1)}, u32[]{:S(2)}, u32[]{:S(2)}) %collective-permute-start) | collective-permute-done | bytes 327712 | tf_op jit(solution)/shard_map/ppermute | solution.py:552
  17.5 1.4 %collective-permute-done.1.from_b = f32[5,16,1024]{2,1,0:T(8,128)S(1)} collective-permute-done((f32[5,16,1024]{2,1,0:T(8,128)S(1)}, f32[5,16,1024]{2,1,0:T(8,128)S(1)}, u32[]{:S(2)}, u32[]{:S(2)}) %collective-permute-start.1) | collective-permute-done | bytes 327712 | tf_op jit(solution)/shard_map/ppermute | solution.py:552
  18.9 1.0 %first_rim.1 = (f32[2,4,16,1024]{3,2,1,0:T(8,128)S(1)}, f32[2,16,1024]{2,1,0:T(8,128)S(1)}, f32[2,8,128]{2,1,0:T(8,128)S(1)}) custom-call(f32[2,8,16,1024]{3,2,1,0:T(8,128)S(1)} %get-tuple-element.41.q, f32[5,16,1024]{2,1,0:T(8,128)S(1)} %collective-permute-done.from_a, f32[5,16,1024]{2,1,0:T(8,128)S(1)} %collective-permute-done.1.from_b, ...), custom_call_target="tpu_custom_call" | custom-call | flops 7864320 | bytes 983040 | tf_op jit(solution)/shard_map/first_rim/pallas_call | solution.py:579
  20.0 3.7 %collective-permute-start.5 = (f32[2,2,16,1024]{3,2,1,0:T(8,128)S(1)}, f32[2,2,16,1024]{3,2,1,0:T(8,128)S(1)}, u32[]{:S(2)}, u32[]{:S(2)}) collective-permute-start(f32[2,2,16,1024]{3,2,1,0:T(8,128)S(1)} %mass_inner_add.1.refs_0_), channel_id=1, source_target_pairs={{0,64},{32,96},{64,0},{96,32},{1,65},{33,97},{65,1},{97,33},{2,66}... | collective-permute-start | bytes 786440 | tf_op jit(solution)/shard_map/ppermute | solution.py:571
  24.0 1.3 %collective-permute-done.4.other = f32[2,16,1024]{2,1,0:T(8,128)S(1)} collective-permute-done((f32[2,16,1024]{2,1,0:T(8,128)S(1)}, f32[2,16,1024]{2,1,0:T(8,128)S(1)}, u32[]{:S(2)}, u32[]{:S(2)}) %collective-permute-start.4) | collective-permute-done | bytes 131104 | tf_op jit(solution)/shard_map/ppermute | solution.py:573
  25.3 0.6 launch_rim.1
  25.9 4.2 %collective-permute-start.7 = (f32[4,16,1024]{2,1,0:T(8,128)S(1)}, f32[4,16,1024]{2,1,0:T(8,128)S(1)}, u32[]{:S(2)}, u32[]{:S(2)}) collective-permute-start(f32[4,16,1024]{2,1,0:T(8,128)S(1)} %get-tuple-element.53), channel_id=1, source_target_pairs={{0,31},{1,2},{2,1},{3,4},{4,3},{5,6},{6,5},{7,8},{8,7},{9,10},{10,... | collective-permute-start | bytes 786440 | tf_op jit(solution)/shard_map/ppermute | solution.py:552
  30.3 1.3 %collective-permute-done.6.other = f32[2,16,1024]{2,1,0:T(8,128)S(1)} collective-permute-done((f32[2,16,1024]{2,1,0:T(8,128)S(1)}, f32[2,16,1024]{2,1,0:T(8,128)S(1)}, u32[]{:S(2)}, u32[]{:S(2)}) %collective-permute-start.6) | collective-permute-done | bytes 131104 | tf_op jit(solution)/shard_map/ppermute | solution.py:573
  31.9 1.3 %leap_inner.1 = (f32[2,6,16,1024]{3,2,1,0:T(8,128)S(1)}, f32[2,4,16,1024]{3,2,1,0:T(8,128)S(1)}, f32[2,4,16,1024]{3,2,1,0:T(8,128)S(1)}) custom-call(f32[2,4,16,1024]{3,2,1,0:T(8,128)S(1)} %get-tuple-element.49.q_rim, f32[2,4,16,1024]{3,2,1,0:T(8,128)S(1)} %get-tuple-element.52.q_inner, f32[8,16,1024]{2,1,0:T(8,128)S(1)} %copy-done, ...), custom_call_target="tpu_custom_call" | custom-call | flops 7864320 | bytes 983040 | tf_op jit(solution)/shard_map/leap_inner/pallas_call | solution.py:596
  33.2 5.4 %collective-permute-done.7.from_a = f32[4,16,1024]{2,1,0:T(8,128)S(1)} collective-permute-done((f32[4,16,1024]{2,1,0:T(8,128)S(1)}, f32[4,16,1024]{2,1,0:T(8,128)S(1)}, u32[]{:S(2)}, u32[]{:S(2)}) %collective-permute-start.7) | collective-permute-done | bytes 262176 | tf_op jit(solution)/shard_map/ppermute | solution.py:552
  38.6 1.5 %leap_rim.1 = (f32[2,4,16,1024]{3,2,1,0:T(8,128)S(1)}, f32[2,4,16,1024]{3,2,1,0:T(8,128)S(1)}, f32[4,16,1024]{2,1,0:T(8,128)S(1)}, f32[4,16,1024]{2,1,0:T(8,128)S(1)}) custom-call(f32[2,4,16,1024]{3,2,1,0:T(8,128)S(1)} %get-tuple-element.49.q_rim, f32[2,4,16,1024]{3,2,1,0:T(8,128)S(1)} %get-tuple-element.52.q_inner, ...), custom_call_target="tpu_custom_call" | custom-call | flops 7864320 | bytes 983040 | tf_op jit(solution)/shard_map/leap_rim/pallas_call | solution.py:599
  40.1 4.2 %collective-permute-start.9 = (f32[4,16,1024]{2,1,0:T(8,128)S(1)}, f32[4,16,1024]{2,1,0:T(8,128)S(1)}, u32[]{:S(2)}, u32[]{:S(2)}) collective-permute-start(f32[4,16,1024]{2,1,0:T(8,128)S(1)} %get-tuple-element.64), channel_id=1, source_target_pairs={{0,31},{1,2},{2,1},{3,4},{4,3},{5,6},{6,5},{7,8},{8,7},{9,10},{10,... | collective-permute-start | bytes 786440 | tf_op jit(solution)/shard_map/ppermute | solution.py:552
  44.3 1.0 %store_q.1 = (f32[2,8,16,1024]{3,2,1,0:T(8,128)}, f32[8,128]{1,0:T(8,128)S(1)}) custom-call(f32[2,4,16,1024]{3,2,1,0:T(8,128)S(1)} %get-tuple-element.61.rim.refs_0_, f32[2,4,16,1024]{3,2,1,0:T(8,128)S(1)} %get-tuple-element.62.inner.refs_1_), custom_call_target="tpu_custom_call" | custom-call | flops 983040 | bytes 122880 | tf_op jit(solution)/shard_map/store_q/pallas_call | solution.py:607
  45.3 1.5 %last_inner.1 = (f32[2,6,16,1024]{3,2,1,0:T(8,128)S(1)}, f32[2,4,16,1024]{3,2,1,0:T(8,128)S(1)}, f32[2,8,128]{2,1,0:T(8,128)S(1)}, f32[1,128]{1,0:T(1,128)S(1)}) custom-call(f32[2,4,16,1024]{3,2,1,0:T(8,128)S(1)} %get-tuple-element.61.rim.refs_0_, f32[2,4,16,1024]{3,2,1,0:T(8,128)S(1)} %get-tuple-element.62.inner.refs_1_, f32[8,16,1024]{2,1,0:T(8,128)S(1)} %copy-done, ...), custom_call_target="tpu_custom_call" | custom-call | flops 7864320 | bytes 983040 | tf_op jit(solution)/shard_map/last_inner/pallas_call | solution.py:614
  46.8 5.1 %collective-permute-done.9.refs_2_ = f32[4,16,1024]{2,1,0:T(8,128)S(1)} collective-permute-done((f32[4,16,1024]{2,1,0:T(8,128)S(1)}, f32[4,16,1024]{2,1,0:T(8,128)S(1)}, u32[]{:S(2)}, u32[]{:S(2)}) %collective-permute-start.9) | collective-permute-done | bytes 262176 | tf_op jit(solution)/shard_map/ppermute | solution.py:552
  51.9 1.8 %last_rim.1 = (f32[2,4,16,1024]{3,2,1,0:T(8,128)S(1)}, f32[32,1,128]{2,1,0:T(1,128)}) custom-call(f32[2,4,16,1024]{3,2,1,0:T(8,128)S(1)} %get-tuple-element.61.rim.refs_0_, f32[2,4,16,1024]{3,2,1,0:T(8,128)S(1)} %get-tuple-element.62.inner.refs_1_, f32[4,16,1024]{2,1,0:T(8,128)S(1)} %collective-permute-done.9.refs_2_, ...), custom_call_target="tpu_custom_call" | custom-call | flops 7864320 | bytes 983040 | tf_op jit(solution)/shard_map/last_rim/pallas_call | solution.py:628
  53.8 5.8 %all-to-all-start = ((f32[32,1,128]{2,1,0:T(1,128)}), f32[32,1,128]{2,1,0:T(1,128)S(1)}, u32[]{:S(2)}, u32[]{:S(2)}) async-start(f32[32,1,128]{2,1,0:T(1,128)} %get-tuple-element.74), calls=%async_computation | async-start | bytes 32768 | tf_op jit(solution)/shard_map/all_to_all | solution.py:631
  59.6 0.8 %store_p.1.partial_p = f32[2,8,16,1024]{3,2,1,0:T(8,128)} custom-call(f32[2,4,16,1024]{3,2,1,0:T(8,128)S(1)} %get-tuple-element.76.inner), custom_call_target="tpu_custom_call" | custom-call | flops 491520 | bytes 61440 | tf_op jit(solution)/shard_map/store_p/pallas_call | solution.py:617
  60.4 7.4 %all-to-all-done.rows = f32[32,1,128]{2,1,0:T(1,128)S(1)} async-done(((f32[32,1,128]{2,1,0:T(1,128)}), f32[32,1,128]{2,1,0:T(1,128)S(1)}, u32[]{:S(2)}, u32[]{:S(2)}) %all-to-all-start) | async-done | bytes 16416 | tf_op jit(solution)/shard_map/all_to_all | solution.py:631
  67.9 1.4 %finish.1 = (f32[2,8,16,1024]{3,2,1,0:T(8,128)}, f32[2,2]{1,0:T(2,128)}) custom-call(f32[32,1,128]{2,1,0:T(1,128)S(1)} %all-to-all-done.rows, f32[2,4,16,1024]{3,2,1,0:T(8,128)S(1)} %get-tuple-element.75.rim_p, f32[2,8,16,1024]{3,2,1,0:T(8,128)} %store_p.1.partial_p), custom_call_target="tpu_custom_call", output_to_operand_aliasing={{0}: (2, {})} | custom-call | flops 122880 | bytes 15360 | tf_op jit(solution)/shard_map/finish/pallas_call | solution.py:645
  (22 shorter events, 0.9 us)
Async XLA Ops:
  2.3 6.8 %collective-permute-start.2 = (f32[4,2,16,1024]{3,2,1,0:T(8,128)S(1)}, f32[4,2,16,1024]{3,2,1,0:T(8,128)S(1)}, u32[]{:S(2)}, u32[]{:S(2)}) collective-permute-start(f32[4,2,16,1024]{3,2,1,0:T(8,128)S(1)} %get-tuple-element.48), channel_id=1, source_target_pairs={{0,32},{32,0},{64,96},{96,64},{1,33},{33,1},{65,97},{97,65},{2,34}... | collective-permute-start | bytes 1572872 | tf_op jit(solution)/shard_map/ppermute | solution.py:561
  2.4 15.1 %collective-permute-start = (f32[5,16,1024]{2,1,0:T(8,128)S(1)}, f32[5,16,1024]{2,1,0:T(8,128)S(1)}, u32[]{:S(2)}, u32[]{:S(2)}) collective-permute-start(f32[5,16,1024]{2,1,0:T(8,128)S(1)} %get-tuple-element.42), channel_id=1, source_target_pairs={{0,31},{1,2},{2,1},{3,4},{4,3},{5,6},{6,5},{7,8},{8,7},{9,10},{10,... | collective-permute-start | bytes 983048 | tf_op jit(solution)/shard_map/ppermute | solution.py:552
  9.1 9.8 %collective-permute-start.1 = (f32[5,16,1024]{2,1,0:T(8,128)S(1)}, f32[5,16,1024]{2,1,0:T(8,128)S(1)}, u32[]{:S(2)}, u32[]{:S(2)}) collective-permute-start(f32[5,16,1024]{2,1,0:T(8,128)S(1)} %get-tuple-element.43), channel_id=1, source_target_pairs={{0,1},{1,0},{2,3},{3,2},{4,5},{5,4},{6,7},{7,6},{8,9},{9,8},{10,11... | collective-permute-start | bytes 983048 | tf_op jit(solution)/shard_map/ppermute | solution.py:552
  9.2 3.7 %copy-start = (f32[8,16,1024]{2,1,0:T(8,128)S(1)}, f32[8,16,1024]{2,1,0:T(8,128)}, u32[]{:S(2)}) copy-start(f32[8,16,1024]{2,1,0:T(8,128)} %refs_4_.1) | copy-start | bytes 1572868
  9.2 3.7 %copy-start.1 = (f32[8,16,1024]{2,1,0:T(8,128)S(1)}, f32[8,16,1024]{2,1,0:T(8,128)}, u32[]{:S(2)}) copy-start(f32[8,16,1024]{2,1,0:T(8,128)} %refs_5_.1) | copy-start | bytes 1572868
  9.2 14.6 %collective-permute-start.3 = (f32[2,2,16,1024]{3,2,1,0:T(8,128)S(1)}, f32[2,2,16,1024]{3,2,1,0:T(8,128)S(1)}, u32[]{:S(2)}, u32[]{:S(2)}) collective-permute-start(f32[2,2,16,1024]{3,2,1,0:T(8,128)S(1)} %mass_rim_add.1.refs_0_), channel_id=1, source_target_pairs={{0,64},{32,96},{64,0},{96,32},{1,65},{33,97},{65,1},{97,33},{2,66}... | collective-permute-start | bytes 786440 | tf_op jit(solution)/shard_map/ppermute | solution.py:571
  19.9 5.4 %copy-start.2 = (f32[2,8,16,1024]{3,2,1,0:T(8,128)S(1)}, f32[2,8,16,1024]{3,2,1,0:T(8,128)}, u32[]{:S(2)}) copy-start(f32[2,8,16,1024]{3,2,1,0:T(8,128)} %draw.3) | copy-start | bytes 3145732
  20.0 10.2 %collective-permute-start.5 = (f32[2,2,16,1024]{3,2,1,0:T(8,128)S(1)}, f32[2,2,16,1024]{3,2,1,0:T(8,128)S(1)}, u32[]{:S(2)}, u32[]{:S(2)}) collective-permute-start(f32[2,2,16,1024]{3,2,1,0:T(8,128)S(1)} %mass_inner_add.1.refs_0_), channel_id=1, source_target_pairs={{0,64},{32,96},{64,0},{96,32},{1,65},{33,97},{65,1},{97,33},{2,66}... | collective-permute-start | bytes 786440 | tf_op jit(solution)/shard_map/ppermute | solution.py:571
  23.9 1.4 %collective-permute-start.4 = (f32[2,16,1024]{2,1,0:T(8,128)S(1)}, f32[2,16,1024]{2,1,0:T(8,128)S(1)}, u32[]{:S(2)}, u32[]{:S(2)}) collective-permute-start(f32[2,16,1024]{2,1,0:T(8,128)S(1)} %mass_rim.1.mine), channel_id=1, source_target_pairs={{0,32},{32,0},{64,96},{96,64},{1,33},{33,1},{65,97},{97,65},{2,34}... | collective-permute-start | bytes 393224 | tf_op jit(solution)/shard_map/ppermute | solution.py:573
  25.9 12.7 %collective-permute-start.7 = (f32[4,16,1024]{2,1,0:T(8,128)S(1)}, f32[4,16,1024]{2,1,0:T(8,128)S(1)}, u32[]{:S(2)}, u32[]{:S(2)}) collective-permute-start(f32[4,16,1024]{2,1,0:T(8,128)S(1)} %get-tuple-element.53), channel_id=1, source_target_pairs={{0,31},{1,2},{2,1},{3,4},{4,3},{5,6},{6,5},{7,8},{8,7},{9,10},{10,... | collective-permute-start | bytes 786440 | tf_op jit(solution)/shard_map/ppermute | solution.py:552
  30.2 8.5 %collective-permute-start.8 = (f32[4,16,1024]{2,1,0:T(8,128)S(1)}, f32[4,16,1024]{2,1,0:T(8,128)S(1)}, u32[]{:S(2)}, u32[]{:S(2)}) collective-permute-start(f32[4,16,1024]{2,1,0:T(8,128)S(1)} %get-tuple-element.54), channel_id=1, source_target_pairs={{0,1},{1,0},{2,3},{3,2},{4,5},{5,4},{6,7},{7,6},{8,9},{9,8},{10,11... | collective-permute-start | bytes 786440 | tf_op jit(solution)/shard_map/ppermute | solution.py:552
  30.2 1.4 %collective-permute-start.6 = (f32[2,16,1024]{2,1,0:T(8,128)S(1)}, f32[2,16,1024]{2,1,0:T(8,128)S(1)}, u32[]{:S(2)}, u32[]{:S(2)}) collective-permute-start(f32[2,16,1024]{2,1,0:T(8,128)S(1)} %mass_inner.1.mine), channel_id=1, source_target_pairs={{0,32},{32,0},{64,96},{96,64},{1,33},{33,1},{65,97},{97,65},{2,34}... | collective-permute-start | bytes 393224 | tf_op jit(solution)/shard_map/ppermute | solution.py:573
  40.1 11.8 %collective-permute-start.9 = (f32[4,16,1024]{2,1,0:T(8,128)S(1)}, f32[4,16,1024]{2,1,0:T(8,128)S(1)}, u32[]{:S(2)}, u32[]{:S(2)}) collective-permute-start(f32[4,16,1024]{2,1,0:T(8,128)S(1)} %get-tuple-element.64), channel_id=1, source_target_pairs={{0,31},{1,2},{2,1},{3,4},{4,3},{5,6},{6,5},{7,8},{8,7},{9,10},{10,... | collective-permute-start | bytes 786440 | tf_op jit(solution)/shard_map/ppermute | solution.py:552
  44.3 7.6 %collective-permute-start.10 = (f32[4,16,1024]{2,1,0:T(8,128)S(1)}, f32[4,16,1024]{2,1,0:T(8,128)S(1)}, u32[]{:S(2)}, u32[]{:S(2)}) collective-permute-start(f32[4,16,1024]{2,1,0:T(8,128)S(1)} %get-tuple-element.65), channel_id=1, source_target_pairs={{0,1},{1,0},{2,3},{3,2},{4,5},{5,4},{6,7},{7,6},{8,9},{9,8},{10,11... | collective-permute-start | bytes 786440 | tf_op jit(solution)/shard_map/ppermute | solution.py:552
  53.8 14.1 %all-to-all-start = ((f32[32,1,128]{2,1,0:T(1,128)}), f32[32,1,128]{2,1,0:T(1,128)S(1)}, u32[]{:S(2)}, u32[]{:S(2)}) async-start(f32[32,1,128]{2,1,0:T(1,128)} %get-tuple-element.74), calls=%async_computation | async-start | bytes 32768 | tf_op jit(solution)/shard_map/all_to_all | solution.py:631
